TPU v7x, 128 devices: a whole 4x4x4 slice. The times are simulated.
128 devices in a mesh: row: 32 (over z, y, core), col: 4 (over x).
Axes of the slice: x: 4, y: 4, z: 4, core: 2. Of those that a mesh axis runs over, the one named last changes fastest.
Arguments:
- positions: bfloat16 [8192, 64], P('row'), as said below
- log_weights: float32 [8192], P('row'), may hold values from 95 to 145
- cotangent: bfloat16 [8192, 64], P('row'), may hold values from -6 to 6
Outputs:
- grad_positions: float32 [8192, 64], P(('row', 'col'))
- grad_log_weights: float32 [8192], P('row')
Inputs may be any that keep to these rules, and one draw needn't show every extreme that they name: `positions`: particle states are finite real vectors.
All inputs are finite; a program needn't handle non-finite values.
Results may differ from a plain program's by a relative error of at most 0.008.
Values may be sent and summed in bfloat16 or wider, within the bound.
No kernel may reach another device: no remote copies, remote signals or barrier semaphores. Data moves between devices by JAX's collectives and lax.ppermute only.
A program may use at most 64 MiB of HBM per device.

v0:
```python
import functools
import math

import jax
import jax.numpy as jnp
from jax import lax
from jax.experimental import pallas as pl
from jax.experimental.pallas import tpu as pltpu
from jax.sharding import Mesh
from jax.sharding import PartitionSpec as P

ITERS = 5
AXES = ("z", "y", "c", "x")
X0, CORE, Y0, Y1, Z0, Z1 = 1, 4, 8, 16, 32, 64
LW_TOP = 145.0
TINY = 1e-37
BLOCK = 256
SPAN = 1024
F32 = jnp.float32
BF16 = jnp.bfloat16


def swap(value, bits):
    return lax.ppermute(value, AXES, [(i, i ^ bits) for i in range(128)])


def merge(a, b):
    top = jnp.maximum(a, b)
    return top + jnp.log(jnp.exp(a - top) + jnp.exp(b - top))


def plus(a, b):
    return a + b


def over_rows(partial, op):
    partial = op(partial, swap(partial, CORE))
    partial = op(partial, swap(partial, Y0 | CORE))
    return partial, swap(partial, Z0 | CORE)


def over_cols(partial):
    return partial, swap(partial, X0)


def mm(a, b):
    return lax.dot_general(a, b, (((1,), (0,)), ((), ())), preferred_element_type=F32)


def parts(v):
    hi = v.astype(BF16).astype(F32)
    mid = (v - hi).astype(BF16).astype(F32)
    lo = (v - hi) - mid
    return hi, mid, lo


def extra(v, w, left):
    at = lax.broadcasted_iota(jnp.int32, (16, v.shape[1]), 0)
    out = jnp.where((at >= 3) & (at < 6) if left else at < 3, 1.0, 0.0)
    for i, part in enumerate(parts(v)):
        out = jnp.where(at == (i if left else i + 3), part, out)
    if w is not None:
        for i, part in enumerate(parts(w)):
            out = jnp.where(at == i + 6, part, out)
    return out.astype(BF16)


def tile_pass(mode, left, right, rows, cols, left_x, right_x, emit, pair=None):
    weighted = mode in ("weight", "pair_weight")
    if weighted:
        at = lax.broadcasted_iota(jnp.int32, (128, 128), 0)
        pick = jnp.where((at >= 70) & (at < 73), 1.0, 0.0).astype(BF16)
    low = jnp.zeros((64, BLOCK), BF16)
    high = jnp.zeros((48, BLOCK), BF16)

    def block(m0, right_block, pair_block, acc):
        x = jnp.concatenate([low, left_x[:, pl.ds(m0, BLOCK)], high], axis=0)
        a = left[pl.ds(m0, BLOCK), :] + x.T
        t = mm(a, right_block)
        if mode == "max":
            e = t
        else:
            e = jnp.exp(t)
        if weighted:
            w = mm(a, pick)
        if pair is not None:
            pr = mm(pair[0][pl.ds(m0, BLOCK), :], pair_block)
        out = []
        for q in range(SPAN // 128):
            y = e[:, q * 128 : (q + 1) * 128]
            if mode == "weight":
                y = y * w
            elif mode == "pair":
                y = y * pr[:, q * 128 : (q + 1) * 128]
            elif mode == "pair_weight":
                y = y * (pr[:, q * 128 : (q + 1) * 128] - w)
            y = y.reshape(BLOCK // 8, 8, 128)
            if mode == "max":
                out.append(jnp.maximum(acc[q], jnp.max(y, axis=0)))
            else:
                out.append(acc[q] + jnp.sum(y, axis=0))
        return tuple(out)

    def right_of(n0):
        sl = pl.ds(n0, SPAN)
        full = jnp.concatenate([right[:, sl], right_x[:, sl], jnp.zeros((48, SPAN), BF16)], axis=0)
        return full, None if pair is None else pair[1][:, sl]

    def fold(acc):
        if mode == "max":
            return jnp.concatenate([jnp.max(a, axis=0, keepdims=True) for a in acc], axis=1)
        return jnp.concatenate([jnp.sum(a, axis=0, keepdims=True) for a in acc], axis=1)

    start = jnp.full((8, 128), -jnp.inf if mode == "max" else 0.0, F32)
    zero = (start,) * (SPAN // 128)
    if rows > cols:
        right_block, pair_block = right_of(0)

        def step(i, acc):
            for b in range(2):
                m0 = pl.multiple_of((2 * i + b) * BLOCK, BLOCK)
                acc = block(m0, right_block, pair_block, acc)
            return acc

        emit(0, fold(lax.fori_loop(0, rows // (2 * BLOCK), step, zero)))
    else:

        def step(i, carry):
            n0 = pl.multiple_of(i * SPAN, SPAN)
            right_block, pair_block = right_of(n0)
            acc = zero
            for b in range(SPAN // BLOCK):
                acc = block(b * BLOCK, right_block, pair_block, acc)
            emit(n0, fold(acc))
            return carry

        lax.fori_loop(0, cols // SPAN, step, 0)


def call(kernel, name, out_shapes, scratch, *args):
    return pl.pallas_call(
        kernel,
        name=name,
        out_shape=tuple(jax.ShapeDtypeStruct(s, d) for s, d in out_shapes),
        scratch_shapes=scratch,
        compiler_params=pltpu.CompilerParams(vmem_limit_bytes=24 * 2**20),
    )(*args)


def halves(v):
    a, b = v[:, :128], v[:, 128:]
    lane = lax.broadcasted_iota(jnp.int32, a.shape, 1)
    even = jnp.where(lane < 64, a, pltpu.roll(b, 64, 1))
    odd = jnp.where(lane < 64, pltpu.roll(a, 64, 1), b)
    return even, odd


def pack_kernel(x0_ref, pos, cot, lw, out, own):
    even, odd = halves(jnp.concatenate([pos[...], cot[...]], axis=0).astype(F32))
    block = jnp.where(x0_ref[0] == 0, even, odd).astype(BF16).T
    for r in range(out.shape[0]):
        out[r] = block
    own[:128, :] = jnp.concatenate([even[:64], odd[:64]], axis=0).astype(BF16).T
    at = lax.broadcasted_iota(jnp.int32, (16, 128), 0)
    rest = jnp.zeros((16, 128), F32)
    for h, half in enumerate(halves(lw[...])):
        for i, part in enumerate(parts(half)):
            rest = jnp.where(at == 3 * h + i, part, rest)
    own[128:, :] = rest.astype(BF16)


def prep_kernel(
    scale, place, mine, other, own, near, far, left_c, right_c, cot_t, both, sq_c, left_r, right_r, sq_r, lw
):
    lane = lax.broadcasted_iota(jnp.int32, (128, 128), 1)
    core, y1, z1 = place[0], place[1], place[2]
    chips = mine.shape[0]

    def norm(p):
        p = p.astype(F32)
        return scale * jnp.sum(p * p, axis=0, keepdims=True)

    def step(r, carry):
        for src, c in ((mine, core), (other, 1 - core)):
            sl = pl.ds(pl.multiple_of((c * chips + r) * 128, 128), 128)
            block = src[r]
            turned = block.T
            both[sl, :] = block
            left_c[sl, :] = jnp.where(lane < 64, block.astype(F32) * (2.0 * scale), 0.0).astype(BF16)
            right_c[:, sl] = turned[:64]
            cot_t[:64, sl] = turned[64:]
            cot_t[64:, sl] = jnp.zeros((64, 128), BF16)
            sq_c[:, sl] = norm(turned[:64])
        return carry

    lax.fori_loop(0, chips, step, 0)
    sources = (
        (own[...], 2 * z1 + y1),
        (near[...], 2 * z1 + 1 - y1),
        (far[0], 2 * (1 - z1) + y1),
        (far[1], 2 * (1 - z1) + 1 - y1),
    )
    for src, q in sources:
        block = src[:128].astype(F32) * (2.0 * scale)
        turned = src[:128].T
        low = src[128:].astype(F32)
        for h in range(2):
            sl = pl.ds(pl.multiple_of(q * 256 + h * 128, 128), 128)
            part = block if h == 0 else pltpu.roll(block, 64, 1)
            left_r[sl, :] = jnp.where(lane < 64, part, 0.0).astype(BF16)
            right_r[:, sl] = turned[64 * h : 64 * h + 64]
            sq_r[:, sl] = norm(turned[64 * h : 64 * h + 64])
            lw[:, sl] = (low[3 * h : 3 * h + 1] + low[3 * h + 1 : 3 * h + 2]) + low[3 * h + 2 : 3 * h + 3]


def pair_up(x):
    lane = lax.broadcasted_iota(jnp.int32, (32, 128), 1)
    a, b = x[:32], x[32:]
    first = jnp.where(lane < 64, a, pltpu.roll(b, 64, 1))
    second = jnp.where(lane < 64, pltpu.roll(a, 64, 1), b)
    return first.astype(BF16), second.astype(BF16)


def final_kernel(scale, log_count, place, both, left_r, right_r, lw, sq_r, sq_c, *refs):
    us, refs = refs[:ITERS], refs[ITERS:]
    vs, refs = refs[:ITERS], refs[ITERS:]
    dvs, refs = refs[:ITERS], refs[ITERS:]
    du_a, du_b, refs = refs[0], refs[1], refs[2:]
    dus, refs = refs[: ITERS - 1], refs[ITERS - 1 :]
    row_out, col_out, glw, stack, pick_v, right_x, turned, near, left_s, left_b, weight, acc_g, acc_q, mass = refs
    q, x1 = place[0], place[1]
    wide = stack.shape[1]
    n_t = wide // 2
    own = pl.ds(pl.multiple_of(q * 256, 256), 256)

    stack[...] = jnp.zeros(stack.shape, F32)
    stack[0:1, :] = -sq_c[...]
    for k in range(ITERS):
        stack[k + 1 : k + 2, :] = vs[k][...] - sq_c[...]
        stack[k + 6 : k + 7, :] = dvs[k][...]
    for t in range(n_t // 128):
        even, odd = halves(stack[:, t * 256 : (t + 1) * 256])
        pick_v[:, t * 128 : (t + 1) * 128] = jnp.where(x1 == 0, even, odd)
        half = [both[pl.ds(pl.multiple_of((2 * t + i) * 128 + x1 * 64, 64), 64), :] for i in range(2)]
        block = jnp.concatenate(half, axis=0)
        near[t * 128 : (t + 1) * 128, :] = block
        turned[:, t * 128 : (t + 1) * 128] = block.T
    for k in range(ITERS + 1):
        right_x[k] = extra(pick_v[k : k + 1, :], None, False)

    low = jnp.zeros((64, 256), BF16)
    high = jnp.zeros((48, 256), BF16)
    at = lax.broadcasted_iota(jnp.int32, (128, 128), 0)
    pick = jnp.where((at >= 70) & (at < 73), 1.0, 0.0).astype(BF16)
    left = left_r[own, :]
    total = None
    for k in reversed(range(ITERS)):
        du = dus[k - 1][:, own] if k > 0 else du_a[:, own] + du_b[:, own]
        total = du if total is None else total + du
        u = us[k][:, own] - sq_r[:, own]
        x = extra(u + lw[:, own], None, True)
        left_s[k] = left + jnp.concatenate([low, x, high], axis=0).T
        x = extra(u - log_count, du, True)
        a = left + jnp.concatenate([low, x, high], axis=0).T
        left_b[k] = a
        weight[k] = mm(a, pick)
    glw[...] = jnp.concatenate(halves(total), axis=1)
    acc_g[...] = jnp.zeros(acc_g.shape, F32)
    acc_q[...] = jnp.zeros(acc_q.shape, F32)
    mass[...] = jnp.zeros(mass.shape, F32)
    p_rows = right_r[:, own]
    chips = col_out.shape[0] // 2

    def step(i, carry):
        sl = pl.ds(pl.multiple_of(i * 256, 256), 256)
        p = turned[:64, sl]
        pair = mm(left, jnp.concatenate([turned[64:, sl], low], axis=0))
        plan = None
        for k in reversed(range(ITERS)):
            right = jnp.concatenate([p, right_x[k + 1, :, sl], high], axis=0)
            s = jnp.exp(mm(left_s[k], right))
            dv = pick_v[k + 6 : k + 7, sl]
            if plan is None:
                plan = s.astype(BF16)
                g = s * (dv - (0.5 / scale) * pair)
            else:
                g = g + s * dv
            right = jnp.concatenate([p, right_x[k, :, sl], high], axis=0)
            r = jnp.exp(mm(left_b[k], right))
            g = g + r * jnp.concatenate([weight[k], weight[k]], axis=1)
        narrow = g.astype(BF16)
        acc_g[...] += mm(narrow, near[sl, :])
        acc_q[...] += mm(plan, near[sl, :])
        mass[...] += g[:, :128] + g[:, 128:]
        pushed = mm(p_rows, narrow)
        term = (2.0 * scale) * (jnp.sum(g, axis=0, keepdims=True) * p.astype(F32) - pushed)
        for t in range(2):
            for j, chunk in enumerate(pair_up(term[:, t * 128 : (t + 1) * 128])):
                c = i * 4 + t * 2 + j
                col_out[(c % chips) * 2 + c // chips] = chunk
        return carry

    lax.fori_loop(0, n_t // 256, step, 0)
    row_mass = jnp.sum(mass[...], axis=1, keepdims=True)
    term = pltpu.roll(acc_q[...], 64, 1) + row_mass * left.astype(F32) - (2.0 * scale) * acc_g[...]
    term = term.T
    for t in range(2):
        for j, chunk in enumerate(pair_up(term[:64, t * 128 : (t + 1) * 128])):
            row_out[2 * j + t] = chunk


def finish_kernel(row_parts, col_parts, out):
    acc = row_parts[0].astype(F32)
    for i in range(1, row_parts.shape[0]):
        acc = acc + row_parts[i].astype(F32)
    for i in range(col_parts.shape[0]):
        acc = acc + col_parts[i].astype(F32)
    both = jnp.concatenate([acc, pltpu.roll(acc, 64, 1)], axis=0)
    out[...] = both.T[:64, :]


def first_u(left_c, right_r, sq_c, sq_r, out, left_x, right_x):
    left_x[...] = extra(-sq_c[...], None, True)
    right_x[...] = extra(-sq_r[...], None, False)

    def emit(n0, value):
        out[...] = jnp.log(jnp.maximum(value, TINY))

    tile_pass("exp", left_c, right_r, sq_c.shape[1], sq_r.shape[1], left_x, right_x, emit)


def next_v(log_count, is_first, pa, pb, u_old, v_old, lw, left_r, right_c, sq_r, sq_c, u_new, out, left_x, right_x, base):
    u = log_count - merge(pa[...], pb[...])
    u_new[...] = u
    if is_first:
        base[...] = jnp.full(base.shape, LW_TOP + log_count, F32)
    else:
        base[...] = jnp.max(u - u_old[...], axis=1, keepdims=True) - v_old[...]
    left_x[...] = extra(u + lw[...] - sq_r[...], None, True)
    right_x[...] = extra(-sq_c[...] - base[...], None, False)

    def emit(n0, value):
        sl = pl.ds(n0, SPAN)
        out[:, sl] = base[:, sl] + jnp.log(jnp.maximum(value, TINY))

    tile_pass("exp", left_r, right_c, sq_r.shape[1], sq_c.shape[1], left_x, right_x, emit)


def next_u(log_count, pa, pb, v_old, u_old, left_c, right_r, sq_c, sq_r, v_new, out, left_x, right_x):
    v = -merge(pa[...], pb[...])
    v_new[...] = v
    base = (log_count - u_old[...]) + jnp.max(v - v_old[...], axis=1, keepdims=True)
    left_x[...] = extra(v - sq_c[...], None, True)
    right_x[...] = extra(-sq_r[...] - base, None, False)

    def emit(n0, value):
        out[...] = base + jnp.log(jnp.maximum(value, TINY))

    tile_pass("exp", left_c, right_r, sq_c.shape[1], sq_r.shape[1], left_x, right_x, emit)


def first_dv(unscale, pa, pb, u, lw, left_r, right_c, cot_t, sq_r, sq_c, v_new, out, left_x, right_x):
    v = -merge(pa[...], pb[...])
    v_new[...] = v
    left_x[...] = extra(u[...] + lw[...] - sq_r[...], None, True)
    right_x[...] = extra(v - sq_c[...], None, False)

    def emit(n0, value):
        out[:, pl.ds(n0, SPAN)] = unscale * value

    tile_pass(
        "pair", left_r, right_c, sq_r.shape[1], sq_c.shape[1], left_x, right_x, emit, (left_r, cot_t)
    )


def first_du(pa, pb, u, v, lw, left_c, right_r, both, sq_c, sq_r, dv_new, out, left_x, right_x, pair_r):
    dv = pa[...] + pb[...]
    dv_new[...] = dv
    left_x[...] = extra(v[...] - sq_c[...], dv, True)
    right_x[...] = extra(u[...] + lw[...] - sq_r[...], None, False)
    pair_r[:64, :] = jnp.zeros_like(right_r)
    pair_r[64:, :] = right_r[...]

    def emit(n0, value):
        out[...] = value

    tile_pass(
        "pair_weight", left_c, right_r, sq_c.shape[1], sq_r.shape[1], left_x, right_x, emit, (both, pair_r)
    )


def next_dv(log_count, pa, pb, u, v, left_r, right_c, sq_r, sq_c, du_new, out, left_x, right_x):
    du = pa[...] + pb[...]
    du_new[...] = du
    left_x[...] = extra(u[...] - log_count - sq_r[...], du, True)
    right_x[...] = extra(v[...] - sq_c[...], None, False)

    def emit(n0, value):
        out[:, pl.ds(n0, SPAN)] = -value

    tile_pass("weight", left_r, right_c, sq_r.shape[1], sq_c.shape[1], left_x, right_x, emit)


def next_du(pa, pb, u, v, lw, left_c, right_r, sq_c, sq_r, dv_new, out, left_x, right_x):
    dv = pa[...] + pb[...]
    dv_new[...] = dv
    left_x[...] = extra(v[...] - sq_c[...], dv, True)
    right_x[...] = extra(u[...] + lw[...] - sq_r[...], None, False)

    def emit(n0, value):
        out[...] = -value

    tile_pass("weight", left_c, right_r, sq_c.shape[1], sq_r.shape[1], left_x, right_x, emit)


def local(positions, log_weights, cotangent):
    z, y, core, x = (lax.axis_index(name) for name in AXES)
    x0, x1, y1, z1 = x & 1, x >> 1, y >> 1, z >> 1
    n_row, dim = positions.shape
    log_count = math.log(n_row * 32)
    scale = 4.0 / dim
    n_r, n_c = 4 * n_row, 16 * n_row
    smem, vmem = pl.BlockSpec(memory_space=pltpu.SMEM), pl.BlockSpec(memory_space=pltpu.VMEM)

    payload, own = pl.pallas_call(
        pack_kernel,
        name="pack",
        in_specs=[smem] + [vmem] * 3,
        out_shape=(jax.ShapeDtypeStruct((16, 128, 128), BF16), jax.ShapeDtypeStruct((144, 128), BF16)),
    )(x0.reshape(1), positions.T, cotangent.T, log_weights.reshape(1, n_row))
    mine = lax.all_to_all(payload, ("z", "y"), 0, 0, tiled=True)
    near = swap(own, Y1)
    far = swap(jnp.stack([own, near]), Z1)
    other = swap(mine, CORE)
    left_c, right_c, cot_t, both, sq_c, left_r, right_r, sq_r, lw = pl.pallas_call(
        functools.partial(prep_kernel, scale),
        name="prep",
        in_specs=[smem] + [vmem] * 5,
        out_shape=tuple(
            jax.ShapeDtypeStruct(shape, kind)
            for shape, kind in (
                ((n_c, 128), BF16),
                ((64, n_c), BF16),
                ((128, n_c), BF16),
                ((n_c, 128), BF16),
                ((1, n_c), F32),
                ((n_r, 128), BF16),
                ((64, n_r), BF16),
                ((1, n_r), F32),
                ((1, n_r), F32),
            )
        ),
    )(jnp.stack([core, y1, z1]), mine, other, own, near, far)

    u_like, v_like = ((1, n_r), F32), ((1, n_c), F32)
    x_r, x_c = pltpu.VMEM((16, n_r), BF16), pltpu.VMEM((16, n_c), BF16)

    (part,) = call(first_u, "u0", (u_like,), [x_c, x_r], left_c, right_r, sq_c, sq_r)
    us, vs = [], [jnp.zeros((1, n_c), F32)]
    for k in range(ITERS):
        pa, pb = over_cols(part)
        old = us[-1] if us else sq_r
        u, part = call(
            functools.partial(next_v, log_count, k == 0),
            f"v{k}",
            (u_like, v_like),
            [x_r, x_c, pltpu.VMEM((1, n_c), F32)],
            *(pa, pb, old, vs[-1], lw, left_r, right_c, sq_r, sq_c),
        )
        us.append(u)
        pa, pb = over_rows(part, merge)
        if k == ITERS - 1:
            break
        v, part = call(
            functools.partial(next_u, log_count),
            f"u{k + 1}",
            (v_like, u_like),
            [x_c, x_r],
            *(pa, pb, vs[-1], us[-1], left_c, right_r, sq_c, sq_r),
        )
        vs.append(v)

    v, part = call(
        functools.partial(first_dv, 0.5 / scale),
        "dv4",
        (v_like, v_like),
        [x_r, x_c],
        *(pa, pb, us[-1], lw, left_r, right_c, cot_t, sq_r, sq_c),
    )
    vs.append(v)
    pa, pb = over_rows(part, plus)
    dv, part = call(
        first_du,
        "du4",
        (v_like, u_like),
        [x_c, x_r, pltpu.VMEM((128, n_r), BF16)],
        *(pa, pb, us[-1], vs[-1], lw, left_c, right_r, both, sq_c, sq_r),
    )
    dus, dvs = [None] * ITERS, [None] * ITERS
    dvs[ITERS - 1] = dv
    for k in reversed(range(ITERS - 1)):
        pa, pb = over_cols(part)
        dus[k + 1], part = call(
            functools.partial(next_dv, log_count),
            f"dv{k}",
            (u_like, v_like),
            [x_r, x_c],
            *(pa, pb, us[k + 1], vs[k + 1], left_r, right_c, sq_r, sq_c),
        )
        pa, pb = over_rows(part, plus)
        dvs[k], part = call(
            next_du,
            f"du{k}",
            (v_like, u_like),
            [x_c, x_r],
            *(pa, pb, us[k], vs[k + 1], lw, left_c, right_r, sq_c, sq_r),
        )
    pa, pb = over_cols(part)
    n_t = n_c // 2
    row_out, col_out, glw = pl.pallas_call(
        functools.partial(final_kernel, scale, log_count),
        name="final",
        in_specs=[smem] + [vmem] * (6 + 3 * ITERS + 2 + ITERS - 1),
        out_shape=(
            jax.ShapeDtypeStruct((4, 32, 128), BF16),
            jax.ShapeDtypeStruct((32, 32, 128), BF16),
            jax.ShapeDtypeStruct((1, n_row), F32),
        ),
        scratch_shapes=[
            pltpu.VMEM((16, n_c), F32),
            pltpu.VMEM((16, n_t), F32),
            pltpu.VMEM((ITERS + 1, 16, n_t), BF16),
            pltpu.VMEM((128, n_t), BF16),
            pltpu.VMEM((n_t, 128), BF16),
            pltpu.VMEM((ITERS, n_row, 128), BF16),
            pltpu.VMEM((ITERS, n_row, 128), BF16),
            pltpu.VMEM((ITERS, n_row, 128), F32),
            pltpu.VMEM((n_row, 128), F32),
            pltpu.VMEM((n_row, 128), F32),
            pltpu.VMEM((n_row, 128), F32),
        ],
        compiler_params=pltpu.CompilerParams(vmem_limit_bytes=24 * 2**20),
    )(
        jnp.stack([2 * z1 + y1, x1]),
        *(both, left_r, right_r, lw, sq_r, sq_c),
        *us,
        *vs[1:],
        *dvs,
        *(pa, pb),
        *dus[1:],
    )
    row_parts = lax.all_to_all(row_out, "x", 0, 0, tiled=True)
    col_parts = lax.all_to_all(col_out, ("z", "y", "c"), 0, 0, tiled=True)
    out = pl.pallas_call(
        finish_kernel, name="finish", out_shape=jax.ShapeDtypeStruct((n_row // 4, dim), F32)
    )(row_parts, col_parts)
    return (out, glw.reshape(n_row))


def solution(mesh):
    fine = Mesh(mesh.devices.reshape(4, 4, 2, 4), AXES)
    rows = ("z", "y", "c")
    in_specs = (P(rows, None), P(rows), P(rows, None))
    out_specs = (P(AXES, None), P(rows))
    return jax.shard_map(local, mesh=fine, in_specs=in_specs, out_specs=out_specs, check_vma=False)
```

profile of v0, /device:TPU:1, one launch (start us, length us, event | category | flops | bytes accessed | tf_op | source)
XLA Modules:
  0.0 279.5 jit_solution(16141549151880918044)
XLA Ops:
  2.4 19.1 %all_to_all.15.mine = bf16[16,128,128]{2,1,0:T(8,128)(2,1)S(1)} all-to-all(bf16[16,128,128]{2,1,0:T(8,128)(2,1)} %get-tuple-element.54), channel_id=1, replica_groups=mesh['z'=4,'y'=4,'c'=2,'x'=4] {'z','y'}, dimensions={0} | all-to-all | bytes 1048576 | tf_op jit(solution)/shard_map/all_to_all | solution.py:431
  24.2 3.8 %collective-permute-done.1.near = bf16[144,128]{1,0:T(8,128)(2,1)S(1)} collective-permute-done((bf16[144,128]{1,0:T(8,128)(2,1)S(1)}, bf16[144,128]{1,0:T(8,128)(2,1)S(1)}, u32[]{:S(2)}, u32[]{:S(2)}) %collective-permute-start.1) | collective-permute-done | bytes 36896 | tf_op jit(solution)/shard_map/ppermute | solution.py:24
  29.8 3.5 %collective-permute-done.2.far = bf16[2,144,128]{2,1,0:T(8,128)(2,1)S(1)} collective-permute-done((bf16[2,144,128]{2,1,0:T(8,128)(2,1)S(1)}, bf16[2,144,128]{2,1,0:T(8,128)(2,1)S(1)}, u32[]{:S(2)}, u32[]{:S(2)}) %collective-permute-start.2) | collective-permute-done | bytes 73760 | tf_op jit(solution)/shard_map/ppermute | solution.py:24
  34.7 4.7 %prep.1 = (bf16[4096,128]{1,0:T(8,128)(2,1)}, bf16[64,4096]{1,0:T(8,128)(2,1)}, bf16[128,4096]{1,0:T(8,128)(2,1)}, bf16[4096,128]{1,0:T(8,128)(2,1)}, f32[1,4096...) custom-call(s32[3]{0:T(128)} %pad_add_fusion.1.place, ...), custom_call_target="tpu_custom_call" | custom-call | tf_op jit(solution)/shard_map/prep/pallas_call | solution.py:435
  42.9 3.9 %u0.1.pa = f32[1,1024]{1,0:T(1,128)S(1)} custom-call(bf16[4096,128]{1,0:T(8,128)(2,1)S(1)} %copy-done, bf16[64,1024]{1,0:T(8,128)(2,1)S(1)} %copy-done.5, f32[1,4096]{1,0:T(1,128)S(1)} %copy-done.7, f32[1,1024]{1,0:T(1,128)S(1)} %copy-done.10), custom_call_target="tpu_custom_call" | custom-call | tf_op jit(solution)/shard_map/u0/pallas_call | solution.py:141
  52.0 3.2 %v0.1 = (f32[1,1024]{1,0:T(1,128)S(1)}, f32[1,4096]{1,0:T(1,128)S(1)}) custom-call(f32[1,1024]{1,0:T(1,128)S(1)} %u0.1.pa, f32[1,1024]{1,0:T(1,128)S(1)} %collective-permute-done.3.pb, f32[1,1024]{1,0:T(1,128)S(1)} %copy-done.10, f32[1,4096]{1,0:T(1,128)S(1)} %broadcast_in_dim.3.v_old, f32[1,1024]{1,0:T(1,128)S(1)} %copy-done.12, ...), custom_call_target="tpu_custom_call" | custom-call | tf_op jit(solution)/shard_map/v0/pallas_call | solution.py:141
  55.2 3.6 %collective-permute-start.4 = (f32[1,4096]{1,0:T(1,128)S(1)}, f32[1,4096]{1,0:T(1,128)S(1)}, u32[]{:S(2)}, u32[]{:S(2)}) collective-permute-start(f32[1,4096]{1,0:T(1,128)S(1)} %get-tuple-element.65), channel_id=1, source_target_pairs={{0,4},{1,5},{2,6},{3,7},{4,0},{5,1},{6,2},{7,3},{8,12},{9,13},{10,... | collective-permute-start | bytes 49160 | tf_op jit(solution)/shard_map/ppermute | solution.py:24
  63.2 3.2 %collective-permute-done.6.pb = f32[1,4096]{1,0:T(1,128)S(1)} collective-permute-done((f32[1,4096]{1,0:T(1,128)S(1)}, f32[1,4096]{1,0:T(1,128)S(1)}, u32[]{:S(2)}, u32[]{:S(2)}) %collective-permute-start.6) | collective-permute-done | bytes 16416 | tf_op jit(solution)/shard_map/ppermute | solution.py:24
  66.3 3.9 %u1_.1 = (f32[1,4096]{1,0:T(1,128)S(1)}, f32[1,1024]{1,0:T(1,128)S(1)}) custom-call(f32[1,4096]{1,0:T(1,128)S(1)} %log_add_fusion.8.pa, f32[1,4096]{1,0:T(1,128)S(1)} %collective-permute-done.6.pb, f32[1,4096]{1,0:T(1,128)S(1)} %broadcast_in_dim.3.v_old, f32[1,1024]{1,0:T(1,128)S(1)} %get-tuple-element.64.u_old.u.refs_0_, bf16[4096,128]{1,0:T(8,128)(2,1)S(1)} %copy-done.1, ...), custom_call_target="tpu_custom_call" | custom-call | tf_op jit(solution)/shard_map/u1/pallas_call | solution.py:141
  72.8 3.3 %v1.1 = (f32[1,1024]{1,0:T(1,128)S(1)}, f32[1,4096]{1,0:T(1,128)S(1)}) custom-call(f32[1,1024]{1,0:T(1,128)S(1)} %get-tuple-element.66.pa, f32[1,1024]{1,0:T(1,128)S(1)} %collective-permute-done.7.pb, f32[1,1024]{1,0:T(1,128)S(1)} %get-tuple-element.64.u_old.u.refs_0_, f32[1,4096]{1,0:T(1,128)S(1)} %get-tuple-element.67.v_old.v.refs_5_, ...), custom_call_target="tpu_custom_call" | custom-call | tf_op jit(solution)/shard_map/v1/pallas_call | solution.py:141
  82.0 3.1 %collective-permute-done.10.pb = f32[1,4096]{1,0:T(1,128)S(1)} collective-permute-done((f32[1,4096]{1,0:T(1,128)S(1)}, f32[1,4096]{1,0:T(1,128)S(1)}, u32[]{:S(2)}, u32[]{:S(2)}) %collective-permute-start.10) | collective-permute-done | bytes 16416 | tf_op jit(solution)/shard_map/ppermute | solution.py:24
  85.2 3.9 %u2_.1 = (f32[1,4096]{1,0:T(1,128)S(1)}, f32[1,1024]{1,0:T(1,128)S(1)}) custom-call(f32[1,4096]{1,0:T(1,128)S(1)} %log_add_fusion.6.pa, f32[1,4096]{1,0:T(1,128)S(1)} %collective-permute-done.10.pb, f32[1,4096]{1,0:T(1,128)S(1)} %get-tuple-element.67.v_old.v.refs_5_, f32[1,1024]{1,0:T(1,128)S(1)} %get-tuple-element.68.u_old.u.refs_1_, ...), custom_call_target="tpu_custom_call" | custom-call | tf_op jit(solution)/shard_map/u2/pallas_call | solution.py:141
  91.7 3.3 %v2.1 = (f32[1,1024]{1,0:T(1,128)S(1)}, f32[1,4096]{1,0:T(1,128)S(1)}) custom-call(f32[1,1024]{1,0:T(1,128)S(1)} %get-tuple-element.70.pa, f32[1,1024]{1,0:T(1,128)S(1)} %collective-permute-done.11.pb, f32[1,1024]{1,0:T(1,128)S(1)} %get-tuple-element.68.u_old.u.refs_1_, f32[1,4096]{1,0:T(1,128)S(1)} %get-tuple-element.71.v_old.v.refs_6_, ...), custom_call_target="tpu_custom_call" | custom-call | tf_op jit(solution)/shard_map/v2/pallas_call | solution.py:141
  104.0 3.9 %u3.1 = (f32[1,4096]{1,0:T(1,128)S(1)}, f32[1,1024]{1,0:T(1,128)S(1)}) custom-call(f32[1,4096]{1,0:T(1,128)S(1)} %log_add_fusion.4.pa, f32[1,4096]{1,0:T(1,128)S(1)} %collective-permute-done.14.pb, f32[1,4096]{1,0:T(1,128)S(1)} %get-tuple-element.71.v_old.v.refs_6_, f32[1,1024]{1,0:T(1,128)S(1)} %get-tuple-element.72.u_old.u.refs_2_, ...), custom_call_target="tpu_custom_call" | custom-call | tf_op jit(solution)/shard_map/u3/pallas_call | solution.py:141
  110.5 3.3 %v3.1 = (f32[1,1024]{1,0:T(1,128)S(1)}, f32[1,4096]{1,0:T(1,128)S(1)}) custom-call(f32[1,1024]{1,0:T(1,128)S(1)} %get-tuple-element.74.pa, f32[1,1024]{1,0:T(1,128)S(1)} %collective-permute-done.15.pb, f32[1,1024]{1,0:T(1,128)S(1)} %get-tuple-element.72.u_old.u.refs_2_, f32[1,4096]{1,0:T(1,128)S(1)} %get-tuple-element.75.v_old.v.refs_7_, ...), custom_call_target="tpu_custom_call" | custom-call | tf_op jit(solution)/shard_map/v3/pallas_call | solution.py:141
  123.0 3.9 %u4_.1 = (f32[1,4096]{1,0:T(1,128)S(1)}, f32[1,1024]{1,0:T(1,128)S(1)}) custom-call(f32[1,4096]{1,0:T(1,128)S(1)} %log_add_fusion.2.pa, f32[1,4096]{1,0:T(1,128)S(1)} %collective-permute-done.18.pb, f32[1,4096]{1,0:T(1,128)S(1)} %get-tuple-element.75.v_old.v.refs_7_, f32[1,1024]{1,0:T(1,128)S(1)} %get-tuple-element.76.u_old.u.refs_3_, ...), custom_call_target="tpu_custom_call" | custom-call | tf_op jit(solution)/shard_map/u4/pallas_call | solution.py:141
  129.5 3.3 %v4.1 = (f32[1,1024]{1,0:T(1,128)S(1)}, f32[1,4096]{1,0:T(1,128)S(1)}) custom-call(f32[1,1024]{1,0:T(1,128)S(1)} %get-tuple-element.78.pa, f32[1,1024]{1,0:T(1,128)S(1)} %collective-permute-done.19.pb, f32[1,1024]{1,0:T(1,128)S(1)} %get-tuple-element.76.u_old.u.refs_3_, f32[1,4096]{1,0:T(1,128)S(1)} %get-tuple-element.79.v_old.v.refs_8_, ...), custom_call_target="tpu_custom_call" | custom-call | tf_op jit(solution)/shard_map/v4/pallas_call | solution.py:141
  138.8 3.1 %collective-permute-done.22.pb = f32[1,4096]{1,0:T(1,128)S(1)} collective-permute-done((f32[1,4096]{1,0:T(1,128)S(1)}, f32[1,4096]{1,0:T(1,128)S(1)}, u32[]{:S(2)}, u32[]{:S(2)}) %collective-permute-start.22) | collective-permute-done | bytes 16416 | tf_op jit(solution)/shard_map/ppermute | solution.py:24
  141.9 5.4 %dv4.1 = (f32[1,4096]{1,0:T(1,128)S(1)}, f32[1,4096]{1,0:T(1,128)S(1)}) custom-call(f32[1,4096]{1,0:T(1,128)S(1)} %log_add_fusion.pa, f32[1,4096]{1,0:T(1,128)S(1)} %collective-permute-done.22.pb, f32[1,1024]{1,0:T(1,128)S(1)} %get-tuple-element.80.u.refs_4_, f32[1,1024]{1,0:T(1,128)S(1)} %copy-done.12, bf16[1024,128]{1,0:T(8,128)(2,1)S(1)} %copy-done.4, ...), custom_call_target="tpu_custom_call" | custom-call | tf_op jit(solution)/shard_map/dv4/pallas_call | solution.py:141
  155.1 6.4 %du4.1 = (f32[1,4096]{1,0:T(1,128)S(1)}, f32[1,1024]{1,0:T(1,128)S(1)}) custom-call(f32[1,4096]{1,0:T(1,128)S(1)} %add.115.pa, f32[1,4096]{1,0:T(1,128)S(1)} %collective-permute-done.25.pb, f32[1,1024]{1,0:T(1,128)S(1)} %get-tuple-element.80.u.refs_4_, f32[1,4096]{1,0:T(1,128)S(1)} %get-tuple-element.83.v.refs_9_, f32[1,1024]{1,0:T(1,128)S(1)} %copy-done.12, ...), custom_call_target="tpu_custom_call" | custom-call | tf_op jit(solution)/shard_map/du4/pallas_call | solution.py:141
  164.0 4.2 %dv3.1 = (f32[1,1024]{1,0:T(1,128)S(1)}, f32[1,4096]{1,0:T(1,128)S(1)}) custom-call(f32[1,1024]{1,0:T(1,128)S(1)} %get-tuple-element.85.pa, f32[1,1024]{1,0:T(1,128)S(1)} %collective-permute-done.26.pb, f32[1,1024]{1,0:T(1,128)S(1)} %get-tuple-element.80.u.refs_4_, f32[1,4096]{1,0:T(1,128)S(1)} %get-tuple-element.79.v_old.v.refs_8_, ...), custom_call_target="tpu_custom_call" | custom-call | tf_op jit(solution)/shard_map/dv3/pallas_call | solution.py:141
  177.2 4.8 %du3.1 = (f32[1,4096]{1,0:T(1,128)S(1)}, f32[1,1024]{1,0:T(1,128)S(1)}) custom-call(f32[1,4096]{1,0:T(1,128)S(1)} %add.117.pa, f32[1,4096]{1,0:T(1,128)S(1)} %collective-permute-done.29.pb, f32[1,1024]{1,0:T(1,128)S(1)} %get-tuple-element.76.u_old.u.refs_3_, f32[1,4096]{1,0:T(1,128)S(1)} %get-tuple-element.79.v_old.v.refs_8_, f32[1,1024]{1,0:T(1,128)S(1)} %copy-done.12, ...), custom_call_target="tpu_custom_call" | custom-call | tf_op jit(solution)/shard_map/du3/pallas_call | solution.py:141
  184.5 4.2 %dv2.1 = (f32[1,1024]{1,0:T(1,128)S(1)}, f32[1,4096]{1,0:T(1,128)S(1)}) custom-call(f32[1,1024]{1,0:T(1,128)S(1)} %get-tuple-element.87.pa, f32[1,1024]{1,0:T(1,128)S(1)} %collective-permute-done.30.pb, f32[1,1024]{1,0:T(1,128)S(1)} %get-tuple-element.76.u_old.u.refs_3_, f32[1,4096]{1,0:T(1,128)S(1)} %get-tuple-element.75.v_old.v.refs_7_, ...), custom_call_target="tpu_custom_call" | custom-call | tf_op jit(solution)/shard_map/dv2/pallas_call | solution.py:141
  197.7 4.8 %du2.1 = (f32[1,4096]{1,0:T(1,128)S(1)}, f32[1,1024]{1,0:T(1,128)S(1)}) custom-call(f32[1,4096]{1,0:T(1,128)S(1)} %add.119.pa, f32[1,4096]{1,0:T(1,128)S(1)} %collective-permute-done.33.pb, f32[1,1024]{1,0:T(1,128)S(1)} %get-tuple-element.72.u_old.u.refs_2_, f32[1,4096]{1,0:T(1,128)S(1)} %get-tuple-element.75.v_old.v.refs_7_, f32[1,1024]{1,0:T(1,128)S(1)} %copy-done.12, ...), custom_call_target="tpu_custom_call" | custom-call | tf_op jit(solution)/shard_map/du2/pallas_call | solution.py:141
  205.3 4.2 %dv1.1 = (f32[1,1024]{1,0:T(1,128)S(1)}, f32[1,4096]{1,0:T(1,128)S(1)}) custom-call(f32[1,1024]{1,0:T(1,128)S(1)} %get-tuple-element.89.pa, f32[1,1024]{1,0:T(1,128)S(1)} %collective-permute-done.34.pb, f32[1,1024]{1,0:T(1,128)S(1)} %get-tuple-element.72.u_old.u.refs_2_, f32[1,4096]{1,0:T(1,128)S(1)} %get-tuple-element.71.v_old.v.refs_6_, ...), custom_call_target="tpu_custom_call" | custom-call | tf_op jit(solution)/shard_map/dv1/pallas_call | solution.py:141
  215.3 3.1 %collective-permute-done.37.pb = f32[1,4096]{1,0:T(1,128)S(1)} collective-permute-done((f32[1,4096]{1,0:T(1,128)S(1)}, f32[1,4096]{1,0:T(1,128)S(1)}, u32[]{:S(2)}, u32[]{:S(2)}) %collective-permute-start.37) | collective-permute-done | bytes 16416 | tf_op jit(solution)/shard_map/ppermute | solution.py:24
  218.4 4.8 %du1.1 = (f32[1,4096]{1,0:T(1,128)S(1)}, f32[1,1024]{1,0:T(1,128)S(1)}) custom-call(f32[1,4096]{1,0:T(1,128)S(1)} %add.121.pa, f32[1,4096]{1,0:T(1,128)S(1)} %collective-permute-done.37.pb, f32[1,1024]{1,0:T(1,128)S(1)} %get-tuple-element.68.u_old.u.refs_1_, f32[1,4096]{1,0:T(1,128)S(1)} %get-tuple-element.71.v_old.v.refs_6_, f32[1,1024]{1,0:T(1,128)S(1)} %copy-done.12, ...), custom_call_target="tpu_custom_call" | custom-call | tf_op jit(solution)/shard_map/du1/pallas_call | solution.py:141
  225.8 4.2 %dv0.1 = (f32[1,1024]{1,0:T(1,128)S(1)}, f32[1,4096]{1,0:T(1,128)S(1)}) custom-call(f32[1,1024]{1,0:T(1,128)S(1)} %get-tuple-element.91.pa, f32[1,1024]{1,0:T(1,128)S(1)} %collective-permute-done.38.pb, f32[1,1024]{1,0:T(1,128)S(1)} %get-tuple-element.68.u_old.u.refs_1_, f32[1,4096]{1,0:T(1,128)S(1)} %get-tuple-element.67.v_old.v.refs_5_, ...), custom_call_target="tpu_custom_call" | custom-call | tf_op jit(solution)/shard_map/dv0/pallas_call | solution.py:141
  238.9 4.8 %du0.1 = (f32[1,4096]{1,0:T(1,128)S(1)}, f32[1,1024]{1,0:T(1,128)S(1)}) custom-call(f32[1,4096]{1,0:T(1,128)S(1)} %add.123.pa, f32[1,4096]{1,0:T(1,128)S(1)} %collective-permute-done.41.pb, f32[1,1024]{1,0:T(1,128)S(1)} %get-tuple-element.64.u_old.u.refs_0_, f32[1,4096]{1,0:T(1,128)S(1)} %get-tuple-element.67.v_old.v.refs_5_, f32[1,1024]{1,0:T(1,128)S(1)} %copy-done.12, ...), custom_call_target="tpu_custom_call" | custom-call | tf_op jit(solution)/shard_map/du0/pallas_call | solution.py:141
  246.3 8.0 %final.1 = (bf16[4,32,128]{2,1,0:T(8,128)(2,1)S(1)}, bf16[32,32,128]{2,1,0:T(8,128)(2,1)S(1)}, f32[1,256]{1,0:T(1,128)}) custom-call(s32[2]{0:T(128)S(1)} %pad_add_fusion.place, bf16[4096,128]{1,0:T(8,128)(2,1)S(1)} %copy-done.9, bf16[1024,128]{1,0:T(8,128)(2,1)S(1)} %copy-done.4, bf16[64,1024]{1,0:T(8,128)(2,1)S(1)} %copy-done.6, f32[1,1024]{1,0:T(1,128)S(1)} %copy-done.12, ...), custom_call_target="tpu_custom_call" | custom-call | tf_op jit(solution)/shard_map/final/pallas_call | solution.py:520
  254.3 8.2 %all_to_all.16.row_parts = bf16[4,32,128]{2,1,0:T(8,128)(2,1)} all-to-all(bf16[4,32,128]{2,1,0:T(8,128)(2,1)S(1)} %get-tuple-element.103), channel_id=1, replica_groups=mesh['z'=4,'y'=4,'c'=2,'x'=4] {'x'}, dimensions={0} | all-to-all | bytes 65536 | tf_op jit(solution)/shard_map/all_to_all | solution.py:552
  262.5 15.2 %all_to_all.17.col_parts = bf16[32,32,128]{2,1,0:T(8,128)(2,1)} all-to-all(bf16[32,32,128]{2,1,0:T(8,128)(2,1)S(1)} %get-tuple-element.104), channel_id=1, replica_groups=mesh['z'=4,'y'=4,'c'=2,'x'=4] {'z','y','c'}, dimensions={0} | all-to-all | bytes 524288 | tf_op jit(solution)/shard_map/all_to_all | solution.py:553
  (141 shorter events, 116.0 us)
Async XLA Ops:
  21.6 11.7 %collective-permute-start = (bf16[16,128,128]{2,1,0:T(8,128)(2,1)S(1)}, bf16[16,128,128]{2,1,0:T(8,128)(2,1)S(1)}, u32[]{:S(2)}, u32[]{:S(2)}) collective-permute-start(bf16[16,128,128]{2,1,0:T(8,128)(2,1)S(1)} %all_to_all.15.mine), channel_id=1, source_target_pairs={{0,4},{1,5},{2,6},{3,7},{4,0},{5,1},{6,2},{7,3},{8,12},{9,13},{10,... | collective-permute-start | bytes 1572872 | tf_op jit(solution)/shard_map/ppermute | solution.py:24
  23.6 4.3 %collective-permute-start.1 = (bf16[144,128]{1,0:T(8,128)(2,1)S(1)}, bf16[144,128]{1,0:T(8,128)(2,1)S(1)}, u32[]{:S(2)}, u32[]{:S(2)}) collective-permute-start(bf16[144,128]{1,0:T(8,128)(2,1)S(1)} %copy-done.15), channel_id=1, source_target_pairs={{0,16},{1,17},{2,18},{3,19},{4,20},{5,21},{6,22},{7,23},{8,24},{9,... | collective-permute-start | bytes 110600 | tf_op jit(solution)/shard_map/ppermute | solution.py:24
  28.6 4.7 %collective-permute-start.2 = (bf16[2,144,128]{2,1,0:T(8,128)(2,1)S(1)}, bf16[2,144,128]{2,1,0:T(8,128)(2,1)S(1)}, u32[]{:S(2)}, u32[]{:S(2)}) collective-permute-start(bf16[2,144,128]{2,1,0:T(8,128)(2,1)S(1)} %pad_maximum_fusion), channel_id=1, source_target_pairs={{0,64},{1,65},{2,66},{3,67},{4,68},{5,69},{6,70},{7,71},{8,72},{9,... | collective-permute-start | bytes 221192 | tf_op jit(solution)/shard_map/ppermute | solution.py:24
  46.8 2.5 collective-permute-start.3
  55.2 4.5 %collective-permute-start.4 = (f32[1,4096]{1,0:T(1,128)S(1)}, f32[1,4096]{1,0:T(1,128)S(1)}, u32[]{:S(2)}, u32[]{:S(2)}) collective-permute-start(f32[1,4096]{1,0:T(1,128)S(1)} %get-tuple-element.65), channel_id=1, source_target_pairs={{0,4},{1,5},{2,6},{3,7},{4,0},{5,1},{6,2},{7,3},{8,12},{9,13},{10,... | collective-permute-start | bytes 49160 | tf_op jit(solution)/shard_map/ppermute | solution.py:24
  59.8 3.2 %collective-permute-start.5 = (f32[1,4096]{1,0:T(1,128)S(1)}, f32[1,4096]{1,0:T(1,128)S(1)}, u32[]{:S(2)}, u32[]{:S(2)}) collective-permute-start(f32[1,4096]{1,0:T(1,128)S(1)} %log_add_fusion.9), channel_id=1, source_target_pairs={{0,12},{1,13},{2,14},{3,15},{4,8},{5,9},{6,10},{7,11},{8,4},{9,5},... | collective-permute-start | bytes 49160 | tf_op jit(solution)/shard_map/ppermute | solution.py:24
  63.1 3.2 %collective-permute-start.6 = (f32[1,4096]{1,0:T(1,128)S(1)}, f32[1,4096]{1,0:T(1,128)S(1)}, u32[]{:S(2)}, u32[]{:S(2)}) collective-permute-start(f32[1,4096]{1,0:T(1,128)S(1)} %log_add_fusion.8.pa), channel_id=1, source_target_pairs={{0,36},{1,37},{2,38},{3,39},{4,32},{5,33},{6,34},{7,35},{8,44},{9,... | collective-permute-start | bytes 49160 | tf_op jit(solution)/shard_map/ppermute | solution.py:24
  70.3 2.5 collective-permute-start.7
  78.6 3.2 %collective-permute-start.9 = (f32[1,4096]{1,0:T(1,128)S(1)}, f32[1,4096]{1,0:T(1,128)S(1)}, u32[]{:S(2)}, u32[]{:S(2)}) collective-permute-start(f32[1,4096]{1,0:T(1,128)S(1)} %log_add_fusion.7), channel_id=1, source_target_pairs={{0,12},{1,13},{2,14},{3,15},{4,8},{5,9},{6,10},{7,11},{8,4},{9,5},... | collective-permute-start | bytes 49160 | tf_op jit(solution)/shard_map/ppermute | solution.py:24
  81.9 3.2 %collective-permute-start.10 = (f32[1,4096]{1,0:T(1,128)S(1)}, f32[1,4096]{1,0:T(1,128)S(1)}, u32[]{:S(2)}, u32[]{:S(2)}) collective-permute-start(f32[1,4096]{1,0:T(1,128)S(1)} %log_add_fusion.6.pa), channel_id=1, source_target_pairs={{0,36},{1,37},{2,38},{3,39},{4,32},{5,33},{6,34},{7,35},{8,44},{9,... | collective-permute-start | bytes 49160 | tf_op jit(solution)/shard_map/ppermute | solution.py:24
  89.1 2.5 collective-permute-start.11
  97.5 3.2 %collective-permute-start.13 = (f32[1,4096]{1,0:T(1,128)S(1)}, f32[1,4096]{1,0:T(1,128)S(1)}, u32[]{:S(2)}, u32[]{:S(2)}) collective-permute-start(f32[1,4096]{1,0:T(1,128)S(1)} %log_add_fusion.5), channel_id=1, source_target_pairs={{0,12},{1,13},{2,14},{3,15},{4,8},{5,9},{6,10},{7,11},{8,4},{9,5},... | collective-permute-start | bytes 49160 | tf_op jit(solution)/shard_map/ppermute | solution.py:24
  100.8 3.2 %collective-permute-start.14 = (f32[1,4096]{1,0:T(1,128)S(1)}, f32[1,4096]{1,0:T(1,128)S(1)}, u32[]{:S(2)}, u32[]{:S(2)}) collective-permute-start(f32[1,4096]{1,0:T(1,128)S(1)} %log_add_fusion.4.pa), channel_id=1, source_target_pairs={{0,36},{1,37},{2,38},{3,39},{4,32},{5,33},{6,34},{7,35},{8,44},{9,... | collective-permute-start | bytes 49160 | tf_op jit(solution)/shard_map/ppermute | solution.py:24
  108.0 2.5 collective-permute-start.15
  116.3 3.2 %collective-permute-start.17 = (f32[1,4096]{1,0:T(1,128)S(1)}, f32[1,4096]{1,0:T(1,128)S(1)}, u32[]{:S(2)}, u32[]{:S(2)}) collective-permute-start(f32[1,4096]{1,0:T(1,128)S(1)} %log_add_fusion.3), channel_id=1, source_target_pairs={{0,12},{1,13},{2,14},{3,15},{4,8},{5,9},{6,10},{7,11},{8,4},{9,5},... | collective-permute-start | bytes 49160 | tf_op jit(solution)/shard_map/ppermute | solution.py:24
  119.6 3.4 %collective-permute-start.18 = (f32[1,4096]{1,0:T(1,128)S(1)}, f32[1,4096]{1,0:T(1,128)S(1)}, u32[]{:S(2)}, u32[]{:S(2)}) collective-permute-start(f32[1,4096]{1,0:T(1,128)S(1)} %log_add_fusion.2.pa), channel_id=1, source_target_pairs={{0,36},{1,37},{2,38},{3,39},{4,32},{5,33},{6,34},{7,35},{8,44},{9,... | collective-permute-start | bytes 49160 | tf_op jit(solution)/shard_map/ppermute | solution.py:24
  135.4 3.2 %collective-permute-start.21 = (f32[1,4096]{1,0:T(1,128)S(1)}, f32[1,4096]{1,0:T(1,128)S(1)}, u32[]{:S(2)}, u32[]{:S(2)}) collective-permute-start(f32[1,4096]{1,0:T(1,128)S(1)} %log_add_fusion.1), channel_id=1, source_target_pairs={{0,12},{1,13},{2,14},{3,15},{4,8},{5,9},{6,10},{7,11},{8,4},{9,5},... | collective-permute-start | bytes 49160 | tf_op jit(solution)/shard_map/ppermute | solution.py:24
  138.7 3.2 %collective-permute-start.22 = (f32[1,4096]{1,0:T(1,128)S(1)}, f32[1,4096]{1,0:T(1,128)S(1)}, u32[]{:S(2)}, u32[]{:S(2)}) collective-permute-start(f32[1,4096]{1,0:T(1,128)S(1)} %log_add_fusion.pa), channel_id=1, source_target_pairs={{0,36},{1,37},{2,38},{3,39},{4,32},{5,33},{6,34},{7,35},{8,44},{9,... | collective-permute-start | bytes 49160 | tf_op jit(solution)/shard_map/ppermute | solution.py:24
  148.6 3.2 %collective-permute-start.24 = (f32[1,4096]{1,0:T(1,128)S(1)}, f32[1,4096]{1,0:T(1,128)S(1)}, u32[]{:S(2)}, u32[]{:S(2)}) collective-permute-start(f32[1,4096]{1,0:T(1,128)S(1)} %add.114), channel_id=1, source_target_pairs={{0,12},{1,13},{2,14},{3,15},{4,8},{5,9},{6,10},{7,11},{8,4},{9,5},... | collective-permute-start | bytes 49160 | tf_op jit(solution)/shard_map/ppermute | solution.py:24
  151.8 3.2 %collective-permute-start.25 = (f32[1,4096]{1,0:T(1,128)S(1)}, f32[1,4096]{1,0:T(1,128)S(1)}, u32[]{:S(2)}, u32[]{:S(2)}) collective-permute-start(f32[1,4096]{1,0:T(1,128)S(1)} %add.115.pa), channel_id=1, source_target_pairs={{0,36},{1,37},{2,38},{3,39},{4,32},{5,33},{6,34},{7,35},{8,44},{9,... | collective-permute-start | bytes 49160 | tf_op jit(solution)/shard_map/ppermute | solution.py:24
  161.5 2.5 collective-permute-start.26
  170.7 3.2 %collective-permute-start.28 = (f32[1,4096]{1,0:T(1,128)S(1)}, f32[1,4096]{1,0:T(1,128)S(1)}, u32[]{:S(2)}, u32[]{:S(2)}) collective-permute-start(f32[1,4096]{1,0:T(1,128)S(1)} %add.116), channel_id=1, source_target_pairs={{0,12},{1,13},{2,14},{3,15},{4,8},{5,9},{6,10},{7,11},{8,4},{9,5},... | collective-permute-start | bytes 49160 | tf_op jit(solution)/shard_map/ppermute | solution.py:24
  173.9 3.2 %collective-permute-start.29 = (f32[1,4096]{1,0:T(1,128)S(1)}, f32[1,4096]{1,0:T(1,128)S(1)}, u32[]{:S(2)}, u32[]{:S(2)}) collective-permute-start(f32[1,4096]{1,0:T(1,128)S(1)} %add.117.pa), channel_id=1, source_target_pairs={{0,36},{1,37},{2,38},{3,39},{4,32},{5,33},{6,34},{7,35},{8,44},{9,... | collective-permute-start | bytes 49160 | tf_op jit(solution)/shard_map/ppermute | solution.py:24
  182.0 2.5 collective-permute-start.30
  191.2 3.2 %collective-permute-start.32 = (f32[1,4096]{1,0:T(1,128)S(1)}, f32[1,4096]{1,0:T(1,128)S(1)}, u32[]{:S(2)}, u32[]{:S(2)}) collective-permute-start(f32[1,4096]{1,0:T(1,128)S(1)} %add.118), channel_id=1, source_target_pairs={{0,12},{1,13},{2,14},{3,15},{4,8},{5,9},{6,10},{7,11},{8,4},{9,5},... | collective-permute-start | bytes 49160 | tf_op jit(solution)/shard_map/ppermute | solution.py:24
  194.4 3.2 %collective-permute-start.33 = (f32[1,4096]{1,0:T(1,128)S(1)}, f32[1,4096]{1,0:T(1,128)S(1)}, u32[]{:S(2)}, u32[]{:S(2)}) collective-permute-start(f32[1,4096]{1,0:T(1,128)S(1)} %add.119.pa), channel_id=1, source_target_pairs={{0,36},{1,37},{2,38},{3,39},{4,32},{5,33},{6,34},{7,35},{8,44},{9,... | collective-permute-start | bytes 49160 | tf_op jit(solution)/shard_map/ppermute | solution.py:24
  202.5 2.8 collective-permute-start.34
  211.9 3.2 %collective-permute-start.36 = (f32[1,4096]{1,0:T(1,128)S(1)}, f32[1,4096]{1,0:T(1,128)S(1)}, u32[]{:S(2)}, u32[]{:S(2)}) collective-permute-start(f32[1,4096]{1,0:T(1,128)S(1)} %add.120), channel_id=1, source_target_pairs={{0,12},{1,13},{2,14},{3,15},{4,8},{5,9},{6,10},{7,11},{8,4},{9,5},... | collective-permute-start | bytes 49160 | tf_op jit(solution)/shard_map/ppermute | solution.py:24
  215.2 3.2 %collective-permute-start.37 = (f32[1,4096]{1,0:T(1,128)S(1)}, f32[1,4096]{1,0:T(1,128)S(1)}, u32[]{:S(2)}, u32[]{:S(2)}) collective-permute-start(f32[1,4096]{1,0:T(1,128)S(1)} %add.121.pa), channel_id=1, source_target_pairs={{0,36},{1,37},{2,38},{3,39},{4,32},{5,33},{6,34},{7,35},{8,44},{9,... | collective-permute-start | bytes 49160 | tf_op jit(solution)/shard_map/ppermute | solution.py:24
  223.2 2.5 collective-permute-start.38
  232.4 3.2 %collective-permute-start.40 = (f32[1,4096]{1,0:T(1,128)S(1)}, f32[1,4096]{1,0:T(1,128)S(1)}, u32[]{:S(2)}, u32[]{:S(2)}) collective-permute-start(f32[1,4096]{1,0:T(1,128)S(1)} %add.122), channel_id=1, source_target_pairs={{0,12},{1,13},{2,14},{3,15},{4,8},{5,9},{6,10},{7,11},{8,4},{9,5},... | collective-permute-start | bytes 49160 | tf_op jit(solution)/shard_map/ppermute | solution.py:24
  235.7 3.2 %collective-permute-start.41 = (f32[1,4096]{1,0:T(1,128)S(1)}, f32[1,4096]{1,0:T(1,128)S(1)}, u32[]{:S(2)}, u32[]{:S(2)}) collective-permute-start(f32[1,4096]{1,0:T(1,128)S(1)} %add.123.pa), channel_id=1, source_target_pairs={{0,36},{1,37},{2,38},{3,39},{4,32},{5,33},{6,34},{7,35},{8,44},{9,... | collective-permute-start | bytes 49160 | tf_op jit(solution)/shard_map/ppermute | solution.py:24
  (29 other events, 161.0 us)
where the time goes:
time: 280 us; the launch traced here: 279 us
  Pallas kernels  100 us (36%)
  waiting for transfers between devices  85.9 us (31%)
  blocking collectives  42.6 us (15%)
  starting transfers between devices  40.1 us (14%)
  local copies, waits for them, and re-layouts  8.24 us (3%)
    ppermute x43, waiting for transfers between devices, swap(): return lax.ppermute(value, AXES, [(i, i ^ bits) for i in range(128)])  85.9 us
    pallas_call x20, Pallas kernels, call(): pl.pallas_call(kernel, name=name, out_shape=tuple((jax.ShapeDtypeStruct(s...  83.9 us
    ppermute x43, starting transfers between devices, swap(): return lax.ppermute(value, AXES, [(i, i ^ bits) for i in range(128)])  40.1 us
    all_to_all x1, blocking collectives, local(): mine = lax.all_to_all(payload, ('z', 'y'), 0, 0, tiled=True)  19.1 us
    all_to_all x1, blocking collectives, local(): col_parts = lax.all_to_all(col_out, ('z', 'y', 'c'), 0, 0, tiled=True)  15.2 us
    unnamed x36, local copies, waits for them, and re-layouts  8.23 us
    all_to_all x1, blocking collectives, local(): row_parts = lax.all_to_all(row_out, 'x', 0, 0, tiled=True)  8.21 us
    pallas_call x1, Pallas kernels, local(): pl.pallas_call(functools.partial(final_kernel, scale, log_count), name='f...  7.96 us
  transfers between devices with their start and end apart: 43, of which 42 were waited for; matrix products, arithmetic and copies ran while one was open for 0% of the time, Pallas kernels for 0%

commit v1 on v0

--- a/solution.py
+++ b/solution.py
@@ -14,8 +14,7 @@
 X0, CORE, Y0, Y1, Z0, Z1 = 1, 4, 8, 16, 32, 64
 LW_TOP = 145.0
 TINY = 1e-37
-BLOCK = 256
-SPAN = 1024
+SMALL = pltpu.CompilerParams(vmem_limit_bytes=24 * 2**20)
 F32 = jnp.float32
 BF16 = jnp.bfloat16
 
@@ -65,85 +64,89 @@
     return out.astype(BF16)
 
 
-def tile_pass(mode, left, right, rows, cols, left_x, right_x, emit, pair=None):
+def shape_of(rows, cols):
+    return (256, cols) if rows > cols else (rows // 2, 512)
+
+
+def room(rows, cols, mode="exp"):
+    b, s = shape_of(rows, cols)
+    shapes = [(b, s)] * 2
+    if mode in ("weight", "pair_weight"):
+        shapes += [(b, 128)] * 2
+    if mode in ("pair", "pair_weight"):
+        shapes += [(b, s)] * 2
+    return [pltpu.VMEM((16, rows), BF16), pltpu.VMEM((16, cols), BF16)] + [
+        pltpu.VMEM(shape, F32) for shape in shapes
+    ]
+
+
+def tile_pass(mode, left, right, rows, cols, scratch, emit, pair=None):
+    left_x, right_x, scratch = scratch[0], scratch[1], scratch[2:]
+    height, span = shape_of(rows, cols)
+    slots, scratch = scratch[:2], scratch[2:]
     weighted = mode in ("weight", "pair_weight")
     if weighted:
+        weights, scratch = scratch[:2], scratch[2:]
         at = lax.broadcasted_iota(jnp.int32, (128, 128), 0)
         pick = jnp.where((at >= 70) & (at < 73), 1.0, 0.0).astype(BF16)
-    low = jnp.zeros((64, BLOCK), BF16)
-    high = jnp.zeros((48, BLOCK), BF16)
-
-    def block(m0, right_block, pair_block, acc):
-        x = jnp.concatenate([low, left_x[:, pl.ds(m0, BLOCK)], high], axis=0)
-        a = left[pl.ds(m0, BLOCK), :] + x.T
-        t = mm(a, right_block)
-        if mode == "max":
-            e = t
-        else:
-            e = jnp.exp(t)
+    pairs = scratch
+    low = jnp.zeros((64, height), BF16)
+    high = jnp.zeros((48, height), BF16)
+    tail = jnp.zeros((48, span), BF16)
+    n_m, n_n = rows // height, cols // span
+
+    def fill(i, slot):
+        m = pl.ds(pl.multiple_of((i % n_m) * height, height), height)
+        n = pl.ds(pl.multiple_of((i // n_m) * span, span), span)
+        a = left[m, :] + jnp.concatenate([low, left_x[:, m], high], axis=0).T
+        slots[slot][...] = mm(a, jnp.concatenate([right[:, n], right_x[:, n], tail], axis=0))
         if weighted:
-            w = mm(a, pick)
+            weights[slot][...] = mm(a, pick)
         if pair is not None:
-            pr = mm(pair[0][pl.ds(m0, BLOCK), :], pair_block)
+            pairs[slot][...] = mm(pair[0][m, :], pair[1][:, n])
+
+    def use(slot, acc):
         out = []
-        for q in range(SPAN // 128):
-            y = e[:, q * 128 : (q + 1) * 128]
+        for q in range(span // 128):
+            lanes = slice(q * 128, (q + 1) * 128)
+            y = jnp.exp(slots[slot][:, lanes])
             if mode == "weight":
-                y = y * w
+                y = y * weights[slot][...]
             elif mode == "pair":
-                y = y * pr[:, q * 128 : (q + 1) * 128]
+                y = y * pairs[slot][:, lanes]
             elif mode == "pair_weight":
-                y = y * (pr[:, q * 128 : (q + 1) * 128] - w)
-            y = y.reshape(BLOCK // 8, 8, 128)
-            if mode == "max":
-                out.append(jnp.maximum(acc[q], jnp.max(y, axis=0)))
-            else:
-                out.append(acc[q] + jnp.sum(y, axis=0))
+                y = y * (pairs[slot][:, lanes] - weights[slot][...])
+            out.append(acc[q] + jnp.sum(y.reshape(height // 8, 8, 128), axis=0))
         return tuple(out)
 
-    def right_of(n0):
-        sl = pl.ds(n0, SPAN)
-        full = jnp.concatenate([right[:, sl], right_x[:, sl], jnp.zeros((48, SPAN), BF16)], axis=0)
-        return full, None if pair is None else pair[1][:, sl]
-
     def fold(acc):
-        if mode == "max":
-            return jnp.concatenate([jnp.max(a, axis=0, keepdims=True) for a in acc], axis=1)
         return jnp.concatenate([jnp.sum(a, axis=0, keepdims=True) for a in acc], axis=1)
 
-    start = jnp.full((8, 128), -jnp.inf if mode == "max" else 0.0, F32)
-    zero = (start,) * (SPAN // 128)
-    if rows > cols:
-        right_block, pair_block = right_of(0)
-
-        def step(i, acc):
-            for b in range(2):
-                m0 = pl.multiple_of((2 * i + b) * BLOCK, BLOCK)
-                acc = block(m0, right_block, pair_block, acc)
-            return acc
-
-        emit(0, fold(lax.fori_loop(0, rows // (2 * BLOCK), step, zero)))
-    else:
-
-        def step(i, carry):
-            n0 = pl.multiple_of(i * SPAN, SPAN)
-            right_block, pair_block = right_of(n0)
-            acc = zero
-            for b in range(SPAN // BLOCK):
-                acc = block(b * BLOCK, right_block, pair_block, acc)
-            emit(n0, fold(acc))
-            return carry
-
-        lax.fori_loop(0, cols // SPAN, step, 0)
-
-
-def call(kernel, name, out_shapes, scratch, *args):
+    zero = (jnp.zeros((8, 128), F32),) * (span // 128)
+    last = n_m * n_n - 1
+    fill(0, 0)
+
+    def step(i, acc):
+        fill(2 * i + 1, 1)
+        acc = use(0, acc)
+        fill(jnp.minimum(2 * i + 2, last), 0)
+        acc = use(1, acc)
+        if n_n > 1:
+            emit(pl.ds(pl.multiple_of(i * span, span), span), fold(acc))
+            return zero
+        return acc
+
+    acc = lax.fori_loop(0, (last + 1) // 2, step, zero)
+    if n_n == 1:
+        emit(slice(None), fold(acc))
+
+
+def call(kernel, out_shapes, scratch, *args):
     return pl.pallas_call(
         kernel,
-        name=name,
         out_shape=tuple(jax.ShapeDtypeStruct(s, d) for s, d in out_shapes),
         scratch_shapes=scratch,
-        compiler_params=pltpu.CompilerParams(vmem_limit_bytes=24 * 2**20),
+        compiler_params=SMALL,
     )(*args)
 
 
@@ -170,7 +173,7 @@
 
 
 def prep_kernel(
-    scale, place, mine, other, own, near, far, left_c, right_c, cot_t, both, sq_c, left_r, right_r, sq_r, lw
+    scale, place, mine, other, own, by_y, by_z, by_zy, left_c, right_c, cot_t, both, sq_c, left_r, right_r, sq_r, lw
 ):
     lane = lax.broadcasted_iota(jnp.int32, (128, 128), 1)
     core, y1, z1 = place[0], place[1], place[2]
@@ -196,9 +199,9 @@
     lax.fori_loop(0, chips, step, 0)
     sources = (
         (own[...], 2 * z1 + y1),
-        (near[...], 2 * z1 + 1 - y1),
-        (far[0], 2 * (1 - z1) + y1),
-        (far[1], 2 * (1 - z1) + 1 - y1),
+        (by_y[...], 2 * z1 + 1 - y1),
+        (by_z[...], 2 * (1 - z1) + y1),
+        (by_zy[...], 2 * (1 - z1) + 1 - y1),
     )
     for src, q in sources:
         block = src[:128].astype(F32) * (2.0 * scale)
@@ -228,7 +231,8 @@
     du_a, du_b, refs = refs[0], refs[1], refs[2:]
     dus, refs = refs[: ITERS - 1], refs[ITERS - 1 :]
     row_out, col_out, glw, stack, pick_v, right_x, turned, near, left_s, left_b, weight, acc_g, acc_q, mass = refs
-    q, x1 = place[0], place[1]
+    q, here = place[0], place[1]
+    x1 = here >> 1
     wide = stack.shape[1]
     n_t = wide // 2
     own = pl.ds(pl.multiple_of(q * 256, 256), 256)
@@ -306,30 +310,30 @@
     term = term.T
     for t in range(2):
         for j, chunk in enumerate(pair_up(term[:64, t * 128 : (t + 1) * 128])):
-            row_out[2 * j + t] = chunk
-
-
-def finish_kernel(row_parts, col_parts, out):
-    acc = row_parts[0].astype(F32)
-    for i in range(1, row_parts.shape[0]):
-        acc = acc + row_parts[i].astype(F32)
+            row_out[(2 * j + t) ^ here] = chunk
+
+
+def finish_kernel(row_0, row_1, row_2, row_3, col_parts, out):
+    acc = (row_0[...].astype(F32) + row_1[...].astype(F32)) + (row_2[...].astype(F32) + row_3[...].astype(F32))
     for i in range(col_parts.shape[0]):
         acc = acc + col_parts[i].astype(F32)
     both = jnp.concatenate([acc, pltpu.roll(acc, 64, 1)], axis=0)
     out[...] = both.T[:64, :]
 
 
-def first_u(left_c, right_r, sq_c, sq_r, out, left_x, right_x):
+def first_u(left_c, right_r, sq_c, sq_r, out, *scratch):
+    left_x, right_x = scratch[:2]
     left_x[...] = extra(-sq_c[...], None, True)
     right_x[...] = extra(-sq_r[...], None, False)
 
-    def emit(n0, value):
+    def emit(at, value):
         out[...] = jnp.log(jnp.maximum(value, TINY))
 
-    tile_pass("exp", left_c, right_r, sq_c.shape[1], sq_r.shape[1], left_x, right_x, emit)
-
-
-def next_v(log_count, is_first, pa, pb, u_old, v_old, lw, left_r, right_c, sq_r, sq_c, u_new, out, left_x, right_x, base):
+    tile_pass("exp", left_c, right_r, sq_c.shape[1], sq_r.shape[1], scratch, emit)
+
+
+def next_v(log_count, is_first, pa, pb, u_old, v_old, lw, left_r, right_c, sq_r, sq_c, u_new, out, base, *scratch):
+    left_x, right_x = scratch[:2]
     u = log_count - merge(pa[...], pb[...])
     u_new[...] = u
     if is_first:
@@ -339,41 +343,43 @@
     left_x[...] = extra(u + lw[...] - sq_r[...], None, True)
     right_x[...] = extra(-sq_c[...] - base[...], None, False)
 
-    def emit(n0, value):
-        sl = pl.ds(n0, SPAN)
-        out[:, sl] = base[:, sl] + jnp.log(jnp.maximum(value, TINY))
-
-    tile_pass("exp", left_r, right_c, sq_r.shape[1], sq_c.shape[1], left_x, right_x, emit)
-
-
-def next_u(log_count, pa, pb, v_old, u_old, left_c, right_r, sq_c, sq_r, v_new, out, left_x, right_x):
+    def emit(at, value):
+        out[:, at] = base[:, at] + jnp.log(jnp.maximum(value, TINY))
+
+    tile_pass("exp", left_r, right_c, sq_r.shape[1], sq_c.shape[1], scratch, emit)
+
+
+def next_u(log_count, pa, pb, v_old, u_old, left_c, right_r, sq_c, sq_r, v_new, out, *scratch):
+    left_x, right_x = scratch[:2]
     v = -merge(pa[...], pb[...])
     v_new[...] = v
     base = (log_count - u_old[...]) + jnp.max(v - v_old[...], axis=1, keepdims=True)
     left_x[...] = extra(v - sq_c[...], None, True)
     right_x[...] = extra(-sq_r[...] - base, None, False)
 
-    def emit(n0, value):
+    def emit(at, value):
         out[...] = base + jnp.log(jnp.maximum(value, TINY))
 
-    tile_pass("exp", left_c, right_r, sq_c.shape[1], sq_r.shape[1], left_x, right_x, emit)
-
-
-def first_dv(unscale, pa, pb, u, lw, left_r, right_c, cot_t, sq_r, sq_c, v_new, out, left_x, right_x):
+    tile_pass("exp", left_c, right_r, sq_c.shape[1], sq_r.shape[1], scratch, emit)
+
+
+def first_dv(unscale, pa, pb, u, lw, left_r, right_c, cot_t, sq_r, sq_c, v_new, out, *scratch):
+    left_x, right_x = scratch[:2]
     v = -merge(pa[...], pb[...])
     v_new[...] = v
     left_x[...] = extra(u[...] + lw[...] - sq_r[...], None, True)
     right_x[...] = extra(v - sq_c[...], None, False)
 
-    def emit(n0, value):
-        out[:, pl.ds(n0, SPAN)] = unscale * value
+    def emit(at, value):
+        out[:, at] = unscale * value
 
     tile_pass(
-        "pair", left_r, right_c, sq_r.shape[1], sq_c.shape[1], left_x, right_x, emit, (left_r, cot_t)
+        "pair", left_r, right_c, sq_r.shape[1], sq_c.shape[1], scratch, emit, (left_r, cot_t)
     )
 
 
-def first_du(pa, pb, u, v, lw, left_c, right_r, both, sq_c, sq_r, dv_new, out, left_x, right_x, pair_r):
+def first_du(pa, pb, u, v, lw, left_c, right_r, both, sq_c, sq_r, dv_new, out, pair_r, *scratch):
+    left_x, right_x = scratch[:2]
     dv = pa[...] + pb[...]
     dv_new[...] = dv
     left_x[...] = extra(v[...] - sq_c[...], dv, True)
@@ -381,41 +387,43 @@
     pair_r[:64, :] = jnp.zeros_like(right_r)
     pair_r[64:, :] = right_r[...]
 
-    def emit(n0, value):
+    def emit(at, value):
         out[...] = value
 
     tile_pass(
-        "pair_weight", left_c, right_r, sq_c.shape[1], sq_r.shape[1], left_x, right_x, emit, (both, pair_r)
+        "pair_weight", left_c, right_r, sq_c.shape[1], sq_r.shape[1], scratch, emit, (both, pair_r)
     )
 
 
-def next_dv(log_count, pa, pb, u, v, left_r, right_c, sq_r, sq_c, du_new, out, left_x, right_x):
+def next_dv(log_count, pa, pb, u, v, left_r, right_c, sq_r, sq_c, du_new, out, *scratch):
+    left_x, right_x = scratch[:2]
     du = pa[...] + pb[...]
     du_new[...] = du
     left_x[...] = extra(u[...] - log_count - sq_r[...], du, True)
     right_x[...] = extra(v[...] - sq_c[...], None, False)
 
-    def emit(n0, value):
-        out[:, pl.ds(n0, SPAN)] = -value
-
-    tile_pass("weight", left_r, right_c, sq_r.shape[1], sq_c.shape[1], left_x, right_x, emit)
-
-
-def next_du(pa, pb, u, v, lw, left_c, right_r, sq_c, sq_r, dv_new, out, left_x, right_x):
+    def emit(at, value):
+        out[:, at] = -value
+
+    tile_pass("weight", left_r, right_c, sq_r.shape[1], sq_c.shape[1], scratch, emit)
+
+
+def next_du(pa, pb, u, v, lw, left_c, right_r, sq_c, sq_r, dv_new, out, *scratch):
+    left_x, right_x = scratch[:2]
     dv = pa[...] + pb[...]
     dv_new[...] = dv
     left_x[...] = extra(v[...] - sq_c[...], dv, True)
     right_x[...] = extra(u[...] + lw[...] - sq_r[...], None, False)
 
-    def emit(n0, value):
+    def emit(at, value):
         out[...] = -value
 
-    tile_pass("weight", left_c, right_r, sq_c.shape[1], sq_r.shape[1], left_x, right_x, emit)
+    tile_pass("weight", left_c, right_r, sq_c.shape[1], sq_r.shape[1], scratch, emit)
 
 
 def local(positions, log_weights, cotangent):
     z, y, core, x = (lax.axis_index(name) for name in AXES)
-    x0, x1, y1, z1 = x & 1, x >> 1, y >> 1, z >> 1
+    x0, y1, z1 = x & 1, y >> 1, z >> 1
     n_row, dim = positions.shape
     log_count = math.log(n_row * 32)
     scale = 4.0 / dim
@@ -425,17 +433,20 @@
     payload, own = pl.pallas_call(
         pack_kernel,
         name="pack",
+        compiler_params=SMALL,
         in_specs=[smem] + [vmem] * 3,
         out_shape=(jax.ShapeDtypeStruct((16, 128, 128), BF16), jax.ShapeDtypeStruct((144, 128), BF16)),
     )(x0.reshape(1), positions.T, cotangent.T, log_weights.reshape(1, n_row))
+    others = []
+    for bits in (Y1, Z1, Y1 | Z1):
+        others.append(swap(own, bits))
     mine = lax.all_to_all(payload, ("z", "y"), 0, 0, tiled=True)
-    near = swap(own, Y1)
-    far = swap(jnp.stack([own, near]), Z1)
     other = swap(mine, CORE)
     left_c, right_c, cot_t, both, sq_c, left_r, right_r, sq_r, lw = pl.pallas_call(
         functools.partial(prep_kernel, scale),
         name="prep",
-        in_specs=[smem] + [vmem] * 5,
+        compiler_params=SMALL,
+        in_specs=[smem] + [vmem] * 6,
         out_shape=tuple(
             jax.ShapeDtypeStruct(shape, kind)
             for shape, kind in (
@@ -450,21 +461,19 @@
                 ((1, n_r), F32),
             )
         ),
-    )(jnp.stack([core, y1, z1]), mine, other, own, near, far)
+    )(jnp.stack([core, y1, z1]), mine, other, own, *others)
 
     u_like, v_like = ((1, n_r), F32), ((1, n_c), F32)
-    x_r, x_c = pltpu.VMEM((16, n_r), BF16), pltpu.VMEM((16, n_c), BF16)
-
-    (part,) = call(first_u, "u0", (u_like,), [x_c, x_r], left_c, right_r, sq_c, sq_r)
+
+    (part,) = call(first_u, (u_like,), room(n_c, n_r), left_c, right_r, sq_c, sq_r)
     us, vs = [], [jnp.zeros((1, n_c), F32)]
     for k in range(ITERS):
         pa, pb = over_cols(part)
         old = us[-1] if us else sq_r
         u, part = call(
             functools.partial(next_v, log_count, k == 0),
-            f"v{k}",
             (u_like, v_like),
-            [x_r, x_c, pltpu.VMEM((1, n_c), F32)],
+            [pltpu.VMEM((1, n_c), F32)] + room(n_r, n_c),
             *(pa, pb, old, vs[-1], lw, left_r, right_c, sq_r, sq_c),
         )
         us.append(u)
@@ -473,27 +482,24 @@
             break
         v, part = call(
             functools.partial(next_u, log_count),
-            f"u{k + 1}",
             (v_like, u_like),
-            [x_c, x_r],
+            room(n_c, n_r),
             *(pa, pb, vs[-1], us[-1], left_c, right_r, sq_c, sq_r),
         )
         vs.append(v)
 
     v, part = call(
         functools.partial(first_dv, 0.5 / scale),
-        "dv4",
         (v_like, v_like),
-        [x_r, x_c],
+        room(n_r, n_c, "pair"),
         *(pa, pb, us[-1], lw, left_r, right_c, cot_t, sq_r, sq_c),
     )
     vs.append(v)
     pa, pb = over_rows(part, plus)
     dv, part = call(
         first_du,
-        "du4",
         (v_like, u_like),
-        [x_c, x_r, pltpu.VMEM((128, n_r), BF16)],
+        [pltpu.VMEM((128, n_r), BF16)] + room(n_c, n_r, "pair_weight"),
         *(pa, pb, us[-1], vs[-1], lw, left_c, right_r, both, sq_c, sq_r),
     )
     dus, dvs = [None] * ITERS, [None] * ITERS
@@ -502,17 +508,15 @@
         pa, pb = over_cols(part)
         dus[k + 1], part = call(
             functools.partial(next_dv, log_count),
-            f"dv{k}",
             (u_like, v_like),
-            [x_r, x_c],
+            room(n_r, n_c, "weight"),
             *(pa, pb, us[k + 1], vs[k + 1], left_r, right_c, sq_r, sq_c),
         )
         pa, pb = over_rows(part, plus)
         dvs[k], part = call(
             next_du,
-            f"du{k}",
             (v_like, u_like),
-            [x_c, x_r],
+            room(n_c, n_r, "weight"),
             *(pa, pb, us[k], vs[k + 1], lw, left_c, right_r, sq_c, sq_r),
         )
     pa, pb = over_cols(part)
@@ -539,9 +543,9 @@
             pltpu.VMEM((n_row, 128), F32),
             pltpu.VMEM((n_row, 128), F32),
         ],
-        compiler_params=pltpu.CompilerParams(vmem_limit_bytes=24 * 2**20),
+        compiler_params=SMALL,
     )(
-        jnp.stack([2 * z1 + y1, x1]),
+        jnp.stack([2 * z1 + y1, x]),
         *(both, left_r, right_r, lw, sq_r, sq_c),
         *us,
         *vs[1:],
@@ -549,11 +553,14 @@
         *(pa, pb),
         *dus[1:],
     )
-    row_parts = lax.all_to_all(row_out, "x", 0, 0, tiled=True)
+    row_parts = [row_out[0]] + [swap(row_out[bits], bits) for bits in (1, 2, 3)]
     col_parts = lax.all_to_all(col_out, ("z", "y", "c"), 0, 0, tiled=True)
     out = pl.pallas_call(
-        finish_kernel, name="finish", out_shape=jax.ShapeDtypeStruct((n_row // 4, dim), F32)
-    )(row_parts, col_parts)
+        finish_kernel,
+        name="finish",
+        compiler_params=SMALL,
+        out_shape=jax.ShapeDtypeStruct((n_row // 4, dim), F32),
+    )(*row_parts, col_parts)
     return (out, glw.reshape(n_row))
 
 

time: 280 us -> 276 us (0.986)
  blocking collectives: 42.6 us -> 18.8 us
  starting transfers between devices: 40.1 us -> 58.7 us
  Pallas kernels: 100 us -> 109 us
  local copies, waits for them, and re-layouts: 8.24 us -> 4.06 us
  waiting for transfers between devices: 85.9 us -> 82.6 us
    all_to_all x2 -> x0, blocking collectives: 23.4 us -> none  [the longest x1 15.2 us: local(): col_parts = lax.all_to_all(col_out, ('z', 'y', 'c'), 0, 0, tiled=True)]
    ppermute x43 -> x47, starting transfers between devices: 40.1 us -> 51.7 us  [swap(): return lax.ppermute(value, AXES, [(i, i ^ bits) for i in range(128)])]
    pallas_call x23, Pallas kernels: 92.2 us -> 101 us  [the longest x20 97.8 us: call(): pl.pallas_call(kernel, out_shape=tuple((jax.ShapeDtypeStruct(s, d) for s,...]
    all_to_all x0 -> x1, starting transfers between devices: none -> 7.06 us  [local(): col_parts = lax.all_to_all(col_out, ('z', 'y', 'c'), 0, 0, tiled=True)]
    ppermute x43 -> x47, waiting for transfers between devices: 85.9 us -> 81.5 us  [swap(): return lax.ppermute(value, AXES, [(i, i ^ bits) for i in range(128)])]
    unnamed x36 -> x10, local copies, waits for them, and re-layouts: 8.23 us -> 4.04 us
  transfers between devices with their start and end apart: 43 -> 48, of which waited for: 42 -> 44; matrix products, arithmetic and copies ran while one was open for 0% -> 0% of each run, Pallas kernels for 0% -> 0%
where the time goes in v1:
time: 276 us; the launch traced here: 275 us
  Pallas kernels  109 us (39%)
  waiting for transfers between devices  82.6 us (30%)
  starting transfers between devices  58.7 us (21%)
  blocking collectives  18.8 us (7%)
  local copies, waits for them, and re-layouts  4.06 us (1%)
    pallas_call x20, Pallas kernels, call(): pl.pallas_call(kernel, out_shape=tuple((jax.ShapeDtypeStruct(s, d) for s,...  97.8 us
    ppermute x47, waiting for transfers between devices, swap(): return lax.ppermute(value, AXES, [(i, i ^ bits) for i in range(128)])  81.5 us
    ppermute x47, starting transfers between devices, swap(): return lax.ppermute(value, AXES, [(i, i ^ bits) for i in range(128)])  51.7 us
    all_to_all x1, blocking collectives, local(): mine = lax.all_to_all(payload, ('z', 'y'), 0, 0, tiled=True)  18.8 us
    pallas_call x1, Pallas kernels, local(): pl.pallas_call(functools.partial(final_kernel, scale, log_count), name='f...  8.21 us
    all_to_all x1, starting transfers between devices, local(): col_parts = lax.all_to_all(col_out, ('z', 'y', 'c'), 0, 0, tiled=True)  7.06 us
  transfers between devices with their start and end apart: 48, of which 44 were waited for; matrix products, arithmetic and copies ran while one was open for 0% of the time, Pallas kernels for 0%

profile of v1, /device:TPU:1, one launch (start us, length us, event | category | flops | bytes accessed | tf_op | source)
XLA Modules:
  0.0 275.2 jit_solution(8516678129638308304)
XLA Ops:
  3.0 18.8 %all_to_all.10.mine = bf16[16,128,128]{2,1,0:T(8,128)(2,1)S(1)} all-to-all(bf16[16,128,128]{2,1,0:T(8,128)(2,1)S(1)} %get-tuple-element.54), channel_id=1, replica_groups=mesh['z'=4,'y'=4,'c'=2,'x'=4] {'z','y'}, dimensions={0} | all-to-all | bytes 1048576 | tf_op jit(solution)/shard_map/all_to_all | solution.py:443
  25.7 3.9 %collective-permute-start.3 = (bf16[144,128]{1,0:T(8,128)(2,1)S(1)}, bf16[144,128]{1,0:T(8,128)(2,1)S(1)}, u32[]{:S(2)}, u32[]{:S(2)}) collective-permute-start(bf16[144,128]{1,0:T(8,128)(2,1)S(1)} %get-tuple-element.55.own), channel_id=1, source_target_pairs={{0,80},{1,81},{2,82},{3,83},{4,84},{5,85},{6,86},{7,87},{8,88},{9,... | collective-permute-start | bytes 110600 | tf_op jit(solution)/shard_map/ppermute | solution.py:23
  29.7 2.8 collective-permute-done.3.by_zy
  36.3 4.0 %shard_map.50.pa = f32[1,1024]{1,0:T(1,128)S(1)} custom-call(bf16[4096,128]{1,0:T(8,128)(2,1)S(1)} %get-tuple-element.62.left_c, bf16[64,1024]{1,0:T(8,128)(2,1)S(1)} %get-tuple-element.58.right_r, f32[1,4096]{1,0:T(1,128)S(1)} %get-tuple-element.61.sq_c, f32[1,1024]{1,0:T(1,128)S(1)} %get-tuple-element.60.sq_r.u_old), custom_call_target="tpu_custom_call" | custom-call | tf_op jit(solution)/shard_map/pallas_call | solution.py:145
  42.9 4.4 %shard_map.51 = (f32[1,1024]{1,0:T(1,128)S(1)}, f32[1,4096]{1,0:T(1,128)S(1)}) custom-call(f32[1,1024]{1,0:T(1,128)S(1)} %shard_map.50.pa, f32[1,1024]{1,0:T(1,128)S(1)} %collective-permute-done.4.pb, f32[1,1024]{1,0:T(1,128)S(1)} %get-tuple-element.60.sq_r.u_old, f32[1,4096]{1,0:T(1,128)S(1)} %broadcast_in_dim.3.v_old, f32[1,1024]{1,0:T(1,128)S(1)} %get-tuple-element.59.lw, ...), custom_call_target="tpu_custom_call" | custom-call | tf_op jit(solution)/shard_map/pallas_call | solution.py:145
  47.3 3.0 %collective-permute-start.5 = (f32[1,4096]{1,0:T(1,128)S(1)}, f32[1,4096]{1,0:T(1,128)S(1)}, u32[]{:S(2)}, u32[]{:S(2)}) collective-permute-start(f32[1,4096]{1,0:T(1,128)S(1)} %get-tuple-element.65), channel_id=1, source_target_pairs={{0,4},{1,5},{2,6},{3,7},{4,0},{5,1},{6,2},{7,3},{8,12},{9,13},{10,... | collective-permute-start | bytes 49160 | tf_op jit(solution)/shard_map/ppermute | solution.py:23
  54.9 2.8 %collective-permute-done.7.pb = f32[1,4096]{1,0:T(1,128)S(1)} collective-permute-done((f32[1,4096]{1,0:T(1,128)S(1)}, f32[1,4096]{1,0:T(1,128)S(1)}, u32[]{:S(2)}, u32[]{:S(2)}) %collective-permute-start.7) | collective-permute-done | bytes 16416 | tf_op jit(solution)/shard_map/ppermute | solution.py:23
  57.7 4.1 %shard_map.52 = (f32[1,4096]{1,0:T(1,128)S(1)}, f32[1,1024]{1,0:T(1,128)S(1)}) custom-call(f32[1,4096]{1,0:T(1,128)S(1)} %log_add_fusion.8.pa, f32[1,4096]{1,0:T(1,128)S(1)} %collective-permute-done.7.pb, f32[1,4096]{1,0:T(1,128)S(1)} %broadcast_in_dim.3.v_old, f32[1,1024]{1,0:T(1,128)S(1)} %get-tuple-element.64.u_old.u.refs_0_, ...), custom_call_target="tpu_custom_call" | custom-call | tf_op jit(solution)/shard_map/pallas_call | solution.py:145
  64.3 4.4 %shard_map.53 = (f32[1,1024]{1,0:T(1,128)S(1)}, f32[1,4096]{1,0:T(1,128)S(1)}) custom-call(f32[1,1024]{1,0:T(1,128)S(1)} %get-tuple-element.66.pa, f32[1,1024]{1,0:T(1,128)S(1)} %collective-permute-done.8.pb, f32[1,1024]{1,0:T(1,128)S(1)} %get-tuple-element.64.u_old.u.refs_0_, f32[1,4096]{1,0:T(1,128)S(1)} %get-tuple-element.67.v_old.v.refs_5_, ...), custom_call_target="tpu_custom_call" | custom-call | tf_op jit(solution)/shard_map/pallas_call | solution.py:145
  75.1 2.8 %collective-permute-done.11.pb = f32[1,4096]{1,0:T(1,128)S(1)} collective-permute-done((f32[1,4096]{1,0:T(1,128)S(1)}, f32[1,4096]{1,0:T(1,128)S(1)}, u32[]{:S(2)}, u32[]{:S(2)}) %collective-permute-start.11) | collective-permute-done | bytes 16416 | tf_op jit(solution)/shard_map/ppermute | solution.py:23
  77.8 4.1 %shard_map.54 = (f32[1,4096]{1,0:T(1,128)S(1)}, f32[1,1024]{1,0:T(1,128)S(1)}) custom-call(f32[1,4096]{1,0:T(1,128)S(1)} %log_add_fusion.6.pa, f32[1,4096]{1,0:T(1,128)S(1)} %collective-permute-done.11.pb, f32[1,4096]{1,0:T(1,128)S(1)} %get-tuple-element.67.v_old.v.refs_5_, f32[1,1024]{1,0:T(1,128)S(1)} %get-tuple-element.68.u_old.u.refs_1_, ...), custom_call_target="tpu_custom_call" | custom-call | tf_op jit(solution)/shard_map/pallas_call | solution.py:145
  84.5 4.4 %shard_map.55 = (f32[1,1024]{1,0:T(1,128)S(1)}, f32[1,4096]{1,0:T(1,128)S(1)}) custom-call(f32[1,1024]{1,0:T(1,128)S(1)} %get-tuple-element.70.pa, f32[1,1024]{1,0:T(1,128)S(1)} %collective-permute-done.12.pb, f32[1,1024]{1,0:T(1,128)S(1)} %get-tuple-element.68.u_old.u.refs_1_, f32[1,4096]{1,0:T(1,128)S(1)} %get-tuple-element.71.v_old.v.refs_6_, ...), custom_call_target="tpu_custom_call" | custom-call | tf_op jit(solution)/shard_map/pallas_call | solution.py:145
  95.2 2.8 %collective-permute-done.15.pb = f32[1,4096]{1,0:T(1,128)S(1)} collective-permute-done((f32[1,4096]{1,0:T(1,128)S(1)}, f32[1,4096]{1,0:T(1,128)S(1)}, u32[]{:S(2)}, u32[]{:S(2)}) %collective-permute-start.15) | collective-permute-done | bytes 16416 | tf_op jit(solution)/shard_map/ppermute | solution.py:23
  98.0 4.1 %shard_map.56 = (f32[1,4096]{1,0:T(1,128)S(1)}, f32[1,1024]{1,0:T(1,128)S(1)}) custom-call(f32[1,4096]{1,0:T(1,128)S(1)} %log_add_fusion.4.pa, f32[1,4096]{1,0:T(1,128)S(1)} %collective-permute-done.15.pb, f32[1,4096]{1,0:T(1,128)S(1)} %get-tuple-element.71.v_old.v.refs_6_, f32[1,1024]{1,0:T(1,128)S(1)} %get-tuple-element.72.u_old.u.refs_2_, ...), custom_call_target="tpu_custom_call" | custom-call | tf_op jit(solution)/shard_map/pallas_call | solution.py:145
  104.6 4.4 %shard_map.57 = (f32[1,1024]{1,0:T(1,128)S(1)}, f32[1,4096]{1,0:T(1,128)S(1)}) custom-call(f32[1,1024]{1,0:T(1,128)S(1)} %get-tuple-element.74.pa, f32[1,1024]{1,0:T(1,128)S(1)} %collective-permute-done.16.pb, f32[1,1024]{1,0:T(1,128)S(1)} %get-tuple-element.72.u_old.u.refs_2_, f32[1,4096]{1,0:T(1,128)S(1)} %get-tuple-element.75.v_old.v.refs_7_, ...), custom_call_target="tpu_custom_call" | custom-call | tf_op jit(solution)/shard_map/pallas_call | solution.py:145
  115.5 2.8 %collective-permute-done.19.pb = f32[1,4096]{1,0:T(1,128)S(1)} collective-permute-done((f32[1,4096]{1,0:T(1,128)S(1)}, f32[1,4096]{1,0:T(1,128)S(1)}, u32[]{:S(2)}, u32[]{:S(2)}) %collective-permute-start.19) | collective-permute-done | bytes 16416 | tf_op jit(solution)/shard_map/ppermute | solution.py:23
  118.3 4.1 %shard_map.58 = (f32[1,4096]{1,0:T(1,128)S(1)}, f32[1,1024]{1,0:T(1,128)S(1)}) custom-call(f32[1,4096]{1,0:T(1,128)S(1)} %log_add_fusion.2.pa, f32[1,4096]{1,0:T(1,128)S(1)} %collective-permute-done.19.pb, f32[1,4096]{1,0:T(1,128)S(1)} %get-tuple-element.75.v_old.v.refs_7_, f32[1,1024]{1,0:T(1,128)S(1)} %get-tuple-element.76.u_old.u.refs_3_, ...), custom_call_target="tpu_custom_call" | custom-call | tf_op jit(solution)/shard_map/pallas_call | solution.py:145
  124.9 4.4 %shard_map.59 = (f32[1,1024]{1,0:T(1,128)S(1)}, f32[1,4096]{1,0:T(1,128)S(1)}) custom-call(f32[1,1024]{1,0:T(1,128)S(1)} %get-tuple-element.78.pa, f32[1,1024]{1,0:T(1,128)S(1)} %collective-permute-done.20.pb, f32[1,1024]{1,0:T(1,128)S(1)} %get-tuple-element.76.u_old.u.refs_3_, f32[1,4096]{1,0:T(1,128)S(1)} %get-tuple-element.79.v_old.v.refs_8_, ...), custom_call_target="tpu_custom_call" | custom-call | tf_op jit(solution)/shard_map/pallas_call | solution.py:145
  135.6 2.8 %collective-permute-done.23.pb = f32[1,4096]{1,0:T(1,128)S(1)} collective-permute-done((f32[1,4096]{1,0:T(1,128)S(1)}, f32[1,4096]{1,0:T(1,128)S(1)}, u32[]{:S(2)}, u32[]{:S(2)}) %collective-permute-start.23) | collective-permute-done | bytes 16416 | tf_op jit(solution)/shard_map/ppermute | solution.py:23
  138.4 6.8 %shard_map.60 = (f32[1,4096]{1,0:T(1,128)S(1)}, f32[1,4096]{1,0:T(1,128)S(1)}) custom-call(f32[1,4096]{1,0:T(1,128)S(1)} %log_add_fusion.pa, f32[1,4096]{1,0:T(1,128)S(1)} %collective-permute-done.23.pb, f32[1,1024]{1,0:T(1,128)S(1)} %get-tuple-element.80.u.refs_4_, f32[1,1024]{1,0:T(1,128)S(1)} %get-tuple-element.59.lw, ...), custom_call_target="tpu_custom_call" | custom-call | tf_op jit(solution)/shard_map/pallas_call | solution.py:145
  150.2 2.8 %collective-permute-done.26.pb = f32[1,4096]{1,0:T(1,128)S(1)} collective-permute-done((f32[1,4096]{1,0:T(1,128)S(1)}, f32[1,4096]{1,0:T(1,128)S(1)}, u32[]{:S(2)}, u32[]{:S(2)}) %collective-permute-start.26) | collective-permute-done | bytes 16416 | tf_op jit(solution)/shard_map/ppermute | solution.py:23
  153.0 7.2 %shard_map.61 = (f32[1,4096]{1,0:T(1,128)S(1)}, f32[1,1024]{1,0:T(1,128)S(1)}) custom-call(f32[1,4096]{1,0:T(1,128)S(1)} %add.115.pa, f32[1,4096]{1,0:T(1,128)S(1)} %collective-permute-done.26.pb, f32[1,1024]{1,0:T(1,128)S(1)} %get-tuple-element.80.u.refs_4_, f32[1,4096]{1,0:T(1,128)S(1)} %get-tuple-element.83.v.refs_9_, ...), custom_call_target="tpu_custom_call" | custom-call | tf_op jit(solution)/shard_map/pallas_call | solution.py:145
  162.8 5.2 %shard_map.62 = (f32[1,1024]{1,0:T(1,128)S(1)}, f32[1,4096]{1,0:T(1,128)S(1)}) custom-call(f32[1,1024]{1,0:T(1,128)S(1)} %get-tuple-element.85.pa, f32[1,1024]{1,0:T(1,128)S(1)} %collective-permute-done.27.pb, f32[1,1024]{1,0:T(1,128)S(1)} %get-tuple-element.80.u.refs_4_, f32[1,4096]{1,0:T(1,128)S(1)} %get-tuple-element.79.v_old.v.refs_8_, ...), custom_call_target="tpu_custom_call" | custom-call | tf_op jit(solution)/shard_map/pallas_call | solution.py:145
  176.9 5.1 %shard_map.63 = (f32[1,4096]{1,0:T(1,128)S(1)}, f32[1,1024]{1,0:T(1,128)S(1)}) custom-call(f32[1,4096]{1,0:T(1,128)S(1)} %add.117.pa, f32[1,4096]{1,0:T(1,128)S(1)} %collective-permute-done.30.pb, f32[1,1024]{1,0:T(1,128)S(1)} %get-tuple-element.76.u_old.u.refs_3_, f32[1,4096]{1,0:T(1,128)S(1)} %get-tuple-element.79.v_old.v.refs_8_, ...), custom_call_target="tpu_custom_call" | custom-call | tf_op jit(solution)/shard_map/pallas_call | solution.py:145
  184.6 5.2 %shard_map.64 = (f32[1,1024]{1,0:T(1,128)S(1)}, f32[1,4096]{1,0:T(1,128)S(1)}) custom-call(f32[1,1024]{1,0:T(1,128)S(1)} %get-tuple-element.87.pa, f32[1,1024]{1,0:T(1,128)S(1)} %collective-permute-done.31.pb, f32[1,1024]{1,0:T(1,128)S(1)} %get-tuple-element.76.u_old.u.refs_3_, f32[1,4096]{1,0:T(1,128)S(1)} %get-tuple-element.75.v_old.v.refs_7_, ...), custom_call_target="tpu_custom_call" | custom-call | tf_op jit(solution)/shard_map/pallas_call | solution.py:145
  199.0 5.1 %shard_map.65 = (f32[1,4096]{1,0:T(1,128)S(1)}, f32[1,1024]{1,0:T(1,128)S(1)}) custom-call(f32[1,4096]{1,0:T(1,128)S(1)} %add.119.pa, f32[1,4096]{1,0:T(1,128)S(1)} %collective-permute-done.34.pb, f32[1,1024]{1,0:T(1,128)S(1)} %get-tuple-element.72.u_old.u.refs_2_, f32[1,4096]{1,0:T(1,128)S(1)} %get-tuple-element.75.v_old.v.refs_7_, ...), custom_call_target="tpu_custom_call" | custom-call | tf_op jit(solution)/shard_map/pallas_call | solution.py:145
  206.6 5.2 %shard_map.66 = (f32[1,1024]{1,0:T(1,128)S(1)}, f32[1,4096]{1,0:T(1,128)S(1)}) custom-call(f32[1,1024]{1,0:T(1,128)S(1)} %get-tuple-element.89.pa, f32[1,1024]{1,0:T(1,128)S(1)} %collective-permute-done.35.pb, f32[1,1024]{1,0:T(1,128)S(1)} %get-tuple-element.72.u_old.u.refs_2_, f32[1,4096]{1,0:T(1,128)S(1)} %get-tuple-element.71.v_old.v.refs_6_, ...), custom_call_target="tpu_custom_call" | custom-call | tf_op jit(solution)/shard_map/pallas_call | solution.py:145
  220.8 5.1 %shard_map.67 = (f32[1,4096]{1,0:T(1,128)S(1)}, f32[1,1024]{1,0:T(1,128)S(1)}) custom-call(f32[1,4096]{1,0:T(1,128)S(1)} %add.121.pa, f32[1,4096]{1,0:T(1,128)S(1)} %collective-permute-done.38.pb, f32[1,1024]{1,0:T(1,128)S(1)} %get-tuple-element.68.u_old.u.refs_1_, f32[1,4096]{1,0:T(1,128)S(1)} %get-tuple-element.71.v_old.v.refs_6_, ...), custom_call_target="tpu_custom_call" | custom-call | tf_op jit(solution)/shard_map/pallas_call | solution.py:145
  228.4 5.2 %shard_map.68 = (f32[1,1024]{1,0:T(1,128)S(1)}, f32[1,4096]{1,0:T(1,128)S(1)}) custom-call(f32[1,1024]{1,0:T(1,128)S(1)} %get-tuple-element.91.pa, f32[1,1024]{1,0:T(1,128)S(1)} %collective-permute-done.39.pb, f32[1,1024]{1,0:T(1,128)S(1)} %get-tuple-element.68.u_old.u.refs_1_, f32[1,4096]{1,0:T(1,128)S(1)} %get-tuple-element.67.v_old.v.refs_5_, ...), custom_call_target="tpu_custom_call" | custom-call | tf_op jit(solution)/shard_map/pallas_call | solution.py:145
  242.6 5.1 %shard_map.69 = (f32[1,4096]{1,0:T(1,128)S(1)}, f32[1,1024]{1,0:T(1,128)S(1)}) custom-call(f32[1,4096]{1,0:T(1,128)S(1)} %add.123.pa, f32[1,4096]{1,0:T(1,128)S(1)} %collective-permute-done.42.pb, f32[1,1024]{1,0:T(1,128)S(1)} %get-tuple-element.64.u_old.u.refs_0_, f32[1,4096]{1,0:T(1,128)S(1)} %get-tuple-element.67.v_old.v.refs_5_, ...), custom_call_target="tpu_custom_call" | custom-call | tf_op jit(solution)/shard_map/pallas_call | solution.py:145
  250.2 8.2 %final.1 = (bf16[4,32,128]{2,1,0:T(8,128)(2,1)S(1)}, bf16[32,32,128]{2,1,0:T(8,128)(2,1)}, f32[1,256]{1,0:T(1,128)}) custom-call(s32[2]{0:T(128)S(1)} %pad_add_fusion.place, bf16[4096,128]{1,0:T(8,128)(2,1)S(1)} %get-tuple-element.56.both, bf16[1024,128]{1,0:T(8,128)(2,1)S(1)} %get-tuple-element.57.left_r, bf16[64,1024]{1,0:T(8,128)(2,1)S(1)} %get-tuple-element.58.right_r, ...), custom_call_target="tpu_custom_call" | custom-call | tf_op jit(solution)/shard_map/final/pallas_call | solution.py:524
  258.4 7.1 %all-to-all-start.1 = ((bf16[32,32,128]{2,1,0:T(8,128)(2,1)}), bf16[32,32,128]{2,1,0:T(8,128)(2,1)S(1)}, u32[]{:S(2)}, u32[]{:S(2)}) async-start(bf16[32,32,128]{2,1,0:T(8,128)(2,1)} %get-tuple-element.104), calls=%async_computation.1 | async-start | bytes 524288 | tf_op jit(solution)/shard_map/all_to_all | solution.py:557
  (123 shorter events, 116.2 us)
Async XLA Ops:
  21.8 10.6 %collective-permute-start = (bf16[16,128,128]{2,1,0:T(8,128)(2,1)S(1)}, bf16[16,128,128]{2,1,0:T(8,128)(2,1)S(1)}, u32[]{:S(2)}, u32[]{:S(2)}) collective-permute-start(bf16[16,128,128]{2,1,0:T(8,128)(2,1)S(1)} %all_to_all.10.mine), channel_id=1, source_target_pairs={{0,4},{1,5},{2,6},{3,7},{4,0},{5,1},{6,2},{7,3},{8,12},{9,13},{10,... | collective-permute-start | bytes 1572872 | tf_op jit(solution)/shard_map/ppermute | solution.py:23
  23.9 5.7 %collective-permute-start.1 = (bf16[144,128]{1,0:T(8,128)(2,1)S(1)}, bf16[144,128]{1,0:T(8,128)(2,1)S(1)}, u32[]{:S(2)}, u32[]{:S(2)}) collective-permute-start(bf16[144,128]{1,0:T(8,128)(2,1)S(1)} %get-tuple-element.55.own), channel_id=1, source_target_pairs={{0,16},{1,17},{2,18},{3,19},{4,20},{5,21},{6,22},{7,23},{8,24},{9,... | collective-permute-start | bytes 110600 | tf_op jit(solution)/shard_map/ppermute | solution.py:23
  24.4 5.2 %collective-permute-start.2 = (bf16[144,128]{1,0:T(8,128)(2,1)S(1)}, bf16[144,128]{1,0:T(8,128)(2,1)S(1)}, u32[]{:S(2)}, u32[]{:S(2)}) collective-permute-start(bf16[144,128]{1,0:T(8,128)(2,1)S(1)} %get-tuple-element.55.own), channel_id=1, source_target_pairs={{0,64},{1,65},{2,66},{3,67},{4,68},{5,69},{6,70},{7,71},{8,72},{9,... | collective-permute-start | bytes 110600 | tf_op jit(solution)/shard_map/ppermute | solution.py:23
  25.7 6.7 %collective-permute-start.3 = (bf16[144,128]{1,0:T(8,128)(2,1)S(1)}, bf16[144,128]{1,0:T(8,128)(2,1)S(1)}, u32[]{:S(2)}, u32[]{:S(2)}) collective-permute-start(bf16[144,128]{1,0:T(8,128)(2,1)S(1)} %get-tuple-element.55.own), channel_id=1, source_target_pairs={{0,80},{1,81},{2,82},{3,83},{4,84},{5,85},{6,86},{7,87},{8,88},{9,... | collective-permute-start | bytes 110600 | tf_op jit(solution)/shard_map/ppermute | solution.py:23
  47.3 3.8 %collective-permute-start.5 = (f32[1,4096]{1,0:T(1,128)S(1)}, f32[1,4096]{1,0:T(1,128)S(1)}, u32[]{:S(2)}, u32[]{:S(2)}) collective-permute-start(f32[1,4096]{1,0:T(1,128)S(1)} %get-tuple-element.65), channel_id=1, source_target_pairs={{0,4},{1,5},{2,6},{3,7},{4,0},{5,1},{6,2},{7,3},{8,12},{9,13},{10,... | collective-permute-start | bytes 49160 | tf_op jit(solution)/shard_map/ppermute | solution.py:23
  51.2 3.2 %collective-permute-start.6 = (f32[1,4096]{1,0:T(1,128)S(1)}, f32[1,4096]{1,0:T(1,128)S(1)}, u32[]{:S(2)}, u32[]{:S(2)}) collective-permute-start(f32[1,4096]{1,0:T(1,128)S(1)} %log_add_fusion.9), channel_id=1, source_target_pairs={{0,12},{1,13},{2,14},{3,15},{4,8},{5,9},{6,10},{7,11},{8,4},{9,5},... | collective-permute-start | bytes 49160 | tf_op jit(solution)/shard_map/ppermute | solution.py:23
  54.5 3.2 %collective-permute-start.7 = (f32[1,4096]{1,0:T(1,128)S(1)}, f32[1,4096]{1,0:T(1,128)S(1)}, u32[]{:S(2)}, u32[]{:S(2)}) collective-permute-start(f32[1,4096]{1,0:T(1,128)S(1)} %log_add_fusion.8.pa), channel_id=1, source_target_pairs={{0,36},{1,37},{2,38},{3,39},{4,32},{5,33},{6,34},{7,35},{8,44},{9,... | collective-permute-start | bytes 49160 | tf_op jit(solution)/shard_map/ppermute | solution.py:23
  61.8 2.5 collective-permute-start.8
  71.3 3.2 %collective-permute-start.10 = (f32[1,4096]{1,0:T(1,128)S(1)}, f32[1,4096]{1,0:T(1,128)S(1)}, u32[]{:S(2)}, u32[]{:S(2)}) collective-permute-start(f32[1,4096]{1,0:T(1,128)S(1)} %log_add_fusion.7), channel_id=1, source_target_pairs={{0,12},{1,13},{2,14},{3,15},{4,8},{5,9},{6,10},{7,11},{8,4},{9,5},... | collective-permute-start | bytes 49160 | tf_op jit(solution)/shard_map/ppermute | solution.py:23
  74.6 3.2 %collective-permute-start.11 = (f32[1,4096]{1,0:T(1,128)S(1)}, f32[1,4096]{1,0:T(1,128)S(1)}, u32[]{:S(2)}, u32[]{:S(2)}) collective-permute-start(f32[1,4096]{1,0:T(1,128)S(1)} %log_add_fusion.6.pa), channel_id=1, source_target_pairs={{0,36},{1,37},{2,38},{3,39},{4,32},{5,33},{6,34},{7,35},{8,44},{9,... | collective-permute-start | bytes 49160 | tf_op jit(solution)/shard_map/ppermute | solution.py:23
  91.4 3.2 %collective-permute-start.14 = (f32[1,4096]{1,0:T(1,128)S(1)}, f32[1,4096]{1,0:T(1,128)S(1)}, u32[]{:S(2)}, u32[]{:S(2)}) collective-permute-start(f32[1,4096]{1,0:T(1,128)S(1)} %log_add_fusion.5), channel_id=1, source_target_pairs={{0,12},{1,13},{2,14},{3,15},{4,8},{5,9},{6,10},{7,11},{8,4},{9,5},... | collective-permute-start | bytes 49160 | tf_op jit(solution)/shard_map/ppermute | solution.py:23
  94.7 3.2 %collective-permute-start.15 = (f32[1,4096]{1,0:T(1,128)S(1)}, f32[1,4096]{1,0:T(1,128)S(1)}, u32[]{:S(2)}, u32[]{:S(2)}) collective-permute-start(f32[1,4096]{1,0:T(1,128)S(1)} %log_add_fusion.4.pa), channel_id=1, source_target_pairs={{0,36},{1,37},{2,38},{3,39},{4,32},{5,33},{6,34},{7,35},{8,44},{9,... | collective-permute-start | bytes 49160 | tf_op jit(solution)/shard_map/ppermute | solution.py:23
  109.0 2.6 collective-permute-start.17
  111.7 3.2 %collective-permute-start.18 = (f32[1,4096]{1,0:T(1,128)S(1)}, f32[1,4096]{1,0:T(1,128)S(1)}, u32[]{:S(2)}, u32[]{:S(2)}) collective-permute-start(f32[1,4096]{1,0:T(1,128)S(1)} %log_add_fusion.3), channel_id=1, source_target_pairs={{0,12},{1,13},{2,14},{3,15},{4,8},{5,9},{6,10},{7,11},{8,4},{9,5},... | collective-permute-start | bytes 49160 | tf_op jit(solution)/shard_map/ppermute | solution.py:23
  115.0 3.2 %collective-permute-start.19 = (f32[1,4096]{1,0:T(1,128)S(1)}, f32[1,4096]{1,0:T(1,128)S(1)}, u32[]{:S(2)}, u32[]{:S(2)}) collective-permute-start(f32[1,4096]{1,0:T(1,128)S(1)} %log_add_fusion.2.pa), channel_id=1, source_target_pairs={{0,36},{1,37},{2,38},{3,39},{4,32},{5,33},{6,34},{7,35},{8,44},{9,... | collective-permute-start | bytes 49160 | tf_op jit(solution)/shard_map/ppermute | solution.py:23
  122.4 2.5 collective-permute-start.20
  131.8 3.2 %collective-permute-start.22 = (f32[1,4096]{1,0:T(1,128)S(1)}, f32[1,4096]{1,0:T(1,128)S(1)}, u32[]{:S(2)}, u32[]{:S(2)}) collective-permute-start(f32[1,4096]{1,0:T(1,128)S(1)} %log_add_fusion.1), channel_id=1, source_target_pairs={{0,12},{1,13},{2,14},{3,15},{4,8},{5,9},{6,10},{7,11},{8,4},{9,5},... | collective-permute-start | bytes 49160 | tf_op jit(solution)/shard_map/ppermute | solution.py:23
  135.1 3.2 %collective-permute-start.23 = (f32[1,4096]{1,0:T(1,128)S(1)}, f32[1,4096]{1,0:T(1,128)S(1)}, u32[]{:S(2)}, u32[]{:S(2)}) collective-permute-start(f32[1,4096]{1,0:T(1,128)S(1)} %log_add_fusion.pa), channel_id=1, source_target_pairs={{0,36},{1,37},{2,38},{3,39},{4,32},{5,33},{6,34},{7,35},{8,44},{9,... | collective-permute-start | bytes 49160 | tf_op jit(solution)/shard_map/ppermute | solution.py:23
  146.5 3.2 %collective-permute-start.25 = (f32[1,4096]{1,0:T(1,128)S(1)}, f32[1,4096]{1,0:T(1,128)S(1)}, u32[]{:S(2)}, u32[]{:S(2)}) collective-permute-start(f32[1,4096]{1,0:T(1,128)S(1)} %add.114), channel_id=1, source_target_pairs={{0,12},{1,13},{2,14},{3,15},{4,8},{5,9},{6,10},{7,11},{8,4},{9,5},... | collective-permute-start | bytes 49160 | tf_op jit(solution)/shard_map/ppermute | solution.py:23
  149.7 3.2 %collective-permute-start.26 = (f32[1,4096]{1,0:T(1,128)S(1)}, f32[1,4096]{1,0:T(1,128)S(1)}, u32[]{:S(2)}, u32[]{:S(2)}) collective-permute-start(f32[1,4096]{1,0:T(1,128)S(1)} %add.115.pa), channel_id=1, source_target_pairs={{0,36},{1,37},{2,38},{3,39},{4,32},{5,33},{6,34},{7,35},{8,44},{9,... | collective-permute-start | bytes 49160 | tf_op jit(solution)/shard_map/ppermute | solution.py:23
  170.4 3.2 %collective-permute-start.29 = (f32[1,4096]{1,0:T(1,128)S(1)}, f32[1,4096]{1,0:T(1,128)S(1)}, u32[]{:S(2)}, u32[]{:S(2)}) collective-permute-start(f32[1,4096]{1,0:T(1,128)S(1)} %add.116), channel_id=1, source_target_pairs={{0,12},{1,13},{2,14},{3,15},{4,8},{5,9},{6,10},{7,11},{8,4},{9,5},... | collective-permute-start | bytes 49160 | tf_op jit(solution)/shard_map/ppermute | solution.py:23
  173.7 3.2 %collective-permute-start.30 = (f32[1,4096]{1,0:T(1,128)S(1)}, f32[1,4096]{1,0:T(1,128)S(1)}, u32[]{:S(2)}, u32[]{:S(2)}) collective-permute-start(f32[1,4096]{1,0:T(1,128)S(1)} %add.117.pa), channel_id=1, source_target_pairs={{0,36},{1,37},{2,38},{3,39},{4,32},{5,33},{6,34},{7,35},{8,44},{9,... | collective-permute-start | bytes 49160 | tf_op jit(solution)/shard_map/ppermute | solution.py:23
  192.2 3.2 %collective-permute-start.33 = (f32[1,4096]{1,0:T(1,128)S(1)}, f32[1,4096]{1,0:T(1,128)S(1)}, u32[]{:S(2)}, u32[]{:S(2)}) collective-permute-start(f32[1,4096]{1,0:T(1,128)S(1)} %add.118), channel_id=1, source_target_pairs={{0,12},{1,13},{2,14},{3,15},{4,8},{5,9},{6,10},{7,11},{8,4},{9,5},... | collective-permute-start | bytes 49160 | tf_op jit(solution)/shard_map/ppermute | solution.py:23
  195.5 3.5 %collective-permute-start.34 = (f32[1,4096]{1,0:T(1,128)S(1)}, f32[1,4096]{1,0:T(1,128)S(1)}, u32[]{:S(2)}, u32[]{:S(2)}) collective-permute-start(f32[1,4096]{1,0:T(1,128)S(1)} %add.119.pa), channel_id=1, source_target_pairs={{0,36},{1,37},{2,38},{3,39},{4,32},{5,33},{6,34},{7,35},{8,44},{9,... | collective-permute-start | bytes 49160 | tf_op jit(solution)/shard_map/ppermute | solution.py:23
  214.3 3.2 %collective-permute-start.37 = (f32[1,4096]{1,0:T(1,128)S(1)}, f32[1,4096]{1,0:T(1,128)S(1)}, u32[]{:S(2)}, u32[]{:S(2)}) collective-permute-start(f32[1,4096]{1,0:T(1,128)S(1)} %add.120), channel_id=1, source_target_pairs={{0,12},{1,13},{2,14},{3,15},{4,8},{5,9},{6,10},{7,11},{8,4},{9,5},... | collective-permute-start | bytes 49160 | tf_op jit(solution)/shard_map/ppermute | solution.py:23
  217.5 3.2 %collective-permute-start.38 = (f32[1,4096]{1,0:T(1,128)S(1)}, f32[1,4096]{1,0:T(1,128)S(1)}, u32[]{:S(2)}, u32[]{:S(2)}) collective-permute-start(f32[1,4096]{1,0:T(1,128)S(1)} %add.121.pa), channel_id=1, source_target_pairs={{0,36},{1,37},{2,38},{3,39},{4,32},{5,33},{6,34},{7,35},{8,44},{9,... | collective-permute-start | bytes 49160 | tf_op jit(solution)/shard_map/ppermute | solution.py:23
  236.1 3.2 %collective-permute-start.41 = (f32[1,4096]{1,0:T(1,128)S(1)}, f32[1,4096]{1,0:T(1,128)S(1)}, u32[]{:S(2)}, u32[]{:S(2)}) collective-permute-start(f32[1,4096]{1,0:T(1,128)S(1)} %add.122), channel_id=1, source_target_pairs={{0,12},{1,13},{2,14},{3,15},{4,8},{5,9},{6,10},{7,11},{8,4},{9,5},... | collective-permute-start | bytes 49160 | tf_op jit(solution)/shard_map/ppermute | solution.py:23
  239.3 3.2 %collective-permute-start.42 = (f32[1,4096]{1,0:T(1,128)S(1)}, f32[1,4096]{1,0:T(1,128)S(1)}, u32[]{:S(2)}, u32[]{:S(2)}) collective-permute-start(f32[1,4096]{1,0:T(1,128)S(1)} %add.123.pa), channel_id=1, source_target_pairs={{0,36},{1,37},{2,38},{3,39},{4,32},{5,33},{6,34},{7,35},{8,44},{9,... | collective-permute-start | bytes 49160 | tf_op jit(solution)/shard_map/ppermute | solution.py:23
  258.4 15.9 %all-to-all-start.1 = ((bf16[32,32,128]{2,1,0:T(8,128)(2,1)}), bf16[32,32,128]{2,1,0:T(8,128)(2,1)S(1)}, u32[]{:S(2)}, u32[]{:S(2)}) async-start(bf16[32,32,128]{2,1,0:T(8,128)(2,1)} %get-tuple-element.104), calls=%async_computation.1 | async-start | bytes 524288 | tf_op jit(solution)/shard_map/all_to_all | solution.py:557
  265.5 3.9 %collective-permute-start.44 = (bf16[32,128]{1,0:T(8,128)(2,1)S(1)}, bf16[32,128]{1,0:T(8,128)(2,1)S(1)}, u32[]{:S(2)}, u32[]{:S(2)}) collective-permute-start(bf16[32,128]{1,0:T(8,128)(2,1)S(1)} %get-tuple-element.108), channel_id=1, source_target_pairs={{0,1},{1,0},{2,3},{3,2},{4,5},{5,4},{6,7},{7,6},{8,9},{9,8},{10,11... | collective-permute-start | bytes 24584 | tf_op jit(solution)/shard_map/ppermute | solution.py:23
  266.8 4.3 %collective-permute-start.45 = (bf16[32,128]{1,0:T(8,128)(2,1)S(1)}, bf16[32,128]{1,0:T(8,128)(2,1)S(1)}, u32[]{:S(2)}, u32[]{:S(2)}) collective-permute-start(bf16[32,128]{1,0:T(8,128)(2,1)S(1)} %get-tuple-element.107), channel_id=1, source_target_pairs={{0,2},{1,3},{2,0},{3,1},{4,6},{5,7},{6,4},{7,5},{8,10},{9,11},{10,... | collective-permute-start | bytes 24584 | tf_op jit(solution)/shard_map/ppermute | solution.py:23
  269.3 4.0 %collective-permute-start.46 = (bf16[32,128]{1,0:T(8,128)(2,1)S(1)}, bf16[32,128]{1,0:T(8,128)(2,1)S(1)}, u32[]{:S(2)}, u32[]{:S(2)}) collective-permute-start(bf16[32,128]{1,0:T(8,128)(2,1)S(1)} %get-tuple-element.106), channel_id=1, source_target_pairs={{0,3},{1,2},{2,1},{3,0},{4,7},{5,6},{6,5},{7,4},{8,11},{9,10},{10,... | collective-permute-start | bytes 24584 | tf_op jit(solution)/shard_map/ppermute | solution.py:23
  (21 other events, 42.5 us)

commit v2 on v1

--- a/solution.py
+++ b/solution.py
@@ -14,6 +14,8 @@
 X0, CORE, Y0, Y1, Z0, Z1 = 1, 4, 8, 16, 32, 64
 LW_TOP = 145.0
 TINY = 1e-37
+BLOCK = 256
+SPAN = 1024
 SMALL = pltpu.CompilerParams(vmem_limit_bytes=24 * 2**20)
 F32 = jnp.float32
 BF16 = jnp.bfloat16
@@ -64,81 +66,78 @@
     return out.astype(BF16)
 
 
-def shape_of(rows, cols):
-    return (256, cols) if rows > cols else (rows // 2, 512)
-
-
-def room(rows, cols, mode="exp"):
-    b, s = shape_of(rows, cols)
-    shapes = [(b, s)] * 2
-    if mode in ("weight", "pair_weight"):
-        shapes += [(b, 128)] * 2
-    if mode in ("pair", "pair_weight"):
-        shapes += [(b, s)] * 2
-    return [pltpu.VMEM((16, rows), BF16), pltpu.VMEM((16, cols), BF16)] + [
-        pltpu.VMEM(shape, F32) for shape in shapes
-    ]
+def room(rows, cols, weighted=False):
+    shapes = [((16, rows), BF16), ((16, cols), BF16)] + [((rows, 128), F32)] * weighted
+    return [pltpu.VMEM(shape, kind) for shape, kind in shapes]
 
 
 def tile_pass(mode, left, right, rows, cols, scratch, emit, pair=None):
-    left_x, right_x, scratch = scratch[0], scratch[1], scratch[2:]
-    height, span = shape_of(rows, cols)
-    slots, scratch = scratch[:2], scratch[2:]
+    left_x, right_x = scratch[:2]
+    height = BLOCK if pair is None else BLOCK // 2
+    deep = 2 if mode == "weight" else 4
     weighted = mode in ("weight", "pair_weight")
     if weighted:
-        weights, scratch = scratch[:2], scratch[2:]
-        at = lax.broadcasted_iota(jnp.int32, (128, 128), 0)
-        pick = jnp.where((at >= 70) & (at < 73), 1.0, 0.0).astype(BF16)
-    pairs = scratch
+        weight = scratch[2]
+        at = lax.broadcasted_iota(jnp.int32, (16, 128), 0)
+        pick = jnp.where((at >= 6) & (at < 9), 1.0, 0.0).astype(BF16)
+        for m in range(0, rows, 512):
+            weight[m : m + 512, :] = mm(left_x[:, m : m + 512].T, pick)
     low = jnp.zeros((64, height), BF16)
     high = jnp.zeros((48, height), BF16)
-    tail = jnp.zeros((48, span), BF16)
-    n_m, n_n = rows // height, cols // span
-
-    def fill(i, slot):
-        m = pl.ds(pl.multiple_of((i % n_m) * height, height), height)
-        n = pl.ds(pl.multiple_of((i // n_m) * span, span), span)
-        a = left[m, :] + jnp.concatenate([low, left_x[:, m], high], axis=0).T
-        slots[slot][...] = mm(a, jnp.concatenate([right[:, n], right_x[:, n], tail], axis=0))
+
+    def block(m0, right_block, pair_block, acc):
+        x = jnp.concatenate([low, left_x[:, pl.ds(m0, height)], high], axis=0)
+        a = left[pl.ds(m0, height), :] + x.T
+        t = mm(a, right_block)
+        e = jnp.exp(t)
         if weighted:
-            weights[slot][...] = mm(a, pick)
+            w = weight[pl.ds(m0, height), :]
         if pair is not None:
-            pairs[slot][...] = mm(pair[0][m, :], pair[1][:, n])
-
-    def use(slot, acc):
+            pr = mm(pair[0][pl.ds(m0, height), :], pair_block)
         out = []
-        for q in range(span // 128):
-            lanes = slice(q * 128, (q + 1) * 128)
-            y = jnp.exp(slots[slot][:, lanes])
+        for q in range(SPAN // 128):
+            y = e[:, q * 128 : (q + 1) * 128]
             if mode == "weight":
-                y = y * weights[slot][...]
+                y = y * w
             elif mode == "pair":
-                y = y * pairs[slot][:, lanes]
+                y = y * pr[:, q * 128 : (q + 1) * 128]
             elif mode == "pair_weight":
-                y = y * (pairs[slot][:, lanes] - weights[slot][...])
-            out.append(acc[q] + jnp.sum(y.reshape(height // 8, 8, 128), axis=0))
+                y = y * (pr[:, q * 128 : (q + 1) * 128] - w)
+            y = y.reshape(height // 8, 8, 128)
+            out.append(acc[q] + jnp.sum(y, axis=0))
         return tuple(out)
+
+    def right_of(n0):
+        sl = pl.ds(n0, SPAN)
+        full = jnp.concatenate([right[:, sl], right_x[:, sl], jnp.zeros((48, SPAN), BF16)], axis=0)
+        return full, None if pair is None else pair[1][:, sl]
 
     def fold(acc):
         return jnp.concatenate([jnp.sum(a, axis=0, keepdims=True) for a in acc], axis=1)
 
-    zero = (jnp.zeros((8, 128), F32),) * (span // 128)
-    last = n_m * n_n - 1
-    fill(0, 0)
-
-    def step(i, acc):
-        fill(2 * i + 1, 1)
-        acc = use(0, acc)
-        fill(jnp.minimum(2 * i + 2, last), 0)
-        acc = use(1, acc)
-        if n_n > 1:
-            emit(pl.ds(pl.multiple_of(i * span, span), span), fold(acc))
-            return zero
-        return acc
-
-    acc = lax.fori_loop(0, (last + 1) // 2, step, zero)
-    if n_n == 1:
-        emit(slice(None), fold(acc))
+    zero = (jnp.zeros((8, 128), F32),) * (SPAN // 128)
+    if rows > cols:
+        right_block, pair_block = right_of(0)
+
+        def step(i, acc):
+            for b in range(deep):
+                m0 = pl.multiple_of((deep * i + b) * height, height)
+                acc = block(m0, right_block, pair_block, acc)
+            return acc
+
+        emit(slice(None), fold(lax.fori_loop(0, rows // (deep * height), step, zero)))
+    else:
+
+        def step(i, carry):
+            n0 = pl.multiple_of(i * SPAN, SPAN)
+            right_block, pair_block = right_of(n0)
+            acc = zero
+            for m0 in range(0, rows, height):
+                acc = block(m0, right_block, pair_block, acc)
+            emit(pl.ds(n0, SPAN), fold(acc))
+            return carry
+
+        lax.fori_loop(0, cols // SPAN, step, 0)
 
 
 def call(kernel, out_shapes, scratch, *args):
@@ -491,7 +490,7 @@
     v, part = call(
         functools.partial(first_dv, 0.5 / scale),
         (v_like, v_like),
-        room(n_r, n_c, "pair"),
+        room(n_r, n_c),
         *(pa, pb, us[-1], lw, left_r, right_c, cot_t, sq_r, sq_c),
     )
     vs.append(v)
@@ -499,7 +498,7 @@
     dv, part = call(
         first_du,
         (v_like, u_like),
-        [pltpu.VMEM((128, n_r), BF16)] + room(n_c, n_r, "pair_weight"),
+        [pltpu.VMEM((128, n_r), BF16)] + room(n_c, n_r, True),
         *(pa, pb, us[-1], vs[-1], lw, left_c, right_r, both, sq_c, sq_r),
     )
     dus, dvs = [None] * ITERS, [None] * ITERS
@@ -509,14 +508,14 @@
         dus[k + 1], part = call(
             functools.partial(next_dv, log_count),
             (u_like, v_like),
-            room(n_r, n_c, "weight"),
+            room(n_r, n_c, True),
             *(pa, pb, us[k + 1], vs[k + 1], left_r, right_c, sq_r, sq_c),
         )
         pa, pb = over_rows(part, plus)
         dvs[k], part = call(
             next_du,
             (v_like, u_like),
-            room(n_c, n_r, "weight"),
+            room(n_c, n_r, True),
             *(pa, pb, us[k], vs[k + 1], lw, left_c, right_r, sq_c, sq_r),
         )
     pa, pb = over_cols(part)

time: 276 us -> 253 us (0.917)
  Pallas kernels: 109 us -> 86.7 us
    pallas_call x20, Pallas kernels: 97.8 us -> 75.4 us  [call(): pl.pallas_call(kernel, out_shape=tuple((jax.ShapeDtypeStruct(s, d) for s,...]
where the time goes in v2:
time: 253 us
  Pallas kernels  86.7 us (34%)
  waiting for transfers between devices  82.6 us (33%)
  starting transfers between devices  58.7 us (23%)
  blocking collectives  18.8 us (7%)
  local copies, waits for them, and re-layouts  4.06 us (2%)
    ppermute x47, waiting for transfers between devices, swap(): return lax.ppermute(value, AXES, [(i, i ^ bits) for i in range(128)])  81.5 us
    pallas_call x20, Pallas kernels, call(): pl.pallas_call(kernel, out_shape=tuple((jax.ShapeDtypeStruct(s, d) for s,...  75.4 us
    ppermute x47, starting transfers between devices, swap(): return lax.ppermute(value, AXES, [(i, i ^ bits) for i in range(128)])  51.6 us
    all_to_all x1, blocking collectives, local(): mine = lax.all_to_all(payload, ('z', 'y'), 0, 0, tiled=True)  18.8 us
    pallas_call x1, Pallas kernels, local(): pl.pallas_call(functools.partial(final_kernel, scale, log_count), name='f...  8.19 us
    all_to_all x1, starting transfers between devices, local(): col_parts = lax.all_to_all(col_out, ('z', 'y', 'c'), 0, 0, tiled=True)  7.07 us
  transfers between devices with their start and end apart: 48, of which 44 were waited for; matrix products, arithmetic and copies ran while one was open for 0% of the time, Pallas kernels for 0%

profile of v2, /device:TPU:1, one launch (start us, length us, event | category | flops | bytes accessed | tf_op | source)
XLA Modules:
  0.0 252.8 jit_solution(17943253361863688481)
XLA Ops:
  3.0 18.8 %all_to_all.10.mine = bf16[16,128,128]{2,1,0:T(8,128)(2,1)S(1)} all-to-all(bf16[16,128,128]{2,1,0:T(8,128)(2,1)S(1)} %get-tuple-element.54), channel_id=1, replica_groups=mesh['z'=4,'y'=4,'c'=2,'x'=4] {'z','y'}, dimensions={0} | all-to-all | bytes 1048576 | tf_op jit(solution)/shard_map/all_to_all | solution.py:442
  25.7 3.9 %collective-permute-start.3 = (bf16[144,128]{1,0:T(8,128)(2,1)S(1)}, bf16[144,128]{1,0:T(8,128)(2,1)S(1)}, u32[]{:S(2)}, u32[]{:S(2)}) collective-permute-start(bf16[144,128]{1,0:T(8,128)(2,1)S(1)} %get-tuple-element.55.own), channel_id=1, source_target_pairs={{0,80},{1,81},{2,82},{3,83},{4,84},{5,85},{6,86},{7,87},{8,88},{9,... | collective-permute-start | bytes 110600 | tf_op jit(solution)/shard_map/ppermute | solution.py:25
  36.3 3.1 %shard_map.50.pa = f32[1,1024]{1,0:T(1,128)S(1)} custom-call(bf16[4096,128]{1,0:T(8,128)(2,1)S(1)} %get-tuple-element.62.left_c, bf16[64,1024]{1,0:T(8,128)(2,1)S(1)} %get-tuple-element.58.right_r, f32[1,4096]{1,0:T(1,128)S(1)} %get-tuple-element.61.sq_c, f32[1,1024]{1,0:T(1,128)S(1)} %get-tuple-element.60.sq_r.u_old), custom_call_target="tpu_custom_call" | custom-call | tf_op jit(solution)/shard_map/pallas_call | solution.py:144
  42.0 3.2 %shard_map.51 = (f32[1,1024]{1,0:T(1,128)S(1)}, f32[1,4096]{1,0:T(1,128)S(1)}) custom-call(f32[1,1024]{1,0:T(1,128)S(1)} %shard_map.50.pa, f32[1,1024]{1,0:T(1,128)S(1)} %collective-permute-done.4.pb, f32[1,1024]{1,0:T(1,128)S(1)} %get-tuple-element.60.sq_r.u_old, f32[1,4096]{1,0:T(1,128)S(1)} %broadcast_in_dim.3.v_old, f32[1,1024]{1,0:T(1,128)S(1)} %get-tuple-element.59.lw, ...), custom_call_target="tpu_custom_call" | custom-call | tf_op jit(solution)/shard_map/pallas_call | solution.py:144
  45.2 3.0 %collective-permute-start.5 = (f32[1,4096]{1,0:T(1,128)S(1)}, f32[1,4096]{1,0:T(1,128)S(1)}, u32[]{:S(2)}, u32[]{:S(2)}) collective-permute-start(f32[1,4096]{1,0:T(1,128)S(1)} %get-tuple-element.65), channel_id=1, source_target_pairs={{0,4},{1,5},{2,6},{3,7},{4,0},{5,1},{6,2},{7,3},{8,12},{9,13},{10,... | collective-permute-start | bytes 49160 | tf_op jit(solution)/shard_map/ppermute | solution.py:25
  52.9 2.8 %collective-permute-done.7.pb = f32[1,4096]{1,0:T(1,128)S(1)} collective-permute-done((f32[1,4096]{1,0:T(1,128)S(1)}, f32[1,4096]{1,0:T(1,128)S(1)}, u32[]{:S(2)}, u32[]{:S(2)}) %collective-permute-start.7) | collective-permute-done | bytes 16416 | tf_op jit(solution)/shard_map/ppermute | solution.py:25
  55.7 3.2 %shard_map.52 = (f32[1,4096]{1,0:T(1,128)S(1)}, f32[1,1024]{1,0:T(1,128)S(1)}) custom-call(f32[1,4096]{1,0:T(1,128)S(1)} %log_add_fusion.8.pa, f32[1,4096]{1,0:T(1,128)S(1)} %collective-permute-done.7.pb, f32[1,4096]{1,0:T(1,128)S(1)} %broadcast_in_dim.3.v_old, f32[1,1024]{1,0:T(1,128)S(1)} %get-tuple-element.64.u_old.u.refs_0_, ...), custom_call_target="tpu_custom_call" | custom-call | tf_op jit(solution)/shard_map/pallas_call | solution.py:144
  61.4 3.3 %shard_map.53 = (f32[1,1024]{1,0:T(1,128)S(1)}, f32[1,4096]{1,0:T(1,128)S(1)}) custom-call(f32[1,1024]{1,0:T(1,128)S(1)} %get-tuple-element.66.pa, f32[1,1024]{1,0:T(1,128)S(1)} %collective-permute-done.8.pb, f32[1,1024]{1,0:T(1,128)S(1)} %get-tuple-element.64.u_old.u.refs_0_, f32[1,4096]{1,0:T(1,128)S(1)} %get-tuple-element.67.v_old.v.refs_5_, ...), custom_call_target="tpu_custom_call" | custom-call | tf_op jit(solution)/shard_map/pallas_call | solution.py:144
  71.0 2.8 %collective-permute-done.11.pb = f32[1,4096]{1,0:T(1,128)S(1)} collective-permute-done((f32[1,4096]{1,0:T(1,128)S(1)}, f32[1,4096]{1,0:T(1,128)S(1)}, u32[]{:S(2)}, u32[]{:S(2)}) %collective-permute-start.11) | collective-permute-done | bytes 16416 | tf_op jit(solution)/shard_map/ppermute | solution.py:25
  73.7 3.2 %shard_map.54 = (f32[1,4096]{1,0:T(1,128)S(1)}, f32[1,1024]{1,0:T(1,128)S(1)}) custom-call(f32[1,4096]{1,0:T(1,128)S(1)} %log_add_fusion.6.pa, f32[1,4096]{1,0:T(1,128)S(1)} %collective-permute-done.11.pb, f32[1,4096]{1,0:T(1,128)S(1)} %get-tuple-element.67.v_old.v.refs_5_, f32[1,1024]{1,0:T(1,128)S(1)} %get-tuple-element.68.u_old.u.refs_1_, ...), custom_call_target="tpu_custom_call" | custom-call | tf_op jit(solution)/shard_map/pallas_call | solution.py:144
  79.5 3.3 %shard_map.55 = (f32[1,1024]{1,0:T(1,128)S(1)}, f32[1,4096]{1,0:T(1,128)S(1)}) custom-call(f32[1,1024]{1,0:T(1,128)S(1)} %get-tuple-element.70.pa, f32[1,1024]{1,0:T(1,128)S(1)} %collective-permute-done.12.pb, f32[1,1024]{1,0:T(1,128)S(1)} %get-tuple-element.68.u_old.u.refs_1_, f32[1,4096]{1,0:T(1,128)S(1)} %get-tuple-element.71.v_old.v.refs_6_, ...), custom_call_target="tpu_custom_call" | custom-call | tf_op jit(solution)/shard_map/pallas_call | solution.py:144
  89.1 2.8 %collective-permute-done.15.pb = f32[1,4096]{1,0:T(1,128)S(1)} collective-permute-done((f32[1,4096]{1,0:T(1,128)S(1)}, f32[1,4096]{1,0:T(1,128)S(1)}, u32[]{:S(2)}, u32[]{:S(2)}) %collective-permute-start.15) | collective-permute-done | bytes 16416 | tf_op jit(solution)/shard_map/ppermute | solution.py:25
  91.8 3.2 %shard_map.56 = (f32[1,4096]{1,0:T(1,128)S(1)}, f32[1,1024]{1,0:T(1,128)S(1)}) custom-call(f32[1,4096]{1,0:T(1,128)S(1)} %log_add_fusion.4.pa, f32[1,4096]{1,0:T(1,128)S(1)} %collective-permute-done.15.pb, f32[1,4096]{1,0:T(1,128)S(1)} %get-tuple-element.71.v_old.v.refs_6_, f32[1,1024]{1,0:T(1,128)S(1)} %get-tuple-element.72.u_old.u.refs_2_, ...), custom_call_target="tpu_custom_call" | custom-call | tf_op jit(solution)/shard_map/pallas_call | solution.py:144
  97.7 3.3 %shard_map.57 = (f32[1,1024]{1,0:T(1,128)S(1)}, f32[1,4096]{1,0:T(1,128)S(1)}) custom-call(f32[1,1024]{1,0:T(1,128)S(1)} %get-tuple-element.74.pa, f32[1,1024]{1,0:T(1,128)S(1)} %collective-permute-done.16.pb, f32[1,1024]{1,0:T(1,128)S(1)} %get-tuple-element.72.u_old.u.refs_2_, f32[1,4096]{1,0:T(1,128)S(1)} %get-tuple-element.75.v_old.v.refs_7_, ...), custom_call_target="tpu_custom_call" | custom-call | tf_op jit(solution)/shard_map/pallas_call | solution.py:144
  107.3 2.8 %collective-permute-done.19.pb = f32[1,4096]{1,0:T(1,128)S(1)} collective-permute-done((f32[1,4096]{1,0:T(1,128)S(1)}, f32[1,4096]{1,0:T(1,128)S(1)}, u32[]{:S(2)}, u32[]{:S(2)}) %collective-permute-start.19) | collective-permute-done | bytes 16416 | tf_op jit(solution)/shard_map/ppermute | solution.py:25
  110.1 3.2 %shard_map.58 = (f32[1,4096]{1,0:T(1,128)S(1)}, f32[1,1024]{1,0:T(1,128)S(1)}) custom-call(f32[1,4096]{1,0:T(1,128)S(1)} %log_add_fusion.2.pa, f32[1,4096]{1,0:T(1,128)S(1)} %collective-permute-done.19.pb, f32[1,4096]{1,0:T(1,128)S(1)} %get-tuple-element.75.v_old.v.refs_7_, f32[1,1024]{1,0:T(1,128)S(1)} %get-tuple-element.76.u_old.u.refs_3_, ...), custom_call_target="tpu_custom_call" | custom-call | tf_op jit(solution)/shard_map/pallas_call | solution.py:144
  115.8 3.3 %shard_map.59 = (f32[1,1024]{1,0:T(1,128)S(1)}, f32[1,4096]{1,0:T(1,128)S(1)}) custom-call(f32[1,1024]{1,0:T(1,128)S(1)} %get-tuple-element.78.pa, f32[1,1024]{1,0:T(1,128)S(1)} %collective-permute-done.20.pb, f32[1,1024]{1,0:T(1,128)S(1)} %get-tuple-element.76.u_old.u.refs_3_, f32[1,4096]{1,0:T(1,128)S(1)} %get-tuple-element.79.v_old.v.refs_8_, ...), custom_call_target="tpu_custom_call" | custom-call | tf_op jit(solution)/shard_map/pallas_call | solution.py:144
  125.4 2.8 %collective-permute-done.23.pb = f32[1,4096]{1,0:T(1,128)S(1)} collective-permute-done((f32[1,4096]{1,0:T(1,128)S(1)}, f32[1,4096]{1,0:T(1,128)S(1)}, u32[]{:S(2)}, u32[]{:S(2)}) %collective-permute-start.23) | collective-permute-done | bytes 16416 | tf_op jit(solution)/shard_map/ppermute | solution.py:25
  128.2 5.3 %shard_map.60 = (f32[1,4096]{1,0:T(1,128)S(1)}, f32[1,4096]{1,0:T(1,128)S(1)}) custom-call(f32[1,4096]{1,0:T(1,128)S(1)} %log_add_fusion.pa, f32[1,4096]{1,0:T(1,128)S(1)} %collective-permute-done.23.pb, f32[1,1024]{1,0:T(1,128)S(1)} %get-tuple-element.80.u.refs_4_, f32[1,1024]{1,0:T(1,128)S(1)} %get-tuple-element.59.lw, ...), custom_call_target="tpu_custom_call" | custom-call | tf_op jit(solution)/shard_map/pallas_call | solution.py:144
  138.5 2.8 %collective-permute-done.26.pb = f32[1,4096]{1,0:T(1,128)S(1)} collective-permute-done((f32[1,4096]{1,0:T(1,128)S(1)}, f32[1,4096]{1,0:T(1,128)S(1)}, u32[]{:S(2)}, u32[]{:S(2)}) %collective-permute-start.26) | collective-permute-done | bytes 16416 | tf_op jit(solution)/shard_map/ppermute | solution.py:25
  141.3 6.5 %shard_map.61 = (f32[1,4096]{1,0:T(1,128)S(1)}, f32[1,1024]{1,0:T(1,128)S(1)}) custom-call(f32[1,4096]{1,0:T(1,128)S(1)} %add.115.pa, f32[1,4096]{1,0:T(1,128)S(1)} %collective-permute-done.26.pb, f32[1,1024]{1,0:T(1,128)S(1)} %get-tuple-element.80.u.refs_4_, f32[1,4096]{1,0:T(1,128)S(1)} %get-tuple-element.83.v.refs_9_, ...), custom_call_target="tpu_custom_call" | custom-call | tf_op jit(solution)/shard_map/pallas_call | solution.py:144
  150.4 3.5 %shard_map.62 = (f32[1,1024]{1,0:T(1,128)S(1)}, f32[1,4096]{1,0:T(1,128)S(1)}) custom-call(f32[1,1024]{1,0:T(1,128)S(1)} %get-tuple-element.85.pa, f32[1,1024]{1,0:T(1,128)S(1)} %collective-permute-done.27.pb, f32[1,1024]{1,0:T(1,128)S(1)} %get-tuple-element.80.u.refs_4_, f32[1,4096]{1,0:T(1,128)S(1)} %get-tuple-element.79.v_old.v.refs_8_, ...), custom_call_target="tpu_custom_call" | custom-call | tf_op jit(solution)/shard_map/pallas_call | solution.py:144
  160.1 2.8 %collective-permute-done.30.pb = f32[1,4096]{1,0:T(1,128)S(1)} collective-permute-done((f32[1,4096]{1,0:T(1,128)S(1)}, f32[1,4096]{1,0:T(1,128)S(1)}, u32[]{:S(2)}, u32[]{:S(2)}) %collective-permute-start.30) | collective-permute-done | bytes 16416 | tf_op jit(solution)/shard_map/ppermute | solution.py:25
  162.8 4.3 %shard_map.63 = (f32[1,4096]{1,0:T(1,128)S(1)}, f32[1,1024]{1,0:T(1,128)S(1)}) custom-call(f32[1,4096]{1,0:T(1,128)S(1)} %add.117.pa, f32[1,4096]{1,0:T(1,128)S(1)} %collective-permute-done.30.pb, f32[1,1024]{1,0:T(1,128)S(1)} %get-tuple-element.76.u_old.u.refs_3_, f32[1,4096]{1,0:T(1,128)S(1)} %get-tuple-element.79.v_old.v.refs_8_, ...), custom_call_target="tpu_custom_call" | custom-call | tf_op jit(solution)/shard_map/pallas_call | solution.py:144
  169.9 3.5 %shard_map.64 = (f32[1,1024]{1,0:T(1,128)S(1)}, f32[1,4096]{1,0:T(1,128)S(1)}) custom-call(f32[1,1024]{1,0:T(1,128)S(1)} %get-tuple-element.87.pa, f32[1,1024]{1,0:T(1,128)S(1)} %collective-permute-done.31.pb, f32[1,1024]{1,0:T(1,128)S(1)} %get-tuple-element.76.u_old.u.refs_3_, f32[1,4096]{1,0:T(1,128)S(1)} %get-tuple-element.75.v_old.v.refs_7_, ...), custom_call_target="tpu_custom_call" | custom-call | tf_op jit(solution)/shard_map/pallas_call | solution.py:144
  182.4 4.3 %shard_map.65 = (f32[1,4096]{1,0:T(1,128)S(1)}, f32[1,1024]{1,0:T(1,128)S(1)}) custom-call(f32[1,4096]{1,0:T(1,128)S(1)} %add.119.pa, f32[1,4096]{1,0:T(1,128)S(1)} %collective-permute-done.34.pb, f32[1,1024]{1,0:T(1,128)S(1)} %get-tuple-element.72.u_old.u.refs_2_, f32[1,4096]{1,0:T(1,128)S(1)} %get-tuple-element.75.v_old.v.refs_7_, ...), custom_call_target="tpu_custom_call" | custom-call | tf_op jit(solution)/shard_map/pallas_call | solution.py:144
  189.2 3.5 %shard_map.66 = (f32[1,1024]{1,0:T(1,128)S(1)}, f32[1,4096]{1,0:T(1,128)S(1)}) custom-call(f32[1,1024]{1,0:T(1,128)S(1)} %get-tuple-element.89.pa, f32[1,1024]{1,0:T(1,128)S(1)} %collective-permute-done.35.pb, f32[1,1024]{1,0:T(1,128)S(1)} %get-tuple-element.72.u_old.u.refs_2_, f32[1,4096]{1,0:T(1,128)S(1)} %get-tuple-element.71.v_old.v.refs_6_, ...), custom_call_target="tpu_custom_call" | custom-call | tf_op jit(solution)/shard_map/pallas_call | solution.py:144
  201.7 4.3 %shard_map.67 = (f32[1,4096]{1,0:T(1,128)S(1)}, f32[1,1024]{1,0:T(1,128)S(1)}) custom-call(f32[1,4096]{1,0:T(1,128)S(1)} %add.121.pa, f32[1,4096]{1,0:T(1,128)S(1)} %collective-permute-done.38.pb, f32[1,1024]{1,0:T(1,128)S(1)} %get-tuple-element.68.u_old.u.refs_1_, f32[1,4096]{1,0:T(1,128)S(1)} %get-tuple-element.71.v_old.v.refs_6_, ...), custom_call_target="tpu_custom_call" | custom-call | tf_op jit(solution)/shard_map/pallas_call | solution.py:144
  208.5 3.5 %shard_map.68 = (f32[1,1024]{1,0:T(1,128)S(1)}, f32[1,4096]{1,0:T(1,128)S(1)}) custom-call(f32[1,1024]{1,0:T(1,128)S(1)} %get-tuple-element.91.pa, f32[1,1024]{1,0:T(1,128)S(1)} %collective-permute-done.39.pb, f32[1,1024]{1,0:T(1,128)S(1)} %get-tuple-element.68.u_old.u.refs_1_, f32[1,4096]{1,0:T(1,128)S(1)} %get-tuple-element.67.v_old.v.refs_5_, ...), custom_call_target="tpu_custom_call" | custom-call | tf_op jit(solution)/shard_map/pallas_call | solution.py:144
  221.0 4.3 %shard_map.69 = (f32[1,4096]{1,0:T(1,128)S(1)}, f32[1,1024]{1,0:T(1,128)S(1)}) custom-call(f32[1,4096]{1,0:T(1,128)S(1)} %add.123.pa, f32[1,4096]{1,0:T(1,128)S(1)} %collective-permute-done.42.pb, f32[1,1024]{1,0:T(1,128)S(1)} %get-tuple-element.64.u_old.u.refs_0_, f32[1,4096]{1,0:T(1,128)S(1)} %get-tuple-element.67.v_old.v.refs_5_, ...), custom_call_target="tpu_custom_call" | custom-call | tf_op jit(solution)/shard_map/pallas_call | solution.py:144
  227.8 8.2 %final.1 = (bf16[4,32,128]{2,1,0:T(8,128)(2,1)S(1)}, bf16[32,32,128]{2,1,0:T(8,128)(2,1)}, f32[1,256]{1,0:T(1,128)}) custom-call(s32[2]{0:T(128)S(1)} %pad_add_fusion.place, bf16[4096,128]{1,0:T(8,128)(2,1)S(1)} %get-tuple-element.56.both, bf16[1024,128]{1,0:T(8,128)(2,1)S(1)} %get-tuple-element.57.left_r, bf16[64,1024]{1,0:T(8,128)(2,1)S(1)} %get-tuple-element.58.right_r, ...), custom_call_target="tpu_custom_call" | custom-call | tf_op jit(solution)/shard_map/final/pallas_call | solution.py:523
  236.0 7.1 %all-to-all-start.1 = ((bf16[32,32,128]{2,1,0:T(8,128)(2,1)}), bf16[32,32,128]{2,1,0:T(8,128)(2,1)S(1)}, u32[]{:S(2)}, u32[]{:S(2)}) async-start(bf16[32,32,128]{2,1,0:T(8,128)(2,1)} %get-tuple-element.104), calls=%async_computation.1 | async-start | bytes 524288 | tf_op jit(solution)/shard_map/all_to_all | solution.py:556
  (123 shorter events, 116.2 us)
Async XLA Ops:
  21.8 10.6 %collective-permute-start = (bf16[16,128,128]{2,1,0:T(8,128)(2,1)S(1)}, bf16[16,128,128]{2,1,0:T(8,128)(2,1)S(1)}, u32[]{:S(2)}, u32[]{:S(2)}) collective-permute-start(bf16[16,128,128]{2,1,0:T(8,128)(2,1)S(1)} %all_to_all.10.mine), channel_id=1, source_target_pairs={{0,4},{1,5},{2,6},{3,7},{4,0},{5,1},{6,2},{7,3},{8,12},{9,13},{10,... | collective-permute-start | bytes 1572872 | tf_op jit(solution)/shard_map/ppermute | solution.py:25
  23.9 5.7 %collective-permute-start.1 = (bf16[144,128]{1,0:T(8,128)(2,1)S(1)}, bf16[144,128]{1,0:T(8,128)(2,1)S(1)}, u32[]{:S(2)}, u32[]{:S(2)}) collective-permute-start(bf16[144,128]{1,0:T(8,128)(2,1)S(1)} %get-tuple-element.55.own), channel_id=1, source_target_pairs={{0,16},{1,17},{2,18},{3,19},{4,20},{5,21},{6,22},{7,23},{8,24},{9,... | collective-permute-start | bytes 110600 | tf_op jit(solution)/shard_map/ppermute | solution.py:25
  24.4 5.2 %collective-permute-start.2 = (bf16[144,128]{1,0:T(8,128)(2,1)S(1)}, bf16[144,128]{1,0:T(8,128)(2,1)S(1)}, u32[]{:S(2)}, u32[]{:S(2)}) collective-permute-start(bf16[144,128]{1,0:T(8,128)(2,1)S(1)} %get-tuple-element.55.own), channel_id=1, source_target_pairs={{0,64},{1,65},{2,66},{3,67},{4,68},{5,69},{6,70},{7,71},{8,72},{9,... | collective-permute-start | bytes 110600 | tf_op jit(solution)/shard_map/ppermute | solution.py:25
  25.7 6.7 %collective-permute-start.3 = (bf16[144,128]{1,0:T(8,128)(2,1)S(1)}, bf16[144,128]{1,0:T(8,128)(2,1)S(1)}, u32[]{:S(2)}, u32[]{:S(2)}) collective-permute-start(bf16[144,128]{1,0:T(8,128)(2,1)S(1)} %get-tuple-element.55.own), channel_id=1, source_target_pairs={{0,80},{1,81},{2,82},{3,83},{4,84},{5,85},{6,86},{7,87},{8,88},{9,... | collective-permute-start | bytes 110600 | tf_op jit(solution)/shard_map/ppermute | solution.py:25
  45.2 3.8 %collective-permute-start.5 = (f32[1,4096]{1,0:T(1,128)S(1)}, f32[1,4096]{1,0:T(1,128)S(1)}, u32[]{:S(2)}, u32[]{:S(2)}) collective-permute-start(f32[1,4096]{1,0:T(1,128)S(1)} %get-tuple-element.65), channel_id=1, source_target_pairs={{0,4},{1,5},{2,6},{3,7},{4,0},{5,1},{6,2},{7,3},{8,12},{9,13},{10,... | collective-permute-start | bytes 49160 | tf_op jit(solution)/shard_map/ppermute | solution.py:25
  49.1 3.2 %collective-permute-start.6 = (f32[1,4096]{1,0:T(1,128)S(1)}, f32[1,4096]{1,0:T(1,128)S(1)}, u32[]{:S(2)}, u32[]{:S(2)}) collective-permute-start(f32[1,4096]{1,0:T(1,128)S(1)} %log_add_fusion.9), channel_id=1, source_target_pairs={{0,12},{1,13},{2,14},{3,15},{4,8},{5,9},{6,10},{7,11},{8,4},{9,5},... | collective-permute-start | bytes 49160 | tf_op jit(solution)/shard_map/ppermute | solution.py:25
  52.4 3.2 %collective-permute-start.7 = (f32[1,4096]{1,0:T(1,128)S(1)}, f32[1,4096]{1,0:T(1,128)S(1)}, u32[]{:S(2)}, u32[]{:S(2)}) collective-permute-start(f32[1,4096]{1,0:T(1,128)S(1)} %log_add_fusion.8.pa), channel_id=1, source_target_pairs={{0,36},{1,37},{2,38},{3,39},{4,32},{5,33},{6,34},{7,35},{8,44},{9,... | collective-permute-start | bytes 49160 | tf_op jit(solution)/shard_map/ppermute | solution.py:25
  58.8 2.5 %collective-permute-start.8 = (f32[1,1024]{1,0:T(1,128)S(1)}, f32[1,1024]{1,0:T(1,128)S(1)}, u32[]{:S(2)}, u32[]{:S(2)}) collective-permute-start(f32[1,1024]{1,0:T(1,128)S(1)} %get-tuple-element.66.pa), channel_id=1, source_target_pairs={{0,1},{1,0},{2,3},{3,2},{4,5},{5,4},{6,7},{7,6},{8,9},{9,8},{10,11... | collective-permute-start | bytes 12296 | tf_op jit(solution)/shard_map/ppermute | solution.py:25
  67.2 3.2 %collective-permute-start.10 = (f32[1,4096]{1,0:T(1,128)S(1)}, f32[1,4096]{1,0:T(1,128)S(1)}, u32[]{:S(2)}, u32[]{:S(2)}) collective-permute-start(f32[1,4096]{1,0:T(1,128)S(1)} %log_add_fusion.7), channel_id=1, source_target_pairs={{0,12},{1,13},{2,14},{3,15},{4,8},{5,9},{6,10},{7,11},{8,4},{9,5},... | collective-permute-start | bytes 49160 | tf_op jit(solution)/shard_map/ppermute | solution.py:25
  70.5 3.2 %collective-permute-start.11 = (f32[1,4096]{1,0:T(1,128)S(1)}, f32[1,4096]{1,0:T(1,128)S(1)}, u32[]{:S(2)}, u32[]{:S(2)}) collective-permute-start(f32[1,4096]{1,0:T(1,128)S(1)} %log_add_fusion.6.pa), channel_id=1, source_target_pairs={{0,36},{1,37},{2,38},{3,39},{4,32},{5,33},{6,34},{7,35},{8,44},{9,... | collective-permute-start | bytes 49160 | tf_op jit(solution)/shard_map/ppermute | solution.py:25
  85.3 3.2 %collective-permute-start.14 = (f32[1,4096]{1,0:T(1,128)S(1)}, f32[1,4096]{1,0:T(1,128)S(1)}, u32[]{:S(2)}, u32[]{:S(2)}) collective-permute-start(f32[1,4096]{1,0:T(1,128)S(1)} %log_add_fusion.5), channel_id=1, source_target_pairs={{0,12},{1,13},{2,14},{3,15},{4,8},{5,9},{6,10},{7,11},{8,4},{9,5},... | collective-permute-start | bytes 49160 | tf_op jit(solution)/shard_map/ppermute | solution.py:25
  88.6 3.2 %collective-permute-start.15 = (f32[1,4096]{1,0:T(1,128)S(1)}, f32[1,4096]{1,0:T(1,128)S(1)}, u32[]{:S(2)}, u32[]{:S(2)}) collective-permute-start(f32[1,4096]{1,0:T(1,128)S(1)} %log_add_fusion.4.pa), channel_id=1, source_target_pairs={{0,36},{1,37},{2,38},{3,39},{4,32},{5,33},{6,34},{7,35},{8,44},{9,... | collective-permute-start | bytes 49160 | tf_op jit(solution)/shard_map/ppermute | solution.py:25
  95.0 2.7 %collective-permute-start.16 = (f32[1,1024]{1,0:T(1,128)S(1)}, f32[1,1024]{1,0:T(1,128)S(1)}, u32[]{:S(2)}, u32[]{:S(2)}) collective-permute-start(f32[1,1024]{1,0:T(1,128)S(1)} %get-tuple-element.74.pa), channel_id=1, source_target_pairs={{0,1},{1,0},{2,3},{3,2},{4,5},{5,4},{6,7},{7,6},{8,9},{9,8},{10,11... | collective-permute-start | bytes 12296 | tf_op jit(solution)/shard_map/ppermute | solution.py:25
  103.5 3.2 %collective-permute-start.18 = (f32[1,4096]{1,0:T(1,128)S(1)}, f32[1,4096]{1,0:T(1,128)S(1)}, u32[]{:S(2)}, u32[]{:S(2)}) collective-permute-start(f32[1,4096]{1,0:T(1,128)S(1)} %log_add_fusion.3), channel_id=1, source_target_pairs={{0,12},{1,13},{2,14},{3,15},{4,8},{5,9},{6,10},{7,11},{8,4},{9,5},... | collective-permute-start | bytes 49160 | tf_op jit(solution)/shard_map/ppermute | solution.py:25
  106.8 3.2 %collective-permute-start.19 = (f32[1,4096]{1,0:T(1,128)S(1)}, f32[1,4096]{1,0:T(1,128)S(1)}, u32[]{:S(2)}, u32[]{:S(2)}) collective-permute-start(f32[1,4096]{1,0:T(1,128)S(1)} %log_add_fusion.2.pa), channel_id=1, source_target_pairs={{0,36},{1,37},{2,38},{3,39},{4,32},{5,33},{6,34},{7,35},{8,44},{9,... | collective-permute-start | bytes 49160 | tf_op jit(solution)/shard_map/ppermute | solution.py:25
  121.6 3.2 %collective-permute-start.22 = (f32[1,4096]{1,0:T(1,128)S(1)}, f32[1,4096]{1,0:T(1,128)S(1)}, u32[]{:S(2)}, u32[]{:S(2)}) collective-permute-start(f32[1,4096]{1,0:T(1,128)S(1)} %log_add_fusion.1), channel_id=1, source_target_pairs={{0,12},{1,13},{2,14},{3,15},{4,8},{5,9},{6,10},{7,11},{8,4},{9,5},... | collective-permute-start | bytes 49160 | tf_op jit(solution)/shard_map/ppermute | solution.py:25
  124.9 3.2 %collective-permute-start.23 = (f32[1,4096]{1,0:T(1,128)S(1)}, f32[1,4096]{1,0:T(1,128)S(1)}, u32[]{:S(2)}, u32[]{:S(2)}) collective-permute-start(f32[1,4096]{1,0:T(1,128)S(1)} %log_add_fusion.pa), channel_id=1, source_target_pairs={{0,36},{1,37},{2,38},{3,39},{4,32},{5,33},{6,34},{7,35},{8,44},{9,... | collective-permute-start | bytes 49160 | tf_op jit(solution)/shard_map/ppermute | solution.py:25
  134.8 3.2 %collective-permute-start.25 = (f32[1,4096]{1,0:T(1,128)S(1)}, f32[1,4096]{1,0:T(1,128)S(1)}, u32[]{:S(2)}, u32[]{:S(2)}) collective-permute-start(f32[1,4096]{1,0:T(1,128)S(1)} %add.114), channel_id=1, source_target_pairs={{0,12},{1,13},{2,14},{3,15},{4,8},{5,9},{6,10},{7,11},{8,4},{9,5},... | collective-permute-start | bytes 49160 | tf_op jit(solution)/shard_map/ppermute | solution.py:25
  138.1 3.2 %collective-permute-start.26 = (f32[1,4096]{1,0:T(1,128)S(1)}, f32[1,4096]{1,0:T(1,128)S(1)}, u32[]{:S(2)}, u32[]{:S(2)}) collective-permute-start(f32[1,4096]{1,0:T(1,128)S(1)} %add.115.pa), channel_id=1, source_target_pairs={{0,36},{1,37},{2,38},{3,39},{4,32},{5,33},{6,34},{7,35},{8,44},{9,... | collective-permute-start | bytes 49160 | tf_op jit(solution)/shard_map/ppermute | solution.py:25
  156.3 3.2 %collective-permute-start.29 = (f32[1,4096]{1,0:T(1,128)S(1)}, f32[1,4096]{1,0:T(1,128)S(1)}, u32[]{:S(2)}, u32[]{:S(2)}) collective-permute-start(f32[1,4096]{1,0:T(1,128)S(1)} %add.116), channel_id=1, source_target_pairs={{0,12},{1,13},{2,14},{3,15},{4,8},{5,9},{6,10},{7,11},{8,4},{9,5},... | collective-permute-start | bytes 49160 | tf_op jit(solution)/shard_map/ppermute | solution.py:25
  159.6 3.2 %collective-permute-start.30 = (f32[1,4096]{1,0:T(1,128)S(1)}, f32[1,4096]{1,0:T(1,128)S(1)}, u32[]{:S(2)}, u32[]{:S(2)}) collective-permute-start(f32[1,4096]{1,0:T(1,128)S(1)} %add.117.pa), channel_id=1, source_target_pairs={{0,36},{1,37},{2,38},{3,39},{4,32},{5,33},{6,34},{7,35},{8,44},{9,... | collective-permute-start | bytes 49160 | tf_op jit(solution)/shard_map/ppermute | solution.py:25
  167.1 2.8 %collective-permute-start.31 = (f32[1,1024]{1,0:T(1,128)S(1)}, f32[1,1024]{1,0:T(1,128)S(1)}, u32[]{:S(2)}, u32[]{:S(2)}) collective-permute-start(f32[1,1024]{1,0:T(1,128)S(1)} %get-tuple-element.87.pa), channel_id=1, source_target_pairs={{0,1},{1,0},{2,3},{3,2},{4,5},{5,4},{6,7},{7,6},{8,9},{9,8},{10,11... | collective-permute-start | bytes 12296 | tf_op jit(solution)/shard_map/ppermute | solution.py:25
  175.8 3.2 %collective-permute-start.33 = (f32[1,4096]{1,0:T(1,128)S(1)}, f32[1,4096]{1,0:T(1,128)S(1)}, u32[]{:S(2)}, u32[]{:S(2)}) collective-permute-start(f32[1,4096]{1,0:T(1,128)S(1)} %add.118), channel_id=1, source_target_pairs={{0,12},{1,13},{2,14},{3,15},{4,8},{5,9},{6,10},{7,11},{8,4},{9,5},... | collective-permute-start | bytes 49160 | tf_op jit(solution)/shard_map/ppermute | solution.py:25
  179.1 3.2 %collective-permute-start.34 = (f32[1,4096]{1,0:T(1,128)S(1)}, f32[1,4096]{1,0:T(1,128)S(1)}, u32[]{:S(2)}, u32[]{:S(2)}) collective-permute-start(f32[1,4096]{1,0:T(1,128)S(1)} %add.119.pa), channel_id=1, source_target_pairs={{0,36},{1,37},{2,38},{3,39},{4,32},{5,33},{6,34},{7,35},{8,44},{9,... | collective-permute-start | bytes 49160 | tf_op jit(solution)/shard_map/ppermute | solution.py:25
  195.2 3.2 %collective-permute-start.37 = (f32[1,4096]{1,0:T(1,128)S(1)}, f32[1,4096]{1,0:T(1,128)S(1)}, u32[]{:S(2)}, u32[]{:S(2)}) collective-permute-start(f32[1,4096]{1,0:T(1,128)S(1)} %add.120), channel_id=1, source_target_pairs={{0,12},{1,13},{2,14},{3,15},{4,8},{5,9},{6,10},{7,11},{8,4},{9,5},... | collective-permute-start | bytes 49160 | tf_op jit(solution)/shard_map/ppermute | solution.py:25
  198.4 3.2 %collective-permute-start.38 = (f32[1,4096]{1,0:T(1,128)S(1)}, f32[1,4096]{1,0:T(1,128)S(1)}, u32[]{:S(2)}, u32[]{:S(2)}) collective-permute-start(f32[1,4096]{1,0:T(1,128)S(1)} %add.121.pa), channel_id=1, source_target_pairs={{0,36},{1,37},{2,38},{3,39},{4,32},{5,33},{6,34},{7,35},{8,44},{9,... | collective-permute-start | bytes 49160 | tf_op jit(solution)/shard_map/ppermute | solution.py:25
  214.5 3.2 %collective-permute-start.41 = (f32[1,4096]{1,0:T(1,128)S(1)}, f32[1,4096]{1,0:T(1,128)S(1)}, u32[]{:S(2)}, u32[]{:S(2)}) collective-permute-start(f32[1,4096]{1,0:T(1,128)S(1)} %add.122), channel_id=1, source_target_pairs={{0,12},{1,13},{2,14},{3,15},{4,8},{5,9},{6,10},{7,11},{8,4},{9,5},... | collective-permute-start | bytes 49160 | tf_op jit(solution)/shard_map/ppermute | solution.py:25
  217.7 3.2 %collective-permute-start.42 = (f32[1,4096]{1,0:T(1,128)S(1)}, f32[1,4096]{1,0:T(1,128)S(1)}, u32[]{:S(2)}, u32[]{:S(2)}) collective-permute-start(f32[1,4096]{1,0:T(1,128)S(1)} %add.123.pa), channel_id=1, source_target_pairs={{0,36},{1,37},{2,38},{3,39},{4,32},{5,33},{6,34},{7,35},{8,44},{9,... | collective-permute-start | bytes 49160 | tf_op jit(solution)/shard_map/ppermute | solution.py:25
  236.0 16.0 %all-to-all-start.1 = ((bf16[32,32,128]{2,1,0:T(8,128)(2,1)}), bf16[32,32,128]{2,1,0:T(8,128)(2,1)S(1)}, u32[]{:S(2)}, u32[]{:S(2)}) async-start(bf16[32,32,128]{2,1,0:T(8,128)(2,1)} %get-tuple-element.104), calls=%async_computation.1 | async-start | bytes 524288 | tf_op jit(solution)/shard_map/all_to_all | solution.py:556
  243.1 3.9 %collective-permute-start.44 = (bf16[32,128]{1,0:T(8,128)(2,1)S(1)}, bf16[32,128]{1,0:T(8,128)(2,1)S(1)}, u32[]{:S(2)}, u32[]{:S(2)}) collective-permute-start(bf16[32,128]{1,0:T(8,128)(2,1)S(1)} %get-tuple-element.108), channel_id=1, source_target_pairs={{0,1},{1,0},{2,3},{3,2},{4,5},{5,4},{6,7},{7,6},{8,9},{9,8},{10,11... | collective-permute-start | bytes 24584 | tf_op jit(solution)/shard_map/ppermute | solution.py:25
  244.4 4.3 %collective-permute-start.45 = (bf16[32,128]{1,0:T(8,128)(2,1)S(1)}, bf16[32,128]{1,0:T(8,128)(2,1)S(1)}, u32[]{:S(2)}, u32[]{:S(2)}) collective-permute-start(bf16[32,128]{1,0:T(8,128)(2,1)S(1)} %get-tuple-element.107), channel_id=1, source_target_pairs={{0,2},{1,3},{2,0},{3,1},{4,6},{5,7},{6,4},{7,5},{8,10},{9,11},{10,... | collective-permute-start | bytes 24584 | tf_op jit(solution)/shard_map/ppermute | solution.py:25
  246.8 4.0 %collective-permute-start.46 = (bf16[32,128]{1,0:T(8,128)(2,1)S(1)}, bf16[32,128]{1,0:T(8,128)(2,1)S(1)}, u32[]{:S(2)}, u32[]{:S(2)}) collective-permute-start(bf16[32,128]{1,0:T(8,128)(2,1)S(1)} %get-tuple-element.106), channel_id=1, source_target_pairs={{0,3},{1,2},{2,1},{3,0},{4,7},{5,6},{6,5},{7,4},{8,11},{9,10},{10,... | collective-permute-start | bytes 24584 | tf_op jit(solution)/shard_map/ppermute | solution.py:25
  (21 other events, 42.4 us)

commit v3 on v2

--- a/solution.py
+++ b/solution.py
@@ -14,9 +14,10 @@
 X0, CORE, Y0, Y1, Z0, Z1 = 1, 4, 8, 16, 32, 64
 LW_TOP = 145.0
 TINY = 1e-37
-BLOCK = 256
-SPAN = 1024
-SMALL = pltpu.CompilerParams(vmem_limit_bytes=24 * 2**20)
+BLOCK = 128
+SPAN = 512
+SAFE = 15.0
+SMALL = pltpu.CompilerParams(vmem_limit_bytes=20 * 2**20)
 F32 = jnp.float32
 BF16 = jnp.bfloat16
 
@@ -73,71 +74,108 @@
 
 def tile_pass(mode, left, right, rows, cols, scratch, emit, pair=None):
     left_x, right_x = scratch[:2]
-    height = BLOCK if pair is None else BLOCK // 2
-    deep = 2 if mode == "weight" else 4
     weighted = mode in ("weight", "pair_weight")
     if weighted:
         weight = scratch[2]
         at = lax.broadcasted_iota(jnp.int32, (16, 128), 0)
         pick = jnp.where((at >= 6) & (at < 9), 1.0, 0.0).astype(BF16)
-        for m in range(0, rows, 512):
-            weight[m : m + 512, :] = mm(left_x[:, m : m + 512].T, pick)
-    low = jnp.zeros((64, height), BF16)
-    high = jnp.zeros((48, height), BF16)
-
-    def block(m0, right_block, pair_block, acc):
-        x = jnp.concatenate([low, left_x[:, pl.ds(m0, height)], high], axis=0)
-        a = left[pl.ds(m0, height), :] + x.T
-        t = mm(a, right_block)
-        e = jnp.exp(t)
-        if weighted:
-            w = weight[pl.ds(m0, height), :]
-        if pair is not None:
-            pr = mm(pair[0][pl.ds(m0, height), :], pair_block)
-        out = []
-        for q in range(SPAN // 128):
-            y = e[:, q * 128 : (q + 1) * 128]
+
+        def spread(i, carry):
+            m = pl.ds(pl.multiple_of(i * BLOCK, BLOCK), BLOCK)
+            weight[m, :] = mm(left_x[:, m].T, pick)
+            return carry
+
+        lax.fori_loop(0, rows // BLOCK, spread, 0)
+    low = jnp.zeros((64, BLOCK), BF16)
+    high = jnp.zeros((48, BLOCK), BF16)
+    tail = jnp.zeros((48, SPAN), BF16)
+
+    def of_span(j, carry):
+        n = pl.ds(pl.multiple_of(j * SPAN, SPAN), SPAN)
+        right_block = jnp.concatenate([right[:, n], right_x[:, n], tail], axis=0)
+
+        def of_block(i, acc):
+            m = pl.ds(pl.multiple_of(i * BLOCK, BLOCK), BLOCK)
+            a = left[m, :] + jnp.concatenate([low, left_x[:, m], high], axis=0).T
+            y = jnp.exp(mm(a, right_block))
+            if weighted:
+                w = jnp.concatenate([weight[m, :]] * (SPAN // 128), axis=1)
+            if pair is not None:
+                pr = mm(pair[0][m, :], pair[1][:, n])
             if mode == "weight":
                 y = y * w
             elif mode == "pair":
-                y = y * pr[:, q * 128 : (q + 1) * 128]
+                y = y * pr
             elif mode == "pair_weight":
-                y = y * (pr[:, q * 128 : (q + 1) * 128] - w)
-            y = y.reshape(height // 8, 8, 128)
-            out.append(acc[q] + jnp.sum(y, axis=0))
-        return tuple(out)
-
-    def right_of(n0):
-        sl = pl.ds(n0, SPAN)
-        full = jnp.concatenate([right[:, sl], right_x[:, sl], jnp.zeros((48, SPAN), BF16)], axis=0)
-        return full, None if pair is None else pair[1][:, sl]
-
-    def fold(acc):
-        return jnp.concatenate([jnp.sum(a, axis=0, keepdims=True) for a in acc], axis=1)
-
-    zero = (jnp.zeros((8, 128), F32),) * (SPAN // 128)
-    if rows > cols:
-        right_block, pair_block = right_of(0)
-
-        def step(i, acc):
-            for b in range(deep):
-                m0 = pl.multiple_of((deep * i + b) * height, height)
-                acc = block(m0, right_block, pair_block, acc)
-            return acc
-
-        emit(slice(None), fold(lax.fori_loop(0, rows // (deep * height), step, zero)))
-    else:
-
-        def step(i, carry):
-            n0 = pl.multiple_of(i * SPAN, SPAN)
-            right_block, pair_block = right_of(n0)
-            acc = zero
-            for m0 in range(0, rows, height):
-                acc = block(m0, right_block, pair_block, acc)
-            emit(pl.ds(n0, SPAN), fold(acc))
-            return carry
-
-        lax.fori_loop(0, cols // SPAN, step, 0)
+                y = y * (pr - w)
+            return acc + jnp.sum(y.reshape(BLOCK // 8, 8, SPAN), axis=0)
+
+        acc = lax.fori_loop(0, rows // BLOCK, of_block, jnp.zeros((8, SPAN), F32))
+        emit(n, jnp.sum(acc, axis=0, keepdims=True))
+        return carry
+
+    lax.fori_loop(0, cols // SPAN, of_span, 0)
+
+
+def column(vector, out):
+    n = vector.shape[1]
+    at = lax.broadcasted_iota(jnp.int32, (16, n), 0)
+    rows = jnp.zeros((16, n), F32)
+    for i, part in enumerate(parts(vector)):
+        rows = jnp.where(at == i, part, rows)
+    at = lax.broadcasted_iota(jnp.int32, (16, 128), 0)
+    out[...] = mm(rows.astype(BF16).T, jnp.where(at < 3, 1.0, 0.0).astype(BF16))
+
+
+def sum_rows(tile, weight, emit, pair=None):
+    rows, cols = tile.shape
+    span = 1024
+
+    def step(j, carry):
+        n = pl.ds(pl.multiple_of(j * span, span), span)
+        acc = [jnp.zeros((8, 128), F32)] * (span // 128)
+        height = 64 if pair is None else 256
+        for m in range(0, rows, height):
+            w = weight[m : m + height, :]
+            if pair is not None:
+                pr = mm(pair[0][m : m + height, :], pair[1][:, n])
+            for q in range(span // 128):
+                y = tile[m : m + height, pl.ds(pl.multiple_of(j * span + q * 128, 128), 128)] * w
+                if pair is not None:
+                    y = y * pr[:, q * 128 : (q + 1) * 128]
+                acc[q] = acc[q] + jnp.sum(y.reshape(height // 8, 8, 128), axis=0)
+        emit(n, jnp.concatenate([jnp.sum(x, axis=0, keepdims=True) for x in acc], axis=1))
+        return carry
+
+    lax.fori_loop(0, cols // span, step, 0)
+
+
+def sum_cols(tile, weight, emit, pair=None):
+    rows, cols = tile.shape
+    height = 256
+
+    def step(i, carry):
+        m = pl.ds(pl.multiple_of(i * height, height), height)
+        acc = jnp.zeros((height, 128), F32)
+        for n in range(0, cols, 512):
+            if pair is not None:
+                pr = mm(pair[0][m, :], pair[1][:, n : n + 512])
+            for q in range(4):
+                lanes = slice(n + q * 128, n + (q + 1) * 128)
+                w = weight[0:1, lanes]
+                if pair is not None:
+                    w = pr[:, q * 128 : (q + 1) * 128] * w - weight[1:2, lanes]
+                acc = acc + tile[m, lanes] * w
+        emit(m, jnp.sum(acc.T, axis=0, keepdims=True))
+        return carry
+
+    lax.fori_loop(0, rows // height, step, 0)
+
+
+def both_ways(safe, fast, slow):
+    ok = jnp.max(safe[...]) > 0.5
+    pl.when(ok)(fast)
+    pl.when(jnp.logical_not(ok))(slow)
 
 
 def call(kernel, out_shapes, scratch, *args):
@@ -145,7 +183,7 @@
         kernel,
         out_shape=tuple(jax.ShapeDtypeStruct(s, d) for s, d in out_shapes),
         scratch_shapes=scratch,
-        compiler_params=SMALL,
+        compiler_params=pltpu.CompilerParams(vmem_limit_bytes=10 * 2**20),
     )(*args)
 
 
@@ -172,7 +210,7 @@
 
 
 def prep_kernel(
-    scale, place, mine, other, own, by_y, by_z, by_zy, left_c, right_c, cot_t, both, sq_c, left_r, right_r, sq_r, lw
+    scale, place, mine, other, own, by_y, by_z, by_zy, left_c, right_c, cot_t, both, sq_c, left_r, right_r, sq_r, lw, safe
 ):
     lane = lax.broadcasted_iota(jnp.int32, (128, 128), 1)
     core, y1, z1 = place[0], place[1], place[2]
@@ -213,6 +251,8 @@
             right_r[:, sl] = turned[64 * h : 64 * h + 64]
             sq_r[:, sl] = norm(turned[64 * h : 64 * h + 64])
             lw[:, sl] = (low[3 * h : 3 * h + 1] + low[3 * h + 1 : 3 * h + 2]) + low[3 * h + 2 : 3 * h + 3]
+    most = jnp.maximum(jnp.max(sq_c[...], axis=1, keepdims=True), jnp.max(sq_r[...], axis=1, keepdims=True))
+    safe[...] = jnp.broadcast_to(jnp.where(most <= SAFE, 1.0, 0.0), safe.shape)
 
 
 def pair_up(x):
@@ -320,104 +360,210 @@
     out[...] = both.T[:64, :]
 
 
-def first_u(left_c, right_r, sq_c, sq_r, out, *scratch):
-    left_x, right_x = scratch[:2]
-    left_x[...] = extra(-sq_c[...], None, True)
-    right_x[...] = extra(-sq_r[...], None, False)
-
-    def emit(at, value):
-        out[...] = jnp.log(jnp.maximum(value, TINY))
-
-    tile_pass("exp", left_c, right_r, sq_c.shape[1], sq_r.shape[1], scratch, emit)
-
-
-def next_v(log_count, is_first, pa, pb, u_old, v_old, lw, left_r, right_c, sq_r, sq_c, u_new, out, base, *scratch):
-    left_x, right_x = scratch[:2]
+def peak(v):
+    return jnp.max(v, axis=1, keepdims=True)
+
+
+def first_u(safe, left_r, right_c, left_c, right_r, sq_c, sq_r, out, tile, acc, row_x, col_x, *scratch):
+    def fast():
+        row_x[...] = extra(-sq_r[...], None, True)
+        col_x[...] = extra(-sq_c[...], None, False)
+        acc[...] = jnp.zeros(acc.shape, F32)
+        low = jnp.zeros((64, 256), BF16)
+        high = jnp.zeros((48, 256), BF16)
+
+        def step(j, carry):
+            n = pl.ds(pl.multiple_of(j * 1024, 1024), 1024)
+            right = jnp.concatenate([right_c[:, n], col_x[:, n], jnp.zeros((48, 1024), BF16)], axis=0)
+            for m in range(0, left_r.shape[0], 256):
+                a = left_r[m : m + 256, :]
+                a = a + jnp.concatenate([low, row_x[:, m : m + 256], high], axis=0).T
+                e = jnp.exp(mm(a, right))
+                tile[m : m + 256, n] = e
+                y = acc[m : m + 256, :]
+                for q in range(8):
+                    y = y + e[:, q * 128 : (q + 1) * 128]
+                acc[m : m + 256, :] = y
+            return carry
+
+        lax.fori_loop(0, tile.shape[1] // 1024, step, 0)
+        out[...] = jnp.log(jnp.sum(acc[...].T, axis=0, keepdims=True))
+
+    def slow():
+        scratch[0][...] = extra(-sq_c[...], None, True)
+        scratch[1][...] = extra(-sq_r[...], None, False)
+
+        def emit(at, value):
+            out[:, at] = jnp.log(jnp.maximum(value, TINY))
+
+        tile_pass("exp", left_c, right_r, sq_c.shape[1], sq_r.shape[1], scratch, emit)
+
+    both_ways(safe, fast, slow)
+
+
+def next_v(
+    log_count, is_first, safe, tile, pa, pb, u_old, v_old, lw, left_r, right_c, sq_r, sq_c, u_new, out, base, w, *scratch
+):
     u = log_count - merge(pa[...], pb[...])
     u_new[...] = u
-    if is_first:
-        base[...] = jnp.full(base.shape, LW_TOP + log_count, F32)
-    else:
-        base[...] = jnp.max(u - u_old[...], axis=1, keepdims=True) - v_old[...]
-    left_x[...] = extra(u + lw[...] - sq_r[...], None, True)
-    right_x[...] = extra(-sq_c[...] - base[...], None, False)
-
-    def emit(at, value):
-        out[:, at] = base[:, at] + jnp.log(jnp.maximum(value, TINY))
-
-    tile_pass("exp", left_r, right_c, sq_r.shape[1], sq_c.shape[1], scratch, emit)
-
-
-def next_u(log_count, pa, pb, v_old, u_old, left_c, right_r, sq_c, sq_r, v_new, out, *scratch):
-    left_x, right_x = scratch[:2]
+
+    def fast():
+        top = peak(u + lw[...])
+        column(jnp.exp(u + lw[...] - top), w)
+
+        def emit(at, value):
+            out[:, at] = top + jnp.log(value)
+
+        sum_rows(tile, w, emit)
+
+    def slow():
+        if is_first:
+            base[...] = jnp.full(base.shape, LW_TOP + log_count, F32)
+        else:
+            base[...] = peak(u - u_old[...]) - v_old[...]
+        scratch[0][...] = extra(u + lw[...] - sq_r[...], None, True)
+        scratch[1][...] = extra(-sq_c[...] - base[...], None, False)
+
+        def emit(at, value):
+            out[:, at] = base[:, at] + jnp.log(jnp.maximum(value, TINY))
+
+        tile_pass("exp", left_r, right_c, sq_r.shape[1], sq_c.shape[1], scratch, emit)
+
+    both_ways(safe, fast, slow)
+
+
+def next_u(log_count, safe, tile, pa, pb, v_old, u_old, left_c, right_r, sq_c, sq_r, v_new, out, base, w, *scratch):
     v = -merge(pa[...], pb[...])
     v_new[...] = v
-    base = (log_count - u_old[...]) + jnp.max(v - v_old[...], axis=1, keepdims=True)
-    left_x[...] = extra(v - sq_c[...], None, True)
-    right_x[...] = extra(-sq_r[...] - base, None, False)
-
-    def emit(at, value):
-        out[...] = base + jnp.log(jnp.maximum(value, TINY))
-
-    tile_pass("exp", left_c, right_r, sq_c.shape[1], sq_r.shape[1], scratch, emit)
-
-
-def first_dv(unscale, pa, pb, u, lw, left_r, right_c, cot_t, sq_r, sq_c, v_new, out, *scratch):
-    left_x, right_x = scratch[:2]
+
+    def fast():
+        top = peak(v)
+        w[0:1, :] = jnp.exp(v - top)
+
+        def emit(at, value):
+            out[:, at] = top + jnp.log(value)
+
+        sum_cols(tile, w, emit)
+
+    def slow():
+        base[...] = (log_count - u_old[...]) + peak(v - v_old[...])
+        scratch[0][...] = extra(v - sq_c[...], None, True)
+        scratch[1][...] = extra(-sq_r[...] - base[...], None, False)
+
+        def emit(at, value):
+            out[:, at] = base[:, at] + jnp.log(jnp.maximum(value, TINY))
+
+        tile_pass("exp", left_c, right_r, sq_c.shape[1], sq_r.shape[1], scratch, emit)
+
+    both_ways(safe, fast, slow)
+
+
+def first_dv(unscale, safe, tile, pa, pb, u, lw, left_r, right_c, cot_t, sq_r, sq_c, v_new, out, w, *scratch):
     v = -merge(pa[...], pb[...])
     v_new[...] = v
-    left_x[...] = extra(u[...] + lw[...] - sq_r[...], None, True)
-    right_x[...] = extra(v - sq_c[...], None, False)
-
-    def emit(at, value):
-        out[:, at] = unscale * value
-
-    tile_pass(
-        "pair", left_r, right_c, sq_r.shape[1], sq_c.shape[1], scratch, emit, (left_r, cot_t)
-    )
-
-
-def first_du(pa, pb, u, v, lw, left_c, right_r, both, sq_c, sq_r, dv_new, out, pair_r, *scratch):
-    left_x, right_x = scratch[:2]
+
+    def fast():
+        top = peak(u[...] + lw[...])
+        column(jnp.exp(u[...] + lw[...] - top), w)
+
+        def emit(at, value):
+            out[:, at] = unscale * jnp.exp(v_new[:, at] + top) * value
+
+        sum_rows(tile, w, emit, (left_r, cot_t))
+
+    def slow():
+        scratch[0][...] = extra(u[...] + lw[...] - sq_r[...], None, True)
+        scratch[1][...] = extra(v - sq_c[...], None, False)
+
+        def emit(at, value):
+            out[:, at] = unscale * value
+
+        pair = (left_r, cot_t)
+        tile_pass("pair", left_r, right_c, sq_r.shape[1], sq_c.shape[1], scratch, emit, pair)
+
+    both_ways(safe, fast, slow)
+
+
+def first_du(
+    unscale, safe, tile, pa, pb, u, v, lw, left_r, cot_t, left_c, right_r, both, sq_c, sq_r, dv_new, out, pair_r, w, *scratch
+):
     dv = pa[...] + pb[...]
     dv_new[...] = dv
-    left_x[...] = extra(v[...] - sq_c[...], dv, True)
-    right_x[...] = extra(u[...] + lw[...] - sq_r[...], None, False)
-    pair_r[:64, :] = jnp.zeros_like(right_r)
-    pair_r[64:, :] = right_r[...]
-
-    def emit(at, value):
-        out[...] = value
-
-    tile_pass(
-        "pair_weight", left_c, right_r, sq_c.shape[1], sq_r.shape[1], scratch, emit, (both, pair_r)
-    )
-
-
-def next_dv(log_count, pa, pb, u, v, left_r, right_c, sq_r, sq_c, du_new, out, *scratch):
-    left_x, right_x = scratch[:2]
+
+    def fast():
+        top = peak(v[...])
+        b = jnp.exp(v[...] - top)
+        w[0:1, :] = unscale * b
+        w[1:2, :] = b * dv
+
+        def emit(at, value):
+            out[:, at] = jnp.exp(u[:, at] + lw[:, at] + top) * value
+
+        sum_cols(tile, w, emit, (left_r, cot_t))
+
+    def slow():
+        scratch[0][...] = extra(v[...] - sq_c[...], dv, True)
+        scratch[1][...] = extra(u[...] + lw[...] - sq_r[...], None, False)
+        pair_r[:64, :] = jnp.zeros_like(right_r)
+        pair_r[64:, :] = right_r[...]
+
+        def emit(at, value):
+            out[:, at] = value
+
+        pair = (both, pair_r)
+        tile_pass("pair_weight", left_c, right_r, sq_c.shape[1], sq_r.shape[1], scratch, emit, pair)
+
+    both_ways(safe, fast, slow)
+
+
+def next_dv(log_count, safe, tile, pa, pb, u, v, left_r, right_c, sq_r, sq_c, du_new, out, w, *scratch):
     du = pa[...] + pb[...]
     du_new[...] = du
-    left_x[...] = extra(u[...] - log_count - sq_r[...], du, True)
-    right_x[...] = extra(v[...] - sq_c[...], None, False)
-
-    def emit(at, value):
-        out[:, at] = -value
-
-    tile_pass("weight", left_r, right_c, sq_r.shape[1], sq_c.shape[1], scratch, emit)
-
-
-def next_du(pa, pb, u, v, lw, left_c, right_r, sq_c, sq_r, dv_new, out, *scratch):
-    left_x, right_x = scratch[:2]
+
+    def fast():
+        top = peak(u[...])
+        column(jnp.exp(u[...] - top) * du, w)
+
+        def emit(at, value):
+            out[:, at] = -jnp.exp(v[:, at] + (top - log_count)) * value
+
+        sum_rows(tile, w, emit)
+
+    def slow():
+        scratch[0][...] = extra(u[...] - log_count - sq_r[...], du, True)
+        scratch[1][...] = extra(v[...] - sq_c[...], None, False)
+
+        def emit(at, value):
+            out[:, at] = -value
+
+        tile_pass("weight", left_r, right_c, sq_r.shape[1], sq_c.shape[1], scratch, emit)
+
+    both_ways(safe, fast, slow)
+
+
+def next_du(safe, tile, pa, pb, u, v, lw, left_c, right_r, sq_c, sq_r, dv_new, out, w, *scratch):
     dv = pa[...] + pb[...]
     dv_new[...] = dv
-    left_x[...] = extra(v[...] - sq_c[...], dv, True)
-    right_x[...] = extra(u[...] + lw[...] - sq_r[...], None, False)
-
-    def emit(at, value):
-        out[...] = -value
-
-    tile_pass("weight", left_c, right_r, sq_c.shape[1], sq_r.shape[1], scratch, emit)
+
+    def fast():
+        top = peak(v[...])
+        w[0:1, :] = jnp.exp(v[...] - top) * dv
+
+        def emit(at, value):
+            out[:, at] = -jnp.exp(u[:, at] + lw[:, at] + top) * value
+
+        sum_cols(tile, w, emit)
+
+    def slow():
+        scratch[0][...] = extra(v[...] - sq_c[...], dv, True)
+        scratch[1][...] = extra(u[...] + lw[...] - sq_r[...], None, False)
+
+        def emit(at, value):
+            out[:, at] = -value
+
+        tile_pass("weight", left_c, right_r, sq_c.shape[1], sq_r.shape[1], scratch, emit)
+
+    both_ways(safe, fast, slow)
 
 
 def local(positions, log_weights, cotangent):
@@ -441,7 +587,7 @@
         others.append(swap(own, bits))
     mine = lax.all_to_all(payload, ("z", "y"), 0, 0, tiled=True)
     other = swap(mine, CORE)
-    left_c, right_c, cot_t, both, sq_c, left_r, right_r, sq_r, lw = pl.pallas_call(
+    left_c, right_c, cot_t, both, sq_c, left_r, right_r, sq_r, lw, safe = pl.pallas_call(
         functools.partial(prep_kernel, scale),
         name="prep",
         compiler_params=SMALL,
@@ -458,13 +604,21 @@
                 ((64, n_r), BF16),
                 ((1, n_r), F32),
                 ((1, n_r), F32),
+                ((1, 128), F32),
             )
         ),
     )(jnp.stack([core, y1, z1]), mine, other, own, *others)
 
     u_like, v_like = ((1, n_r), F32), ((1, n_c), F32)
-
-    (part,) = call(first_u, (u_like,), room(n_c, n_r), left_c, right_r, sq_c, sq_r)
+    w_r, w_c = pltpu.VMEM((n_r, 128), F32), pltpu.VMEM((8, n_c), F32)
+    unscale = 0.5 / scale
+
+    part, tile = call(
+        first_u,
+        (u_like, ((n_r, n_c), F32)),
+        [w_r] + room(n_r, n_c) + room(n_c, n_r),
+        *(safe, left_r, right_c, left_c, right_r, sq_c, sq_r),
+    )
     us, vs = [], [jnp.zeros((1, n_c), F32)]
     for k in range(ITERS):
         pa, pb = over_cols(part)
@@ -472,8 +626,8 @@
         u, part = call(
             functools.partial(next_v, log_count, k == 0),
             (u_like, v_like),
-            [pltpu.VMEM((1, n_c), F32)] + room(n_r, n_c),
-            *(pa, pb, old, vs[-1], lw, left_r, right_c, sq_r, sq_c),
+            [pltpu.VMEM((1, n_c), F32), w_r] + room(n_r, n_c),
+            *(safe, tile, pa, pb, old, vs[-1], lw, left_r, right_c, sq_r, sq_c),
         )
         us.append(u)
         pa, pb = over_rows(part, merge)
@@ -482,24 +636,24 @@
         v, part = call(
             functools.partial(next_u, log_count),
             (v_like, u_like),
-            room(n_c, n_r),
-            *(pa, pb, vs[-1], us[-1], left_c, right_r, sq_c, sq_r),
+            [pltpu.VMEM((1, n_r), F32), w_c] + room(n_c, n_r),
+            *(safe, tile, pa, pb, vs[-1], us[-1], left_c, right_r, sq_c, sq_r),
         )
         vs.append(v)
 
     v, part = call(
-        functools.partial(first_dv, 0.5 / scale),
+        functools.partial(first_dv, unscale),
         (v_like, v_like),
-        room(n_r, n_c),
-        *(pa, pb, us[-1], lw, left_r, right_c, cot_t, sq_r, sq_c),
+        [w_r] + room(n_r, n_c),
+        *(safe, tile, pa, pb, us[-1], lw, left_r, right_c, cot_t, sq_r, sq_c),
     )
     vs.append(v)
     pa, pb = over_rows(part, plus)
     dv, part = call(
-        first_du,
+        functools.partial(first_du, unscale),
         (v_like, u_like),
-        [pltpu.VMEM((128, n_r), BF16)] + room(n_c, n_r, True),
-        *(pa, pb, us[-1], vs[-1], lw, left_c, right_r, both, sq_c, sq_r),
+        [pltpu.VMEM((128, n_r), BF16), w_c] + room(n_c, n_r, True),
+        *(safe, tile, pa, pb, us[-1], vs[-1], lw, left_r, cot_t, left_c, right_r, both, sq_c, sq_r),
     )
     dus, dvs = [None] * ITERS, [None] * ITERS
     dvs[ITERS - 1] = dv
@@ -508,15 +662,15 @@
         dus[k + 1], part = call(
             functools.partial(next_dv, log_count),
             (u_like, v_like),
-            room(n_r, n_c, True),
-            *(pa, pb, us[k + 1], vs[k + 1], left_r, right_c, sq_r, sq_c),
+            [w_r] + room(n_r, n_c, True),
+            *(safe, tile, pa, pb, us[k + 1], vs[k + 1], left_r, right_c, sq_r, sq_c),
         )
         pa, pb = over_rows(part, plus)
         dvs[k], part = call(
             next_du,
             (v_like, u_like),
-            room(n_c, n_r, True),
-            *(pa, pb, us[k], vs[k + 1], lw, left_c, right_r, sq_c, sq_r),
+            [w_c] + room(n_c, n_r, True),
+            *(safe, tile, pa, pb, us[k], vs[k + 1], lw, left_c, right_r, sq_c, sq_r),
         )
     pa, pb = over_cols(part)
     n_t = n_c // 2

time: 253 us -> 517 us (2.04)
  Pallas kernels: 86.7 us -> 347 us
  local copies, waits for them, and re-layouts: 4.06 us -> 9.85 us
    pallas_call x20, Pallas kernels: 75.4 us -> 336 us  [call(): pl.pallas_call(kernel, out_shape=tuple((jax.ShapeDtypeStruct(s, d) for s,...]
    unnamed x10 -> x14, local copies, waits for them, and re-layouts: 4.04 us -> 9.83 us
  transfers between devices with their start and end apart: 48 -> 48, of which waited for: 44 -> 45; matrix products, arithmetic and copies ran while one was open for 0% -> 0% of each run, Pallas kernels for 0% -> 0%
where the time goes in v3:
time: 517 us
  Pallas kernels  347 us (67%)
  waiting for transfers between devices  80.8 us (16%)
  starting transfers between devices  58.2 us (11%)
  blocking collectives  18.8 us (4%)
  local copies, waits for them, and re-layouts  9.85 us (2%)
    pallas_call x20, Pallas kernels, call(): pl.pallas_call(kernel, out_shape=tuple((jax.ShapeDtypeStruct(s, d) for s,...  336 us
    ppermute x47, waiting for transfers between devices, swap(): return lax.ppermute(value, AXES, [(i, i ^ bits) for i in range(128)])  78.8 us
    ppermute x47, starting transfers between devices, swap(): return lax.ppermute(value, AXES, [(i, i ^ bits) for i in range(128)])  52.3 us
    all_to_all x1, blocking collectives, local(): mine = lax.all_to_all(payload, ('z', 'y'), 0, 0, tiled=True)  18.8 us
  transfers between devices with their start and end apart: 48, of which 45 were waited for; matrix products, arithmetic and copies ran while one was open for 0% of the time, Pallas kernels for 0%

profile of v3, /device:TPU:1, one launch (start us, length us, event | category | flops | bytes accessed | tf_op | source)
XLA Modules:
  0.0 516.7 jit_solution(493470632338800532)
XLA Ops:
  3.0 18.8 %all_to_all.10.mine = bf16[16,128,128]{2,1,0:T(8,128)(2,1)S(1)} all-to-all(bf16[16,128,128]{2,1,0:T(8,128)(2,1)S(1)} %get-tuple-element.57), channel_id=1, replica_groups=mesh['z'=4,'y'=4,'c'=2,'x'=4] {'z','y'}, dimensions={0} | all-to-all | bytes 1048576 | tf_op jit(solution)/shard_map/all_to_all | solution.py:588
  35.5 14.7 %shard_map.50 = (f32[1,1024]{1,0:T(1,128)S(1)}, f32[1024,4096]{1,0:T(8,128)S(1)}) custom-call(f32[1,128]{1,0:T(1,128)S(1)} %get-tuple-element.65.safe, bf16[1024,128]{1,0:T(8,128)(2,1)S(1)} %get-tuple-element.60.left_r, bf16[64,4096]{1,0:T(8,128)(2,1)S(1)} %get-tuple-element.66.right_c, bf16[4096,128]{1,0:T(8,128)(2,1)S(1)} %get-tuple-element.67.left_c, ...), custom_call_target="tpu_custom_call" | custom-call | tf_op jit(solution)/shard_map/pallas_call | solution.py:182
  52.8 14.7 %shard_map.51 = (f32[1,1024]{1,0:T(1,128)S(1)}, f32[1,4096]{1,0:T(1,128)S(1)}) custom-call(f32[1,128]{1,0:T(1,128)S(1)} %get-tuple-element.65.safe, f32[1024,4096]{1,0:T(8,128)S(1)} %get-tuple-element.68.tile, f32[1,1024]{1,0:T(1,128)S(1)} %get-tuple-element.69.pa, f32[1,1024]{1,0:T(1,128)S(1)} %collective-permute-done.4.pb, ...), custom_call_target="tpu_custom_call" | custom-call | tf_op jit(solution)/shard_map/pallas_call | solution.py:182
  67.5 2.8 collective-permute-start.5
  77.8 14.6 %shard_map.52 = (f32[1,4096]{1,0:T(1,128)S(1)}, f32[1,1024]{1,0:T(1,128)S(1)}) custom-call(f32[1,128]{1,0:T(1,128)S(1)} %get-tuple-element.65.safe, f32[1024,4096]{1,0:T(8,128)S(1)} %get-tuple-element.68.tile, f32[1,4096]{1,0:T(1,128)S(1)} %log_add_fusion.8.pa, f32[1,4096]{1,0:T(1,128)S(1)} %collective-permute-done.7.pb, ...), custom_call_target="tpu_custom_call" | custom-call | tf_op jit(solution)/shard_map/pallas_call | solution.py:182
  95.0 14.8 %shard_map.53 = (f32[1,1024]{1,0:T(1,128)S(1)}, f32[1,4096]{1,0:T(1,128)S(1)}) custom-call(f32[1,128]{1,0:T(1,128)S(1)} %get-tuple-element.65.safe, f32[1024,4096]{1,0:T(8,128)S(1)} %get-tuple-element.68.tile, f32[1,1024]{1,0:T(1,128)S(1)} %get-tuple-element.72.pa, f32[1,1024]{1,0:T(1,128)S(1)} %collective-permute-done.8.pb, ...), custom_call_target="tpu_custom_call" | custom-call | tf_op jit(solution)/shard_map/pallas_call | solution.py:182
  118.8 14.6 %shard_map.54 = (f32[1,4096]{1,0:T(1,128)S(1)}, f32[1,1024]{1,0:T(1,128)S(1)}) custom-call(f32[1,128]{1,0:T(1,128)S(1)} %get-tuple-element.65.safe, f32[1024,4096]{1,0:T(8,128)S(1)} %get-tuple-element.68.tile, f32[1,4096]{1,0:T(1,128)S(1)} %log_add_fusion.6.pa, f32[1,4096]{1,0:T(1,128)S(1)} %collective-permute-done.11.pb, ...), custom_call_target="tpu_custom_call" | custom-call | tf_op jit(solution)/shard_map/pallas_call | solution.py:182
  136.0 14.8 %shard_map.55 = (f32[1,1024]{1,0:T(1,128)S(1)}, f32[1,4096]{1,0:T(1,128)S(1)}) custom-call(f32[1,128]{1,0:T(1,128)S(1)} %get-tuple-element.65.safe, f32[1024,4096]{1,0:T(8,128)S(1)} %get-tuple-element.68.tile, f32[1,1024]{1,0:T(1,128)S(1)} %get-tuple-element.76.pa, f32[1,1024]{1,0:T(1,128)S(1)} %collective-permute-done.12.pb, ...), custom_call_target="tpu_custom_call" | custom-call | tf_op jit(solution)/shard_map/pallas_call | solution.py:182
  159.8 14.6 %shard_map.56 = (f32[1,4096]{1,0:T(1,128)S(1)}, f32[1,1024]{1,0:T(1,128)S(1)}) custom-call(f32[1,128]{1,0:T(1,128)S(1)} %get-tuple-element.65.safe, f32[1024,4096]{1,0:T(8,128)S(1)} %get-tuple-element.68.tile, f32[1,4096]{1,0:T(1,128)S(1)} %log_add_fusion.4.pa, f32[1,4096]{1,0:T(1,128)S(1)} %collective-permute-done.15.pb, ...), custom_call_target="tpu_custom_call" | custom-call | tf_op jit(solution)/shard_map/pallas_call | solution.py:182
  177.2 14.8 %shard_map.57 = (f32[1,1024]{1,0:T(1,128)S(1)}, f32[1,4096]{1,0:T(1,128)S(1)}) custom-call(f32[1,128]{1,0:T(1,128)S(1)} %get-tuple-element.65.safe, f32[1024,4096]{1,0:T(8,128)S(1)} %get-tuple-element.68.tile, f32[1,1024]{1,0:T(1,128)S(1)} %get-tuple-element.80.pa, f32[1,1024]{1,0:T(1,128)S(1)} %collective-permute-done.16.pb, ...), custom_call_target="tpu_custom_call" | custom-call | tf_op jit(solution)/shard_map/pallas_call | solution.py:182
  195.1 2.7 collective-permute-done.18
  201.0 14.6 %shard_map.58 = (f32[1,4096]{1,0:T(1,128)S(1)}, f32[1,1024]{1,0:T(1,128)S(1)}) custom-call(f32[1,128]{1,0:T(1,128)S(1)} %get-tuple-element.65.safe, f32[1024,4096]{1,0:T(8,128)S(1)} %get-tuple-element.68.tile, f32[1,4096]{1,0:T(1,128)S(1)} %log_add_fusion.2.pa, f32[1,4096]{1,0:T(1,128)S(1)} %collective-permute-done.19.pb, ...), custom_call_target="tpu_custom_call" | custom-call | tf_op jit(solution)/shard_map/pallas_call | solution.py:182
  218.2 14.8 %shard_map.59 = (f32[1,1024]{1,0:T(1,128)S(1)}, f32[1,4096]{1,0:T(1,128)S(1)}) custom-call(f32[1,128]{1,0:T(1,128)S(1)} %get-tuple-element.65.safe, f32[1024,4096]{1,0:T(8,128)S(1)} %get-tuple-element.68.tile, f32[1,1024]{1,0:T(1,128)S(1)} %get-tuple-element.84.pa, f32[1,1024]{1,0:T(1,128)S(1)} %collective-permute-done.20.pb, ...), custom_call_target="tpu_custom_call" | custom-call | tf_op jit(solution)/shard_map/pallas_call | solution.py:182
  242.0 17.0 %shard_map.60 = (f32[1,4096]{1,0:T(1,128)S(1)}, f32[1,4096]{1,0:T(1,128)S(1)}) custom-call(f32[1,128]{1,0:T(1,128)S(1)} %get-tuple-element.65.safe, f32[1024,4096]{1,0:T(8,128)S(1)} %get-tuple-element.68.tile, f32[1,4096]{1,0:T(1,128)S(1)} %log_add_fusion.pa, f32[1,4096]{1,0:T(1,128)S(1)} %collective-permute-done.23.pb, ...), custom_call_target="tpu_custom_call" | custom-call | tf_op jit(solution)/shard_map/pallas_call | solution.py:182
  260.9 2.7 collective-permute-done.25
  266.8 23.0 %shard_map.61 = (f32[1,4096]{1,0:T(1,128)S(1)}, f32[1,1024]{1,0:T(1,128)S(1)}) custom-call(f32[1,128]{1,0:T(1,128)S(1)} %get-tuple-element.65.safe, f32[1024,4096]{1,0:T(8,128)S(1)} %get-tuple-element.68.tile, f32[1,4096]{1,0:T(1,128)S(1)} %add.115.pa, f32[1,4096]{1,0:T(1,128)S(1)} %collective-permute-done.26.pb, f32[1,1024]{1,0:T(1,128)S(1)} %get-tuple-element.86.u.refs_4_, ...), custom_call_target="tpu_custom_call" | custom-call | tf_op jit(solution)/shard_map/pallas_call | solution.py:182
  292.4 16.3 %shard_map.62 = (f32[1,1024]{1,0:T(1,128)S(1)}, f32[1,4096]{1,0:T(1,128)S(1)}) custom-call(f32[1,128]{1,0:T(1,128)S(1)} %get-tuple-element.65.safe, f32[1024,4096]{1,0:T(8,128)S(1)} %get-tuple-element.68.tile, f32[1,1024]{1,0:T(1,128)S(1)} %get-tuple-element.91.pa, f32[1,1024]{1,0:T(1,128)S(1)} %collective-permute-done.27.pb, ...), custom_call_target="tpu_custom_call" | custom-call | tf_op jit(solution)/shard_map/pallas_call | solution.py:182
  311.7 2.7 collective-permute-done.29
  317.7 20.8 %shard_map.63 = (f32[1,4096]{1,0:T(1,128)S(1)}, f32[1,1024]{1,0:T(1,128)S(1)}) custom-call(f32[1,128]{1,0:T(1,128)S(1)} %get-tuple-element.65.safe, f32[1024,4096]{1,0:T(8,128)S(1)} %get-tuple-element.68.tile, f32[1,4096]{1,0:T(1,128)S(1)} %add.117.pa, f32[1,4096]{1,0:T(1,128)S(1)} %collective-permute-done.30.pb, ...), custom_call_target="tpu_custom_call" | custom-call | tf_op jit(solution)/shard_map/pallas_call | solution.py:182
  341.0 16.6 %shard_map.64 = (f32[1,1024]{1,0:T(1,128)S(1)}, f32[1,4096]{1,0:T(1,128)S(1)}) custom-call(f32[1,128]{1,0:T(1,128)S(1)} %get-tuple-element.65.safe, f32[1024,4096]{1,0:T(8,128)S(1)} %get-tuple-element.68.tile, f32[1,1024]{1,0:T(1,128)S(1)} %get-tuple-element.93.pa, f32[1,1024]{1,0:T(1,128)S(1)} %collective-permute-done.31.pb, ...), custom_call_target="tpu_custom_call" | custom-call | tf_op jit(solution)/shard_map/pallas_call | solution.py:182
  360.6 2.7 collective-permute-done.33
  366.5 20.8 %shard_map.65 = (f32[1,4096]{1,0:T(1,128)S(1)}, f32[1,1024]{1,0:T(1,128)S(1)}) custom-call(f32[1,128]{1,0:T(1,128)S(1)} %get-tuple-element.65.safe, f32[1024,4096]{1,0:T(8,128)S(1)} %get-tuple-element.68.tile, f32[1,4096]{1,0:T(1,128)S(1)} %add.119.pa, f32[1,4096]{1,0:T(1,128)S(1)} %collective-permute-done.34.pb, ...), custom_call_target="tpu_custom_call" | custom-call | tf_op jit(solution)/shard_map/pallas_call | solution.py:182
  389.9 16.4 %shard_map.66 = (f32[1,1024]{1,0:T(1,128)S(1)}, f32[1,4096]{1,0:T(1,128)S(1)}) custom-call(f32[1,128]{1,0:T(1,128)S(1)} %get-tuple-element.65.safe, f32[1024,4096]{1,0:T(8,128)S(1)} %get-tuple-element.68.tile, f32[1,1024]{1,0:T(1,128)S(1)} %get-tuple-element.95.pa, f32[1,1024]{1,0:T(1,128)S(1)} %collective-permute-done.35.pb, ...), custom_call_target="tpu_custom_call" | custom-call | tf_op jit(solution)/shard_map/pallas_call | solution.py:182
  409.2 2.7 collective-permute-done.37
  415.2 20.8 %shard_map.67 = (f32[1,4096]{1,0:T(1,128)S(1)}, f32[1,1024]{1,0:T(1,128)S(1)}) custom-call(f32[1,128]{1,0:T(1,128)S(1)} %get-tuple-element.65.safe, f32[1024,4096]{1,0:T(8,128)S(1)} %get-tuple-element.68.tile, f32[1,4096]{1,0:T(1,128)S(1)} %add.121.pa, f32[1,4096]{1,0:T(1,128)S(1)} %collective-permute-done.38.pb, ...), custom_call_target="tpu_custom_call" | custom-call | tf_op jit(solution)/shard_map/pallas_call | solution.py:182
  438.5 16.4 %shard_map.68 = (f32[1,1024]{1,0:T(1,128)S(1)}, f32[1,4096]{1,0:T(1,128)S(1)}) custom-call(f32[1,128]{1,0:T(1,128)S(1)} %get-tuple-element.65.safe, f32[1024,4096]{1,0:T(8,128)S(1)} %get-tuple-element.68.tile, f32[1,1024]{1,0:T(1,128)S(1)} %get-tuple-element.97.pa, f32[1,1024]{1,0:T(1,128)S(1)} %collective-permute-done.39.pb, ...), custom_call_target="tpu_custom_call" | custom-call | tf_op jit(solution)/shard_map/pallas_call | solution.py:182
  457.9 2.7 collective-permute-done.41
  463.8 5.8 %copy-done.1 = f32[1024,4096]{1,0:T(8,128)S(1)} copy-done((f32[1024,4096]{1,0:T(8,128)S(1)}, f32[1024,4096]{1,0:T(8,128)}, u32[]{:S(2)}) %copy-start.1) | copy-done | bytes 16777240
  469.6 20.8 %shard_map.69 = (f32[1,4096]{1,0:T(1,128)S(1)}, f32[1,1024]{1,0:T(1,128)S(1)}) custom-call(f32[1,128]{1,0:T(1,128)S(1)} %get-tuple-element.65.safe, f32[1024,4096]{1,0:T(8,128)S(1)} %copy-done.1, f32[1,4096]{1,0:T(1,128)S(1)} %add.123.pa, f32[1,4096]{1,0:T(1,128)S(1)} %collective-permute-done.42.pb, f32[1,1024]{1,0:T(1,128)S(1)} %get-tuple-element.70.u_old.u.refs_0_, ...), custom_call_target="tpu_custom_call" | custom-call | tf_op jit(solution)/shard_map/pallas_call | solution.py:182
  492.9 8.2 %final.1 = (bf16[4,32,128]{2,1,0:T(8,128)(2,1)S(1)}, bf16[32,32,128]{2,1,0:T(8,128)(2,1)}, f32[1,256]{1,0:T(1,128)}) custom-call(s32[2]{0:T(128)S(1)} %pad_add_fusion.place, bf16[4096,128]{1,0:T(8,128)(2,1)S(1)} %get-tuple-element.59.both, bf16[1024,128]{1,0:T(8,128)(2,1)S(1)} %get-tuple-element.60.left_r, bf16[64,1024]{1,0:T(8,128)(2,1)S(1)} %get-tuple-element.61.right_r, ...), custom_call_target="tpu_custom_call" | custom-call | tf_op jit(solution)/shard_map/final/pallas_call | solution.py:677
  501.1 5.9 %all-to-all-start.1 = ((bf16[32,32,128]{2,1,0:T(8,128)(2,1)}), bf16[32,32,128]{2,1,0:T(8,128)(2,1)S(1)}, u32[]{:S(2)}, u32[]{:S(2)}) async-start(bf16[32,32,128]{2,1,0:T(8,128)(2,1)} %get-tuple-element.110), calls=%async_computation.1 | async-start | bytes 524288 | tf_op jit(solution)/shard_map/all_to_all | solution.py:710
  511.1 2.8 collective-permute-done.45.row_2
  (127 shorter events, 119.7 us)
Async XLA Ops:
  21.8 9.7 %collective-permute-start = (bf16[16,128,128]{2,1,0:T(8,128)(2,1)S(1)}, bf16[16,128,128]{2,1,0:T(8,128)(2,1)S(1)}, u32[]{:S(2)}, u32[]{:S(2)}) collective-permute-start(bf16[16,128,128]{2,1,0:T(8,128)(2,1)S(1)} %all_to_all.10.mine), channel_id=1, source_target_pairs={{0,4},{1,5},{2,6},{3,7},{4,0},{5,1},{6,2},{7,3},{8,12},{9,13},{10,... | collective-permute-start | bytes 1572872 | tf_op jit(solution)/shard_map/ppermute | solution.py:26
  23.9 6.8 %collective-permute-start.3 = (bf16[144,128]{1,0:T(8,128)(2,1)S(1)}, bf16[144,128]{1,0:T(8,128)(2,1)S(1)}, u32[]{:S(2)}, u32[]{:S(2)}) collective-permute-start(bf16[144,128]{1,0:T(8,128)(2,1)S(1)} %get-tuple-element.58.own), channel_id=1, source_target_pairs={{0,80},{1,81},{2,82},{3,83},{4,84},{5,85},{6,86},{7,87},{8,88},{9,... | collective-permute-start | bytes 110600 | tf_op jit(solution)/shard_map/ppermute | solution.py:26
  25.4 5.3 %collective-permute-start.2 = (bf16[144,128]{1,0:T(8,128)(2,1)S(1)}, bf16[144,128]{1,0:T(8,128)(2,1)S(1)}, u32[]{:S(2)}, u32[]{:S(2)}) collective-permute-start(bf16[144,128]{1,0:T(8,128)(2,1)S(1)} %get-tuple-element.58.own), channel_id=1, source_target_pairs={{0,64},{1,65},{2,66},{3,67},{4,68},{5,69},{6,70},{7,71},{8,72},{9,... | collective-permute-start | bytes 110600 | tf_op jit(solution)/shard_map/ppermute | solution.py:26
  27.1 4.4 collective-permute-start.1
  50.2 2.5 collective-permute-start.4
  67.5 3.7 collective-permute-start.5
  71.3 3.2 collective-permute-start.6
  74.6 3.2 collective-permute-start.7
  112.3 3.2 collective-permute-start.10
  115.6 3.2 collective-permute-start.11
  153.3 3.2 collective-permute-start.14
  156.6 3.2 collective-permute-start.15
  174.5 2.7 collective-permute-start.16
  194.5 3.2 collective-permute-start.18
  197.8 3.2 collective-permute-start.19
  235.5 3.2 collective-permute-start.22
  238.8 3.2 collective-permute-start.23
  260.3 3.2 collective-permute-start.25
  263.6 3.2 collective-permute-start.26
  311.1 3.2 collective-permute-start.29
  314.4 3.2 collective-permute-start.30
  338.5 2.5 collective-permute-start.31
  360.0 3.2 collective-permute-start.33
  363.3 3.2 collective-permute-start.34
  408.6 3.2 collective-permute-start.37
  411.9 3.2 collective-permute-start.38
  457.3 3.2 collective-permute-start.41
  460.6 3.2 collective-permute-start.42
  501.1 14.8 %all-to-all-start.1 = ((bf16[32,32,128]{2,1,0:T(8,128)(2,1)}), bf16[32,32,128]{2,1,0:T(8,128)(2,1)S(1)}, u32[]{:S(2)}, u32[]{:S(2)}) async-start(bf16[32,32,128]{2,1,0:T(8,128)(2,1)} %get-tuple-element.110), calls=%async_computation.1 | async-start | bytes 524288 | tf_op jit(solution)/shard_map/all_to_all | solution.py:710
  507.1 4.1 collective-permute-start.46
  509.6 4.3 collective-permute-start.45
  510.1 3.8 collective-permute-start.44
  (23 other events, 436.5 us)

commit v4 on v3

--- a/solution.py
+++ b/solution.py
@@ -129,25 +129,25 @@
 
 def sum_rows(tile, weight, emit, pair=None):
     rows, cols = tile.shape
-    span = 1024
-
-    def step(j, carry):
-        n = pl.ds(pl.multiple_of(j * span, span), span)
-        acc = [jnp.zeros((8, 128), F32)] * (span // 128)
-        height = 64 if pair is None else 256
-        for m in range(0, rows, height):
-            w = weight[m : m + height, :]
+    span, height = (2048, 128) if pair is None else (1024, 256)
+    for n in range(0, cols, span):
+
+        def of_block(i, acc, n=n):
+            m = pl.ds(pl.multiple_of(i * height, height), height)
+            w = weight[m, :]
             if pair is not None:
-                pr = mm(pair[0][m : m + height, :], pair[1][:, n])
-            for q in range(span // 128):
-                y = tile[m : m + height, pl.ds(pl.multiple_of(j * span + q * 128, 128), 128)] * w
+                pr = mm(pair[0][m, :], pair[1][:, n : n + span])
+            out = []
+            for q in range(0, span, 128):
+                y = tile[m, n + q : n + q + 128] * w
                 if pair is not None:
-                    y = y * pr[:, q * 128 : (q + 1) * 128]
-                acc[q] = acc[q] + jnp.sum(y.reshape(height // 8, 8, 128), axis=0)
-        emit(n, jnp.concatenate([jnp.sum(x, axis=0, keepdims=True) for x in acc], axis=1))
-        return carry
-
-    lax.fori_loop(0, cols // span, step, 0)
+                    y = y * pr[:, q : q + 128]
+                out.append(acc[q // 128] + jnp.sum(y.reshape(height // 8, 8, 128), axis=0))
+            return tuple(out)
+
+        acc = (jnp.zeros((8, 128), F32),) * (span // 128)
+        acc = lax.fori_loop(0, rows // height, of_block, acc)
+        emit(slice(n, n + span), jnp.concatenate([jnp.sum(x, axis=0, keepdims=True) for x in acc], axis=1))
 
 
 def sum_cols(tile, weight, emit, pair=None):
@@ -364,30 +364,39 @@
     return jnp.max(v, axis=1, keepdims=True)
 
 
+def row_sums(left_r, right_c, row_vector, col_vector, row_x, col_x, acc, tile=None, weight=None):
+    row_x[...] = extra(row_vector, None, True)
+    col_x[...] = extra(col_vector, None, False)
+    acc[...] = jnp.zeros(acc.shape, F32)
+    low = jnp.zeros((64, 256), BF16)
+    high = jnp.zeros((48, 256), BF16)
+
+    def step(j, carry):
+        n = pl.ds(pl.multiple_of(j * 1024, 1024), 1024)
+        right = jnp.concatenate([right_c[:, n], col_x[:, n], jnp.zeros((48, 1024), BF16)], axis=0)
+        for m in range(0, left_r.shape[0], 256):
+            a = left_r[m : m + 256, :]
+            a = a + jnp.concatenate([low, row_x[:, m : m + 256], high], axis=0).T
+            e = jnp.exp(mm(a, right))
+            if tile is not None:
+                tile[m : m + 256, n] = e
+            y = acc[m : m + 256, :]
+            for q in range(8):
+                part = e[:, q * 128 : (q + 1) * 128]
+                if weight is not None:
+                    part = part * weight[:, pl.ds(pl.multiple_of(j * 1024 + q * 128, 128), 128)]
+                y = y + part
+            acc[m : m + 256, :] = y
+        return carry
+
+    lax.fori_loop(0, right_c.shape[1] // 1024, step, 0)
+    return jnp.sum(acc[...].T, axis=0, keepdims=True)
+
+
 def first_u(safe, left_r, right_c, left_c, right_r, sq_c, sq_r, out, tile, acc, row_x, col_x, *scratch):
     def fast():
-        row_x[...] = extra(-sq_r[...], None, True)
-        col_x[...] = extra(-sq_c[...], None, False)
-        acc[...] = jnp.zeros(acc.shape, F32)
-        low = jnp.zeros((64, 256), BF16)
-        high = jnp.zeros((48, 256), BF16)
-
-        def step(j, carry):
-            n = pl.ds(pl.multiple_of(j * 1024, 1024), 1024)
-            right = jnp.concatenate([right_c[:, n], col_x[:, n], jnp.zeros((48, 1024), BF16)], axis=0)
-            for m in range(0, left_r.shape[0], 256):
-                a = left_r[m : m + 256, :]
-                a = a + jnp.concatenate([low, row_x[:, m : m + 256], high], axis=0).T
-                e = jnp.exp(mm(a, right))
-                tile[m : m + 256, n] = e
-                y = acc[m : m + 256, :]
-                for q in range(8):
-                    y = y + e[:, q * 128 : (q + 1) * 128]
-                acc[m : m + 256, :] = y
-            return carry
-
-        lax.fori_loop(0, tile.shape[1] // 1024, step, 0)
-        out[...] = jnp.log(jnp.sum(acc[...].T, axis=0, keepdims=True))
+        total = row_sums(left_r, right_c, -sq_r[...], -sq_c[...], row_x, col_x, acc, tile)
+        out[...] = jnp.log(total)
 
     def slow():
         scratch[0][...] = extra(-sq_c[...], None, True)
@@ -432,7 +441,9 @@
     both_ways(safe, fast, slow)
 
 
-def next_u(log_count, safe, tile, pa, pb, v_old, u_old, left_c, right_r, sq_c, sq_r, v_new, out, base, w, *scratch):
+def next_u(
+    log_count, safe, tile, pa, pb, v_old, u_old, left_c, right_r, sq_c, sq_r, v_new, out, base, w, *scratch
+):
     v = -merge(pa[...], pb[...])
     v_new[...] = v
 
@@ -541,11 +552,16 @@
     both_ways(safe, fast, slow)
 
 
-def next_du(safe, tile, pa, pb, u, v, lw, left_c, right_r, sq_c, sq_r, dv_new, out, w, *scratch):
+def next_du(kept, safe, tile, pa, pb, u, v, lw, left_c, right_r, sq_c, sq_r, left_r, right_c, dv_new, out, w, *scratch):
     dv = pa[...] + pb[...]
     dv_new[...] = dv
 
     def fast():
+        if not kept:
+            row_vector, col_vector = u[...] + lw[...] - sq_r[...], v[...] - sq_c[...]
+            acc, row_x, col_x = scratch[3:]
+            out[...] = -row_sums(left_r, right_c, row_vector, col_vector, row_x, col_x, acc, None, dv_new)
+            return
         top = peak(v[...])
         w[0:1, :] = jnp.exp(v[...] - top) * dv
 
@@ -667,10 +683,10 @@
         )
         pa, pb = over_rows(part, plus)
         dvs[k], part = call(
-            next_du,
+            functools.partial(next_du, k > 0),
             (v_like, u_like),
-            [w_c] + room(n_c, n_r, True),
-            *(safe, tile, pa, pb, us[k], vs[k + 1], lw, left_c, right_r, sq_c, sq_r),
+            [w_c] + room(n_c, n_r, True) + ([] if k else [w_r] + room(n_r, n_c)),
+            *(safe, tile if k else sq_r, pa, pb, us[k], vs[k + 1], lw, left_c, right_r, sq_c, sq_r, left_r, right_c),
         )
     pa, pb = over_cols(part)
     n_t = n_c // 2

time: 517 us -> 513 us (level)
  no operation moved by 1% of the time
where the time goes in v4:
time: 513 us
  Pallas kernels  347 us (68%)
  waiting for transfers between devices  80.9 us (16%)
  starting transfers between devices  58.2 us (11%)
  blocking collectives  18.8 us (4%)
  local copies, waits for them, and re-layouts  5.92 us (1%)
    pallas_call x20, Pallas kernels, call(): pl.pallas_call(kernel, out_shape=tuple((jax.ShapeDtypeStruct(s, d) for s,...  336 us
    ppermute x47, waiting for transfers between devices, swap(): return lax.ppermute(value, AXES, [(i, i ^ bits) for i in range(128)])  78.9 us
    ppermute x47, starting transfers between devices, swap(): return lax.ppermute(value, AXES, [(i, i ^ bits) for i in range(128)])  52.2 us
    all_to_all x1, blocking collectives, local(): mine = lax.all_to_all(payload, ('z', 'y'), 0, 0, tiled=True)  18.8 us
  transfers between devices with their start and end apart: 48, of which 45 were waited for; matrix products, arithmetic and copies ran while one was open for 0% of the time, Pallas kernels for 0%

profile of v4, /device:TPU:1, one launch (start us, length us, event | category | flops | bytes accessed | tf_op | source)
XLA Modules:
  0.0 512.9 jit_solution(14740179982594152675)
XLA Ops:
  3.0 18.8 %all_to_all.10.mine = bf16[16,128,128]{2,1,0:T(8,128)(2,1)S(1)} all-to-all(bf16[16,128,128]{2,1,0:T(8,128)(2,1)S(1)} %get-tuple-element.57), channel_id=1, replica_groups=mesh['z'=4,'y'=4,'c'=2,'x'=4] {'z','y'}, dimensions={0} | all-to-all | bytes 1048576 | tf_op jit(solution)/shard_map/all_to_all | solution.py:604
  37.4 14.7 %shard_map.50 = (f32[1,1024]{1,0:T(1,128)S(1)}, f32[1024,4096]{1,0:T(8,128)S(1)}) custom-call(f32[1,128]{1,0:T(1,128)S(1)} %get-tuple-element.65.safe, bf16[1024,128]{1,0:T(8,128)(2,1)S(1)} %get-tuple-element.60.left_r, bf16[64,4096]{1,0:T(8,128)(2,1)S(1)} %get-tuple-element.66.right_c, bf16[4096,128]{1,0:T(8,128)(2,1)S(1)} %get-tuple-element.67.left_c, ...), custom_call_target="tpu_custom_call" | custom-call | tf_op jit(solution)/shard_map/pallas_call | solution.py:182
  54.6 14.7 %shard_map.51 = (f32[1,1024]{1,0:T(1,128)S(1)}, f32[1,4096]{1,0:T(1,128)S(1)}) custom-call(f32[1,128]{1,0:T(1,128)S(1)} %get-tuple-element.65.safe, f32[1024,4096]{1,0:T(8,128)S(1)} %get-tuple-element.68.tile, f32[1,1024]{1,0:T(1,128)S(1)} %get-tuple-element.69.pa, f32[1,1024]{1,0:T(1,128)S(1)} %collective-permute-done.4.pb, ...), custom_call_target="tpu_custom_call" | custom-call | tf_op jit(solution)/shard_map/pallas_call | solution.py:182
  69.4 2.8 collective-permute-start.5
  79.7 14.6 %shard_map.52 = (f32[1,4096]{1,0:T(1,128)S(1)}, f32[1,1024]{1,0:T(1,128)S(1)}) custom-call(f32[1,128]{1,0:T(1,128)S(1)} %get-tuple-element.65.safe, f32[1024,4096]{1,0:T(8,128)S(1)} %get-tuple-element.68.tile, f32[1,4096]{1,0:T(1,128)S(1)} %log_add_fusion.8.pa, f32[1,4096]{1,0:T(1,128)S(1)} %collective-permute-done.7.pb, ...), custom_call_target="tpu_custom_call" | custom-call | tf_op jit(solution)/shard_map/pallas_call | solution.py:182
  96.8 14.8 %shard_map.53 = (f32[1,1024]{1,0:T(1,128)S(1)}, f32[1,4096]{1,0:T(1,128)S(1)}) custom-call(f32[1,128]{1,0:T(1,128)S(1)} %get-tuple-element.65.safe, f32[1024,4096]{1,0:T(8,128)S(1)} %get-tuple-element.68.tile, f32[1,1024]{1,0:T(1,128)S(1)} %get-tuple-element.72.pa, f32[1,1024]{1,0:T(1,128)S(1)} %collective-permute-done.8.pb, ...), custom_call_target="tpu_custom_call" | custom-call | tf_op jit(solution)/shard_map/pallas_call | solution.py:182
  120.7 14.6 %shard_map.54 = (f32[1,4096]{1,0:T(1,128)S(1)}, f32[1,1024]{1,0:T(1,128)S(1)}) custom-call(f32[1,128]{1,0:T(1,128)S(1)} %get-tuple-element.65.safe, f32[1024,4096]{1,0:T(8,128)S(1)} %get-tuple-element.68.tile, f32[1,4096]{1,0:T(1,128)S(1)} %log_add_fusion.6.pa, f32[1,4096]{1,0:T(1,128)S(1)} %collective-permute-done.11.pb, ...), custom_call_target="tpu_custom_call" | custom-call | tf_op jit(solution)/shard_map/pallas_call | solution.py:182
  137.8 14.8 %shard_map.55 = (f32[1,1024]{1,0:T(1,128)S(1)}, f32[1,4096]{1,0:T(1,128)S(1)}) custom-call(f32[1,128]{1,0:T(1,128)S(1)} %get-tuple-element.65.safe, f32[1024,4096]{1,0:T(8,128)S(1)} %get-tuple-element.68.tile, f32[1,1024]{1,0:T(1,128)S(1)} %get-tuple-element.76.pa, f32[1,1024]{1,0:T(1,128)S(1)} %collective-permute-done.12.pb, ...), custom_call_target="tpu_custom_call" | custom-call | tf_op jit(solution)/shard_map/pallas_call | solution.py:182
  155.7 2.7 collective-permute-done.14
  161.7 14.6 %shard_map.56 = (f32[1,4096]{1,0:T(1,128)S(1)}, f32[1,1024]{1,0:T(1,128)S(1)}) custom-call(f32[1,128]{1,0:T(1,128)S(1)} %get-tuple-element.65.safe, f32[1024,4096]{1,0:T(8,128)S(1)} %get-tuple-element.68.tile, f32[1,4096]{1,0:T(1,128)S(1)} %log_add_fusion.4.pa, f32[1,4096]{1,0:T(1,128)S(1)} %collective-permute-done.15.pb, ...), custom_call_target="tpu_custom_call" | custom-call | tf_op jit(solution)/shard_map/pallas_call | solution.py:182
  178.9 14.8 %shard_map.57 = (f32[1,1024]{1,0:T(1,128)S(1)}, f32[1,4096]{1,0:T(1,128)S(1)}) custom-call(f32[1,128]{1,0:T(1,128)S(1)} %get-tuple-element.65.safe, f32[1024,4096]{1,0:T(8,128)S(1)} %get-tuple-element.68.tile, f32[1,1024]{1,0:T(1,128)S(1)} %get-tuple-element.80.pa, f32[1,1024]{1,0:T(1,128)S(1)} %collective-permute-done.16.pb, ...), custom_call_target="tpu_custom_call" | custom-call | tf_op jit(solution)/shard_map/pallas_call | solution.py:182
  196.9 2.7 collective-permute-done.18
  202.9 14.6 %shard_map.58 = (f32[1,4096]{1,0:T(1,128)S(1)}, f32[1,1024]{1,0:T(1,128)S(1)}) custom-call(f32[1,128]{1,0:T(1,128)S(1)} %get-tuple-element.65.safe, f32[1024,4096]{1,0:T(8,128)S(1)} %get-tuple-element.68.tile, f32[1,4096]{1,0:T(1,128)S(1)} %log_add_fusion.2.pa, f32[1,4096]{1,0:T(1,128)S(1)} %collective-permute-done.19.pb, ...), custom_call_target="tpu_custom_call" | custom-call | tf_op jit(solution)/shard_map/pallas_call | solution.py:182
  220.1 14.8 %shard_map.59 = (f32[1,1024]{1,0:T(1,128)S(1)}, f32[1,4096]{1,0:T(1,128)S(1)}) custom-call(f32[1,128]{1,0:T(1,128)S(1)} %get-tuple-element.65.safe, f32[1024,4096]{1,0:T(8,128)S(1)} %get-tuple-element.68.tile, f32[1,1024]{1,0:T(1,128)S(1)} %get-tuple-element.84.pa, f32[1,1024]{1,0:T(1,128)S(1)} %collective-permute-done.20.pb, ...), custom_call_target="tpu_custom_call" | custom-call | tf_op jit(solution)/shard_map/pallas_call | solution.py:182
  237.9 2.7 collective-permute-done.22
  243.9 17.0 %shard_map.60 = (f32[1,4096]{1,0:T(1,128)S(1)}, f32[1,4096]{1,0:T(1,128)S(1)}) custom-call(f32[1,128]{1,0:T(1,128)S(1)} %get-tuple-element.65.safe, f32[1024,4096]{1,0:T(8,128)S(1)} %get-tuple-element.68.tile, f32[1,4096]{1,0:T(1,128)S(1)} %log_add_fusion.pa, f32[1,4096]{1,0:T(1,128)S(1)} %collective-permute-done.23.pb, ...), custom_call_target="tpu_custom_call" | custom-call | tf_op jit(solution)/shard_map/pallas_call | solution.py:182
  262.8 2.7 collective-permute-done.25
  268.8 23.0 %shard_map.61 = (f32[1,4096]{1,0:T(1,128)S(1)}, f32[1,1024]{1,0:T(1,128)S(1)}) custom-call(f32[1,128]{1,0:T(1,128)S(1)} %get-tuple-element.65.safe, f32[1024,4096]{1,0:T(8,128)S(1)} %get-tuple-element.68.tile, f32[1,4096]{1,0:T(1,128)S(1)} %add.115.pa, f32[1,4096]{1,0:T(1,128)S(1)} %collective-permute-done.26.pb, f32[1,1024]{1,0:T(1,128)S(1)} %get-tuple-element.86.u.refs_4_, ...), custom_call_target="tpu_custom_call" | custom-call | tf_op jit(solution)/shard_map/pallas_call | solution.py:182
  294.3 16.3 %shard_map.62 = (f32[1,1024]{1,0:T(1,128)S(1)}, f32[1,4096]{1,0:T(1,128)S(1)}) custom-call(f32[1,128]{1,0:T(1,128)S(1)} %get-tuple-element.65.safe, f32[1024,4096]{1,0:T(8,128)S(1)} %get-tuple-element.68.tile, f32[1,1024]{1,0:T(1,128)S(1)} %get-tuple-element.91.pa, f32[1,1024]{1,0:T(1,128)S(1)} %collective-permute-done.27.pb, ...), custom_call_target="tpu_custom_call" | custom-call | tf_op jit(solution)/shard_map/pallas_call | solution.py:182
  313.7 2.7 collective-permute-done.29
  319.6 20.8 %shard_map.63 = (f32[1,4096]{1,0:T(1,128)S(1)}, f32[1,1024]{1,0:T(1,128)S(1)}) custom-call(f32[1,128]{1,0:T(1,128)S(1)} %get-tuple-element.65.safe, f32[1024,4096]{1,0:T(8,128)S(1)} %get-tuple-element.68.tile, f32[1,4096]{1,0:T(1,128)S(1)} %add.117.pa, f32[1,4096]{1,0:T(1,128)S(1)} %collective-permute-done.30.pb, ...), custom_call_target="tpu_custom_call" | custom-call | tf_op jit(solution)/shard_map/pallas_call | solution.py:182
  342.9 16.4 %shard_map.64 = (f32[1,1024]{1,0:T(1,128)S(1)}, f32[1,4096]{1,0:T(1,128)S(1)}) custom-call(f32[1,128]{1,0:T(1,128)S(1)} %get-tuple-element.65.safe, f32[1024,4096]{1,0:T(8,128)S(1)} %get-tuple-element.68.tile, f32[1,1024]{1,0:T(1,128)S(1)} %get-tuple-element.93.pa, f32[1,1024]{1,0:T(1,128)S(1)} %collective-permute-done.31.pb, ...), custom_call_target="tpu_custom_call" | custom-call | tf_op jit(solution)/shard_map/pallas_call | solution.py:182
  362.3 2.7 collective-permute-done.33
  368.2 20.8 %shard_map.65 = (f32[1,4096]{1,0:T(1,128)S(1)}, f32[1,1024]{1,0:T(1,128)S(1)}) custom-call(f32[1,128]{1,0:T(1,128)S(1)} %get-tuple-element.65.safe, f32[1024,4096]{1,0:T(8,128)S(1)} %get-tuple-element.68.tile, f32[1,4096]{1,0:T(1,128)S(1)} %add.119.pa, f32[1,4096]{1,0:T(1,128)S(1)} %collective-permute-done.34.pb, ...), custom_call_target="tpu_custom_call" | custom-call | tf_op jit(solution)/shard_map/pallas_call | solution.py:182
  391.6 16.6 %shard_map.66 = (f32[1,1024]{1,0:T(1,128)S(1)}, f32[1,4096]{1,0:T(1,128)S(1)}) custom-call(f32[1,128]{1,0:T(1,128)S(1)} %get-tuple-element.65.safe, f32[1024,4096]{1,0:T(8,128)S(1)} %get-tuple-element.68.tile, f32[1,1024]{1,0:T(1,128)S(1)} %get-tuple-element.95.pa, f32[1,1024]{1,0:T(1,128)S(1)} %collective-permute-done.35.pb, ...), custom_call_target="tpu_custom_call" | custom-call | tf_op jit(solution)/shard_map/pallas_call | solution.py:182
  411.2 2.7 collective-permute-done.37
  417.1 20.8 %shard_map.67 = (f32[1,4096]{1,0:T(1,128)S(1)}, f32[1,1024]{1,0:T(1,128)S(1)}) custom-call(f32[1,128]{1,0:T(1,128)S(1)} %get-tuple-element.65.safe, f32[1024,4096]{1,0:T(8,128)S(1)} %get-tuple-element.68.tile, f32[1,4096]{1,0:T(1,128)S(1)} %add.121.pa, f32[1,4096]{1,0:T(1,128)S(1)} %collective-permute-done.38.pb, ...), custom_call_target="tpu_custom_call" | custom-call | tf_op jit(solution)/shard_map/pallas_call | solution.py:182
  440.4 16.4 %shard_map.68 = (f32[1,1024]{1,0:T(1,128)S(1)}, f32[1,4096]{1,0:T(1,128)S(1)}) custom-call(f32[1,128]{1,0:T(1,128)S(1)} %get-tuple-element.65.safe, f32[1024,4096]{1,0:T(8,128)S(1)} %get-tuple-element.68.tile, f32[1,1024]{1,0:T(1,128)S(1)} %get-tuple-element.97.pa, f32[1,1024]{1,0:T(1,128)S(1)} %collective-permute-done.39.pb, ...), custom_call_target="tpu_custom_call" | custom-call | tf_op jit(solution)/shard_map/pallas_call | solution.py:182
  465.7 20.8 %shard_map.69 = (f32[1,4096]{1,0:T(1,128)S(1)}, f32[1,1024]{1,0:T(1,128)S(1)}) custom-call(f32[1,128]{1,0:T(1,128)S(1)} %get-tuple-element.65.safe, f32[1,1024]{1,0:T(1,128)S(1)} %get-tuple-element.63.sq_r.u_old.tile, f32[1,4096]{1,0:T(1,128)S(1)} %add.123.pa, f32[1,4096]{1,0:T(1,128)S(1)} %collective-permute-done.42.pb, ...), custom_call_target="tpu_custom_call" | custom-call | tf_op jit(solution)/shard_map/pallas_call | solution.py:182
  489.1 8.2 %final.1 = (bf16[4,32,128]{2,1,0:T(8,128)(2,1)S(1)}, bf16[32,32,128]{2,1,0:T(8,128)(2,1)}, f32[1,256]{1,0:T(1,128)}) custom-call(s32[2]{0:T(128)S(1)} %pad_add_fusion.place, bf16[4096,128]{1,0:T(8,128)(2,1)S(1)} %get-tuple-element.59.both, bf16[1024,128]{1,0:T(8,128)(2,1)S(1)} %get-tuple-element.60.left_r, bf16[64,1024]{1,0:T(8,128)(2,1)S(1)} %get-tuple-element.61.right_r, ...), custom_call_target="tpu_custom_call" | custom-call | tf_op jit(solution)/shard_map/final/pallas_call | solution.py:693
  497.2 5.9 %all-to-all-start.1 = ((bf16[32,32,128]{2,1,0:T(8,128)(2,1)}), bf16[32,32,128]{2,1,0:T(8,128)(2,1)S(1)}, u32[]{:S(2)}, u32[]{:S(2)}) async-start(bf16[32,32,128]{2,1,0:T(8,128)(2,1)} %get-tuple-element.110), calls=%async_computation.1 | async-start | bytes 524288 | tf_op jit(solution)/shard_map/all_to_all | solution.py:726
  507.3 2.8 collective-permute-done.45.row_2
  (127 shorter events, 118.9 us)
Async XLA Ops:
  21.8 10.5 %collective-permute-start = (bf16[16,128,128]{2,1,0:T(8,128)(2,1)S(1)}, bf16[16,128,128]{2,1,0:T(8,128)(2,1)S(1)}, u32[]{:S(2)}, u32[]{:S(2)}) collective-permute-start(bf16[16,128,128]{2,1,0:T(8,128)(2,1)S(1)} %all_to_all.10.mine), channel_id=1, source_target_pairs={{0,4},{1,5},{2,6},{3,7},{4,0},{5,1},{6,2},{7,3},{8,12},{9,13},{10,... | collective-permute-start | bytes 1572872 | tf_op jit(solution)/shard_map/ppermute | solution.py:26
  24.7 6.8 %collective-permute-start.3 = (bf16[144,128]{1,0:T(8,128)(2,1)S(1)}, bf16[144,128]{1,0:T(8,128)(2,1)S(1)}, u32[]{:S(2)}, u32[]{:S(2)}) collective-permute-start(bf16[144,128]{1,0:T(8,128)(2,1)S(1)} %get-tuple-element.58.own), channel_id=1, source_target_pairs={{0,80},{1,81},{2,82},{3,83},{4,84},{5,85},{6,86},{7,87},{8,88},{9,... | collective-permute-start | bytes 110600 | tf_op jit(solution)/shard_map/ppermute | solution.py:26
  26.2 5.3 %collective-permute-start.2 = (bf16[144,128]{1,0:T(8,128)(2,1)S(1)}, bf16[144,128]{1,0:T(8,128)(2,1)S(1)}, u32[]{:S(2)}, u32[]{:S(2)}) collective-permute-start(bf16[144,128]{1,0:T(8,128)(2,1)S(1)} %get-tuple-element.58.own), channel_id=1, source_target_pairs={{0,64},{1,65},{2,66},{3,67},{4,68},{5,69},{6,70},{7,71},{8,72},{9,... | collective-permute-start | bytes 110600 | tf_op jit(solution)/shard_map/ppermute | solution.py:26
  28.0 4.4 collective-permute-start.1
  69.4 3.7 collective-permute-start.5
  73.1 3.2 collective-permute-start.6
  76.4 3.2 collective-permute-start.7
  94.3 2.5 collective-permute-start.8
  114.1 3.2 collective-permute-start.10
  117.4 3.2 collective-permute-start.11
  155.1 3.2 collective-permute-start.14
  158.5 3.2 collective-permute-start.15
  196.2 3.4 collective-permute-start.18
  199.7 3.2 collective-permute-start.19
  217.5 2.5 collective-permute-start.20
  237.4 3.2 collective-permute-start.22
  240.7 3.2 collective-permute-start.23
  262.2 3.2 collective-permute-start.25
  265.5 3.2 collective-permute-start.26
  313.1 3.2 collective-permute-start.29
  316.3 3.2 collective-permute-start.30
  340.4 2.5 collective-permute-start.31
  361.7 3.2 collective-permute-start.33
  365.0 3.2 collective-permute-start.34
  410.6 3.2 collective-permute-start.37
  413.8 3.2 collective-permute-start.38
  459.2 3.2 collective-permute-start.41
  462.5 3.2 collective-permute-start.42
  497.2 14.8 %all-to-all-start.1 = ((bf16[32,32,128]{2,1,0:T(8,128)(2,1)}), bf16[32,32,128]{2,1,0:T(8,128)(2,1)S(1)}, u32[]{:S(2)}, u32[]{:S(2)}) async-start(bf16[32,32,128]{2,1,0:T(8,128)(2,1)} %get-tuple-element.110), calls=%async_computation.1 | async-start | bytes 524288 | tf_op jit(solution)/shard_map/all_to_all | solution.py:726
  503.2 4.1 collective-permute-start.46
  505.7 4.3 collective-permute-start.45
  506.3 3.8 collective-permute-start.44
  (23 other events, 44.3 us)
